TPU v7x, 512 devices: a whole 4x4x16 slice. The times are simulated.
512 devices in a mesh: ctx: 64 (over z_lo, y, core), section: 2 (over z_hi), tp: 4 (over x).
Axes of the slice: x: 4, y: 4, z: 16 (z_hi: 2, z_lo: 8; z = z_hi * 8 + z_lo), core: 2. Of those that a mesh axis runs over, the one named last changes fastest.
Arguments:
- text_embed: bfloat16 [8192, 4096], P('ctx', ('section', 'tp')), may hold values from -6 to 6
- frame_feats: bfloat16 [8192, 1024], P('ctx', ('section', 'tp')), may hold values from -6 to 6
- frame_count: int32 [64], P('ctx'), may hold values from 0 to 128
- proj_weight: bfloat16 [1024, 4096], P(None, ('section', 'tp')), may hold values from -0.1875 to 0.1875
- norm_gain: bfloat16 [4096], replicated, may hold values from 0.099609375 to 1.8984375
- q_weight: bfloat16 [4096, 2048], P('ctx', ('section', 'tp')), may hold values from -0.046875 to 0.046875
- k_weight: bfloat16 [4096, 2048], P('ctx', ('section', 'tp')), may hold values from -0.046875 to 0.046875
- v_weight: bfloat16 [4096, 2048], P('ctx', ('section', 'tp')), may hold values from -0.09375 to 0.09375
Outputs:
- attended: bfloat16 [8192, 2048], P('ctx', ('section', 'tp'))
All inputs are finite; a program needn't handle non-finite values.
Results may differ from a plain program's by a relative error of at most 0.012.
Values may be sent and summed in bfloat16 or wider, within the bound.
No kernel may reach another device: no remote copies, remote signals or barrier semaphores. Data moves between devices by JAX's collectives and lax.ppermute only.
A program may use at most 64 MiB of HBM per device.

v0:
```python
import math

import jax
import jax.numpy as jnp
from jax import lax
from jax.sharding import PartitionSpec as P

HD = 128


ROPE_BASE = 1000000.0
NORM_EPS = 1e-05
MASKED = -1e30


def rotate(values, positions):
    half = values.shape[-1] // 2
    ladder = jnp.arange(half, dtype=jnp.float32) * 2.0 / values.shape[-1]
    freq = ROPE_BASE ** (-ladder)
    angle = positions.astype(jnp.float32)[:, None] * freq[None, :]
    cosine = jnp.cos(angle)[:, None, :]
    sine = jnp.sin(angle)[:, None, :]
    first = values[..., :half]
    second = values[..., half:]
    return jnp.concatenate(
        [first * cosine - second * sine, second * cosine + first * sine], axis=-1
    )


def attend_block(state, key_rows, value_rows, queries, query_pos, scale):
    best, total, accum = state
    rows = key_rows.shape[0]
    heads = queries.shape[1]
    width = queries.shape[2]
    keys_three = key_rows.reshape(rows, heads, width)
    values_three = value_rows.reshape(rows, heads, width)
    scores = (
        jnp.einsum("qhd,khd->hqk", queries, keys_three, preferred_element_type=jnp.float32) * scale
    )
    key_pos = jnp.arange(rows, dtype=jnp.int32)
    allowed = key_pos[None, None, :] <= query_pos[None, :, None]
    block_best = jnp.max(jnp.where(allowed, scores, MASKED), axis=-1)
    new_best = jnp.maximum(best, block_best)
    weights = jnp.where(allowed, jnp.exp(scores - new_best[..., None]), 0.0)
    total = jnp.sum(weights, axis=-1)
    product = jnp.einsum(
        "hqk,khd->hqd",
        weights.astype(jnp.bfloat16),
        values_three,
        preferred_element_type=jnp.float32,
    )
    accum = product
    return (new_best, total, accum)


def local(
    text_embed, frame_feats, frame_count, proj_weight, norm_gain, q_weight, k_weight, v_weight
):
    tok_rows = text_embed.shape[0]
    vision = jnp.dot(
        lax.all_gather(frame_feats, ("section", "tp"), axis=1, tiled=True),
        proj_weight,
        preferred_element_type=jnp.float32,
    )
    offsets = jnp.arange(tok_rows, dtype=jnp.int32)
    is_frame = offsets < frame_count[0]
    joined = jnp.where(is_frame[:, None], vision, text_embed.astype(jnp.float32)).astype(
        jnp.bfloat16
    )
    whole = lax.all_gather(joined, ("section", "tp"), axis=1, tiled=True)
    wide = whole.astype(jnp.float32)
    mean_square = jnp.mean(wide * wide, axis=-1, keepdims=True)
    normed = (wide * lax.rsqrt(mean_square + NORM_EPS) * norm_gain.astype(jnp.float32)).astype(
        jnp.bfloat16
    )
    head_cols = q_weight.shape[1]

    def add_rows(piece):
        return jnp.dot(normed, piece, preferred_element_type=jnp.float32)

    q_full = add_rows(lax.all_gather(q_weight, "ctx", axis=0, tiled=True))
    k_full = add_rows(lax.all_gather(k_weight, "ctx", axis=0, tiled=True))
    v_full = add_rows(lax.all_gather(v_weight, "ctx", axis=0, tiled=True))
    first_pos = lax.axis_index("ctx") * tok_rows
    query_pos = first_pos + offsets
    heads = head_cols // HD
    queries = rotate(q_full.reshape(tok_rows, heads, HD), query_pos).astype(jnp.bfloat16)
    keys = (
        rotate(k_full.reshape(tok_rows, heads, HD), query_pos)
        .astype(jnp.bfloat16)
        .reshape(tok_rows, head_cols)
    )
    values = v_full.astype(jnp.bfloat16)
    scale = 1.0 / math.sqrt(HD)
    initial = (
        jnp.full((heads, tok_rows), MASKED, jnp.float32),
        jnp.zeros((heads, tok_rows), jnp.float32),
        jnp.zeros((heads, tok_rows, HD), jnp.float32),
    )
    state = attend_block(
        initial,
        lax.all_gather(keys, "ctx", axis=0, tiled=True),
        lax.all_gather(values, "ctx", axis=0, tiled=True),
        queries,
        query_pos,
        scale,
    )
    best, total, accum = state
    result = accum / total[..., None]
    return result.transpose(1, 0, 2).reshape(tok_rows, head_cols).astype(jnp.bfloat16)


def solution(mesh):
    in_specs = (
        P("ctx", ("section", "tp")),
        P("ctx", ("section", "tp")),
        P("ctx"),
        P(None, ("section", "tp")),
        P(),
        P("ctx", ("section", "tp")),
        P("ctx", ("section", "tp")),
        P("ctx", ("section", "tp")),
    )
    out_specs = P("ctx", ("section", "tp"))
    return jax.shard_map(local, mesh=mesh, in_specs=in_specs, out_specs=out_specs, check_vma=False)
```

profile of v0, /device:TPU:1, one launch (start us, length us, event | category | flops | bytes accessed | tf_op | source)
XLA Modules:
  0.0 779.1 jit_solution(16113145483510165626)
XLA Ops:
  6.5 63.1 %all_gather.21 = bf16[128,1024]{1,0:T(8,128)(2,1)S(1)} all-gather(bf16[128,128]{1,0:T(8,128)(2,1)} %param.9), channel_id=1, replica_groups=mesh['ctx'=64,'section'=2,'tp'=4] {'section','tp'}, dimensions={1}, use_global_device_ids=true | all-gather | bytes 294912 | tf_op jit(solution)/shard_map/all_gather | solution.py:61
  70.4 1.9 fusion.10
  72.3 0.7 all-gather.9.cloned.1.call-update
  73.1 0.7 all-gather.11.cloned.1.call-update
  73.8 0.5 all-gather.15.cloned.1.call-update
  74.4 0.7 convert_element_type.44
  75.4 86.0 %all-gather.7.cloned.1.call-done = bf16[128,4096]{1,0:T(8,128)(2,1)} async-done(((bf16[128,512]{1,0:T(8,128)(2,1)}), bf16[128,4096]{1,0:T(8,128)(2,1)}) %all-gather.7.cloned.1.call-update) | async-done | bytes 1048592 | tf_op jit(solution)/shard_map/all_gather | solution.py:70
  161.5 1.6 fusion.7
  163.1 113.9 %all-gather.9.cloned.1.call-done = bf16[4096,256]{1,0:T(8,128)(2,1)} async-done(((bf16[64,256]{1,0:T(8,128)(2,1)}), bf16[4096,256]{1,0:T(8,128)(2,1)}) %all-gather.9.cloned.1.call-update) | async-done | bytes 2097168 | tf_op jit(solution)/shard_map/all_gather | solution.py:81
  277.0 2.4 fusion.29
  279.5 116.2 %all-gather.11.cloned.1.call-done = bf16[4096,256]{1,0:T(8,128)(2,1)} async-done(((bf16[64,256]{1,0:T(8,128)(2,1)}), bf16[4096,256]{1,0:T(8,128)(2,1)}) %all-gather.11.cloned.1.call-update) | async-done | bytes 2097168 | tf_op jit(solution)/shard_map/all_gather | solution.py:82
  395.7 2.1 fusion.27
  398.4 0.7 copy.19
  399.2 115.1 %all-gather.15.cloned.1.call-done = bf16[4096,256]{1,0:T(8,128)(2,1)} async-done(((bf16[64,256]{1,0:T(8,128)(2,1)}), bf16[4096,256]{1,0:T(8,128)(2,1)}) %all-gather.15.cloned.1.call-update) | async-done | bytes 2097168 | tf_op jit(solution)/shard_map/all_gather | solution.py:83
  514.2 2.7 convolution_convert_fusion
  517.0 0.7 iota_compare_fusion
  517.7 119.6 %all-gather.13.cloned.1.call-done = bf16[8192,256]{0,1:T(8,128)(2,1)} async-done(((bf16[128,256]{0,1:T(8,128)(2,1)}), bf16[8192,256]{0,1:T(8,128)(2,1)}) %all-gather.13.cloned.1.call-update) | async-done | bytes 4194320 | tf_op jit(solution)/shard_map/all_gather | solution.py:102
  637.2 4.7 select_reduce_fusion
  641.9 3.2 copy-done.1
  645.1 2.1 fusion
  647.3 111.5 %all-gather.17.cloned.1.call-done = bf16[8192,256]{1,0:T(8,128)(2,1)} async-done(((bf16[128,256]{1,0:T(8,128)(2,1)}), bf16[8192,256]{1,0:T(8,128)(2,1)}) %all-gather.17.cloned.1.call-update) | async-done | bytes 4194320 | tf_op jit(solution)/shard_map/all_gather | solution.py:103
  758.7 6.4 copy.24
  765.2 6.4 fusion.17
  771.5 0.7 copy.22
  (26 shorter events, 1.3 us)
Async XLA Ops:
  6.5 63.8 %copy-start = (bf16[1024,512]{1,0:T(8,128)(2,1)S(1)}, bf16[1024,512]{1,0:T(8,128)(2,1)}, u32[]{:S(2)}) copy-start(bf16[1024,512]{1,0:T(8,128)(2,1)} %param.11) | copy-start | bytes 3145732
  6.5 154.9 %all-gather.7.cloned.1.call-start = ((), (), s32[]{:S(2)}) async-start(), calls=%async_computation | async-start | bytes 1179648 | tf_op jit(solution)/shard_map/all_gather | solution.py:70
  72.3 204.7 %all-gather.9.cloned.1.call-start = ((), (), s32[]{:S(2)}) async-start(), calls=%async_computation.1 | async-start | bytes 2129920 | tf_op jit(solution)/shard_map/all_gather | solution.py:81
  73.0 322.7 %all-gather.11.cloned.1.call-start = ((), (), s32[]{:S(2)}) async-start(), calls=%async_computation.2 | async-start | bytes 2129920 | tf_op jit(solution)/shard_map/all_gather | solution.py:82
  73.8 440.5 %all-gather.15.cloned.1.call-start = ((), (), s32[]{:S(2)}) async-start(), calls=%async_computation.4 | async-start | bytes 2129920 | tf_op jit(solution)/shard_map/all_gather | solution.py:83
  74.3 562.9 %all-gather.13.cloned.1.call-start = ((), (), s32[]{:S(2)}) async-start(), calls=%async_computation.3 | async-start | bytes 4259840 | tf_op jit(solution)/shard_map/all_gather | solution.py:102
  161.5 234.2 %copy-start.2 = (bf16[128,4096]{1,0:T(8,128)(2,1)S(1)}, bf16[128,4096]{1,0:T(8,128)(2,1)}, u32[]{:S(2)}) copy-start(bf16[128,4096]{1,0:T(8,128)(2,1)} %all-gather.7.cloned.1.call-done) | copy-start | bytes 3145732
  399.1 359.6 %all-gather.17.cloned.1.call-start = ((), (), s32[]{:S(2)}) async-start(), calls=%async_computation.5 | async-start | bytes 4259840 | tf_op jit(solution)/shard_map/all_gather | solution.py:103
  641.9 3.2 copy-start.1
Sparse Core Ops, SparseCore 0:
  72.4 89.0 all-gather.6
  163.6 113.3 all-gather.8
  279.1 116.4 all-gather.10
  397.7 116.4 all-gather.14
  516.1 121.0 all-gather.12
  639.2 119.4 all-gather.16
where the time goes:
time: 780 us; the launch traced here: 779 us
  waiting for transfers between devices  664 us (85%)
  blocking collectives  63.1 us (8%)
  matrix products  20.1 us (3%)
  between operations  14.2 us (2%)
  local copies, waits for them, and re-layouts  11.6 us (1%)
    all_gather x1, waiting for transfers between devices, local(): lax.all_gather(keys, 'ctx', axis=0, tiled=True)  120 us
    all_gather x1, waiting for transfers between devices, local(): k_full = add_rows(lax.all_gather(k_weight, 'ctx', axis=0, tiled=True))  116 us
    all_gather x1, waiting for transfers between devices, local(): v_full = add_rows(lax.all_gather(v_weight, 'ctx', axis=0, tiled=True))  115 us
    all_gather x1, waiting for transfers between devices, local(): q_full = add_rows(lax.all_gather(q_weight, 'ctx', axis=0, tiled=True))  114 us
    all_gather x1, waiting for transfers between devices, local(): lax.all_gather(values, 'ctx', axis=0, tiled=True)  111 us
    all_gather x1, waiting for transfers between devices, local(): whole = lax.all_gather(joined, ('section', 'tp'), axis=1, tiled=True)  86 us
    all_gather x1, blocking collectives, local(): lax.all_gather(frame_feats, ('section', 'tp'), axis=1, tiled=True)  63.1 us
  transfers between devices with their start and end apart: 6, of which 6 were waited for; matrix products, arithmetic and copies ran while one was open for 2% of the time, Pallas kernels for 0%

commit v1 on v0

v1 whole, which is shorter than its diff:
```python
import math

import jax
import jax.numpy as jnp
from jax import lax
from jax.sharding import Mesh, PartitionSpec as P

HD = 128
ROPE_BASE = 1000000.0
NORM_EPS = 1e-05
MASKED = -1e30

Z, Y, CORES, SECTIONS, TP = 8, 4, 2, 2, 4
F = ("section", "tp")


def gather(v, axes, n):
    return lax.all_to_all(
        jnp.broadcast_to(v[None], (n, *v.shape)), axes, split_axis=0, concat_axis=0, tiled=True
    )


def rotate(values, positions):
    half = values.shape[-1] // 2
    ladder = jnp.arange(half, dtype=jnp.float32) * 2.0 / values.shape[-1]
    freq = ROPE_BASE ** (-ladder)
    angle = positions.astype(jnp.float32)[:, None] * freq[None, :]
    cosine = jnp.cos(angle)
    sine = jnp.sin(angle)
    first = values[..., :half]
    second = values[..., half:]
    return jnp.concatenate(
        [first * cosine - second * sine, second * cosine + first * sine], axis=-1
    )


def local(text, feats, count, proj, gain, q_weight, k_weight, v_weight):
    rows = text.shape[0]
    z, y, core = lax.axis_index("z"), lax.axis_index("y"), lax.axis_index("core")

    weight = jnp.stack([q_weight, k_weight, v_weight], axis=1).reshape(64, 3, 2, HD)
    weight = weight.transpose(2, 0, 1, 3).reshape(2, 64, 3 * HD)
    weight = lax.all_to_all(weight, "core", 0, 0, tiled=True).reshape(128, 3 * HD)
    weight = gather(weight, "z", Z)
    weight = gather(weight, "y", Y)

    feats_all = gather(feats, F, 8)
    vision = jnp.einsum(
        "frk,fkn->rn", feats_all, proj.reshape(8, 128, 512), preferred_element_type=jnp.float32
    )
    is_frame = jnp.arange(rows, dtype=jnp.int32) < count[0]
    joined = jnp.where(is_frame[:, None], vision, text.astype(jnp.float32)).astype(jnp.bfloat16)

    swapped = gather(joined, "section", SECTIONS)
    whole = gather(swapped, "tp", TP)
    whole = gather(whole, "core", CORES)
    whole = whole.transpose(0, 3, 2, 1, 4).reshape(2 * rows, 4096)
    wide = whole.astype(jnp.float32)
    mean_square = jnp.mean(wide * wide, axis=-1, keepdims=True)
    normed = (wide * lax.rsqrt(mean_square + NORM_EPS) * gain.astype(jnp.float32)).astype(
        jnp.bfloat16
    )
    qkv = jnp.einsum(
        "rzyk,yzkn->rn",
        normed.reshape(2 * rows, Z, Y, HD),
        weight.reshape(Y, Z, HD, 3 * HD),
        preferred_element_type=jnp.float32,
    )
    chip_rows = 2 * rows
    pos = (z * Y + y) * chip_rows + jnp.arange(chip_rows, dtype=jnp.int32)
    queries = rotate(qkv[:, :HD], pos).astype(jnp.bfloat16)
    keys = rotate(qkv[:, HD : 2 * HD], pos).astype(jnp.bfloat16)
    values = qkv[:, 2 * HD :].astype(jnp.bfloat16)

    kv = gather(jnp.concatenate([keys, values], axis=1), "z", Z).reshape(Z * chip_rows, 2 * HD)
    q_all = gather(queries, "y", Y).reshape(Y * chip_rows, HD)
    q_pos = z * (Y * chip_rows) + jnp.arange(Y * chip_rows, dtype=jnp.int32)
    k_pos = (
        jnp.arange(Z, dtype=jnp.int32)[:, None] * (Y * chip_rows)
        + y * chip_rows
        + jnp.arange(chip_rows, dtype=jnp.int32)[None, :]
    ).reshape(-1)
    scores = jnp.dot(q_all, kv[:, :HD].T, preferred_element_type=jnp.float32) / math.sqrt(HD)
    allowed = k_pos[None, :] <= q_pos[:, None]
    best = jnp.max(jnp.where(allowed, scores, MASKED), axis=-1)
    weights = jnp.where(allowed, jnp.exp(scores - best[:, None]), 0.0)
    total = jnp.sum(weights, axis=-1)
    product = jnp.dot(weights.astype(jnp.bfloat16), kv[:, HD:], preferred_element_type=jnp.float32)
    part = product / jnp.where(total > 0.0, total, 1.0)[:, None]
    lse = jnp.where(total > 0.0, best + jnp.log(jnp.where(total > 0.0, total, 1.0)), MASKED)

    parts = lax.all_to_all(
        part.astype(jnp.bfloat16).reshape(Y, chip_rows, HD), "y", 0, 0, tiled=True
    )
    lses = lax.all_to_all(lse.reshape(Y, 2, HD), "y", 0, 0, tiled=True).reshape(Y, chip_rows)
    top = jnp.max(lses, axis=0)
    share = jnp.exp(lses - top)
    share = share / jnp.sum(share, axis=0)
    result = jnp.sum(parts.astype(jnp.float32) * share[..., None], axis=0).astype(jnp.bfloat16)

    result = lax.all_to_all(result.reshape(2, rows, HD), "core", 0, 0, tiled=True)
    return result.transpose(1, 0, 2).reshape(rows, 2 * HD)


def solution(mesh):
    fine = Mesh(
        mesh.devices.reshape(Z, Y, CORES, SECTIONS, TP), ("z", "y", "core", "section", "tp")
    )
    ctx = ("z", "y", "core")
    in_specs = (P(ctx, F), P(ctx, F), P(ctx), P(None, F), P(), P(ctx, F), P(ctx, F), P(ctx, F))
    return jax.shard_map(
        local, mesh=fine, in_specs=in_specs, out_specs=P(ctx, F), check_vma=False
    )
```

time: 780 us -> 284 us (0.36)
  waiting for transfers between devices: 664 us -> 93.8 us
  starting transfers between devices: 0.2 us -> 55.5 us
  blocking collectives: 63.1 us -> 94.3 us
  between operations: 14.2 us -> 1 us
  matrix products: 20.1 us -> 11.8 us
    all_gather x6 -> x0, waiting for transfers between devices: 662 us -> none  [the longest x1 120 us: local(): lax.all_gather(keys, 'ctx', axis=0, tiled=True)]
    all_to_all x0 -> x4, blocking collectives: none -> 94.3 us  [the longest x3 72.3 us: gather(): lax.all_to_all(jnp.broadcast_to(v[None], (n, *v.shape)), axes, split_axis...]
    all_to_all x0 -> x8, waiting for transfers between devices: none -> 93.8 us  [the longest x5 87.3 us: gather(): lax.all_to_all(jnp.broadcast_to(v[None], (n, *v.shape)), axes, split_axis...]
    all_gather x1 -> x0, blocking collectives: 63.1 us -> none  [local(): lax.all_gather(frame_feats, ('section', 'tp'), axis=1, tiled=True)]
    all_to_all x0 -> x8, starting transfers between devices: none -> 55.5 us  [the longest x5 35.2 us: gather(): lax.all_to_all(jnp.broadcast_to(v[None], (n, *v.shape)), axes, split_axis...]
    dot_general x6 -> x4, matrix products: 20.1 us -> 11.8 us  [the longest x1 5.85 us: local(): jnp.dot(weights.astype(jnp.bfloat16), kv[:, HD:], preferred_element_type=...]
  transfers between devices with their start and end apart: 6 -> 8, of which waited for: 6 -> 7; matrix products, arithmetic and copies ran while one was open for 2% -> 7% of each run, Pallas kernels for 0% -> 0%
where the time goes in v1:
time: 284 us; the launch traced here: 283 us
  blocking collectives  94.3 us (33%)
  waiting for transfers between devices  93.8 us (33%)
  starting transfers between devices  55.5 us (20%)
  local copies, waits for them, and re-layouts  18.1 us (6%)
  matrix products  11.8 us (4%)
  other arithmetic  8.25 us (3%)
    all_to_all x5, waiting for transfers between devices, gather(): lax.all_to_all(jnp.broadcast_to(v[None], (n, *v.shape)), axes, split_axis...  87.3 us
    all_to_all x3, blocking collectives, gather(): lax.all_to_all(jnp.broadcast_to(v[None], (n, *v.shape)), axes, split_axis...  72.3 us
    all_to_all x5, starting transfers between devices, gather(): lax.all_to_all(jnp.broadcast_to(v[None], (n, *v.shape)), axes, split_axis...  35.2 us
    all_to_all x1, blocking collectives, local(): lax.all_to_all(result.reshape(2, rows, HD), 'core', 0, 0, tiled=True)  22.1 us
    all_to_all x1, starting transfers between devices, local(): lax.all_to_all(weight, 'core', 0, 0, tiled=True).reshape(128, 3 * HD)  12.8 us
    convert_element_type x2, local copies, waits for them, and re-layouts, local(): wide = whole.astype(jnp.float32)  7.91 us
    broadcast_in_dim x8, local copies, waits for them, and re-layouts, gather(): jnp.broadcast_to(v[None], (n, *v.shape))  6.9 us
    dot_general x1, matrix products, local(): jnp.dot(weights.astype(jnp.bfloat16), kv[:, HD:], preferred_element_type=...  5.85 us
  transfers between devices with their start and end apart: 8, of which 7 were waited for; matrix products, arithmetic and copies ran while one was open for 7% of the time, Pallas kernels for 0%

profile of v1, /device:TPU:1, one launch (start us, length us, event | category | flops | bytes accessed | tf_op | source)
XLA Modules:
  0.0 282.7 jit_solution(8640830196267066059)
XLA Ops:
  1.6 18.1 %all-to-all-start = ((bf16[8,128,128]{2,1,0:T(8,128)(2,1)}), bf16[8,128,128]{2,1,0:T(8,128)(2,1)S(1)}, u32[]{:S(2)}, u32[]{:S(2)}) async-start(bf16[8,128,128]{2,1,0:T(8,128)(2,1)} %broadcast_in_dim.42), calls=%async_computation | async-start | bytes 524288 | tf_op jit(solution)/shard_map/all_to_all | solution.py:18
  20.4 14.6 %all-to-all-done = bf16[8,128,128]{2,1,0:T(8,128)(2,1)S(1)} async-done(((bf16[8,128,128]{2,1,0:T(8,128)(2,1)}), bf16[8,128,128]{2,1,0:T(8,128)(2,1)S(1)}, u32[]{:S(2)}, u32[]{:S(2)}) %all-to-all-start) | async-done | bytes 262176 | tf_op jit(solution)/shard_map/all_to_all | solution.py:18
  36.2 16.2 %all_to_all.60 = bf16[2,128,512]{2,1,0:T(8,128)(2,1)S(1)} all-to-all(bf16[2,128,512]{2,1,0:T(8,128)(2,1)S(1)} %broadcast_in_dim.43), channel_id=1, replica_groups=mesh['z'=8,'y'=4,'core'=2,'section'=2,'tp'=4] {'section'}, dimensions={0} | all-to-all | bytes 524288 | tf_op jit(solution)/shard_map/all_to_all | solution.py:18
  53.5 3.5 %all-to-all-start.2 = ((bf16[4,2,128,512]{3,2,1,0:T(8,128)(2,1)}), bf16[4,2,128,512]{3,2,1,0:T(8,128)(2,1)S(1)}, u32[]{:S(2)}, u32[]{:S(2)}) async-start(bf16[4,2,128,512]{3,2,1,0:T(8,128)(2,1)} %broadcast_in_dim.44), calls=%async_computation.2 | async-start | bytes 2097152 | tf_op jit(solution)/shard_map/all_to_all | solution.py:18
  58.2 8.5 %all-to-all-done.2 = bf16[4,2,128,512]{3,2,1,0:T(8,128)(2,1)S(1)} async-done(((bf16[4,2,128,512]{3,2,1,0:T(8,128)(2,1)}), bf16[4,2,128,512]{3,2,1,0:T(8,128)(2,1)S(1)}, u32[]{:S(2)}, u32[]{:S(2)}) %all-to-all-start.2) | async-done | bytes 1048608 | tf_op jit(solution)/shard_map/all_to_all | solution.py:18
  66.7 12.8 %all-to-all-start.4 = ((bf16[2,64,384]{2,1,0:T(8,128)(2,1)}), bf16[2,64,384]{2,1,0:T(8,128)(2,1)S(1)}, u32[]{:S(2)}, u32[]{:S(2)}) async-start(bf16[2,64,384]{2,1,0:T(8,128)(2,1)} %reshape.180), calls=%async_computation.4 | async-start | bytes 196608 | tf_op jit(solution)/shard_map/all_to_all | solution.py:43
  80.8 5.4 %all_to_all.61 = bf16[2,4,2,128,512]{4,3,1,2,0:T(8,128)(2,1)S(1)} all-to-all(bf16[2,4,2,128,512]{4,3,1,2,0:T(8,128)(2,1)S(1)} %broadcast_in_dim.45), channel_id=1, replica_groups=mesh['z'=8,'y'=4,'core'=2,'section'=2,'tp'=4] {'core'}, dimensions={0} | all-to-all | bytes 4194304 | tf_op jit(solution)/shard_map/all_to_all | solution.py:18
  86.3 50.6 %all_to_all.62 = bf16[8,128,384]{2,1,0:T(8,128)(2,1)S(1)} all-to-all(bf16[8,128,384]{2,1,0:T(8,128)(2,1)S(1)} %broadcast_in_dim.47), channel_id=1, replica_groups=mesh['z'=8,'y'=4,'core'=2,'section'=2,'tp'=4] {'z'}, dimensions={0} | all-to-all | bytes 1572864 | tf_op jit(solution)/shard_map/all_to_all | solution.py:18
  139.2 4.7 %all-to-all-start.6 = ((bf16[4,8,128,384]{3,2,1,0:T(8,128)(2,1)}), bf16[4,8,128,384]{3,2,1,0:T(8,128)(2,1)}, u32[]{:S(2)}, u32[]{:S(2)}) async-start(bf16[4,8,128,384]{3,2,1,0:T(8,128)(2,1)} %broadcast_in_dim.49), calls=%async_computation.6 | async-start | bytes 6291456 | tf_op jit(solution)/shard_map/all_to_all | solution.py:18
  144.5 2.7 copy.28
  147.2 5.3 %reshape.186 = f32[256,8,4,128]{3,2,0,1:T(4,128)} reshape(f32[2,128,2,4,512]{4,1,0,3,2:T(8,128)} %copy.28) | data formatting | bytes 8388608 | tf_op jit(solution)/shard_map/convert_element_type | solution.py:58
  152.9 2.9 %multiply_convert_fusion = bf16[256,8,4,128]{3,2,0,1:T(4,128)(2,1)S(1)} fusion(f32[256,8,4,128]{3,2,0,1:T(4,128)} %reshape.186, f32[8,4,128]{2,1,0:T(4,128)S(1)} %convert.23, f32[256]{0:T(256)S(1)} %rsqrt_bitcast_fusion), kind=kLoop, calls=%fused_computation.8 | loop fusion | flops 3145728 | bytes 6308864 | tf_op jit(solution)/shard_map/convert_element_type | solution.py:60
  155.8 23.9 %all-to-all-done.6 = bf16[4,8,128,384]{3,2,1,0:T(8,128)(2,1)} async-done(((bf16[4,8,128,384]{3,2,1,0:T(8,128)(2,1)}), bf16[4,8,128,384]{3,2,1,0:T(8,128)(2,1)}, u32[]{:S(2)}, u32[]{:S(2)}) %all-to-all-start.6) | async-done | bytes 3145760 | tf_op jit(solution)/shard_map/all_to_all | solution.py:18
  179.7 3.1 %fusion.8 = f32[256,384]{1,0:T(8,128)S(1)} fusion(bf16[4,8,128,384]{3,2,1,0:T(8,128)(2,1)} %all-to-all-done.6, bf16[256,8,4,128]{3,2,0,1:T(4,128)(2,1)S(1)} %multiply_convert_fusion), kind=kOutput, calls=%fused_computation.12 | convolution fusion | flops 805306368 | bytes 5636096 | tf_op jit(solution)/shard_map/rzyk,yzkn->rn/dot_general | solution.py:63
  184.6 3.4 %all-to-all-start.7 = ((bf16[4,256,128]{2,1,0:T(8,128)(2,1)}), bf16[4,256,128]{2,1,0:T(8,128)(2,1)S(1)}, u32[]{:S(2)}, u32[]{:S(2)}) async-start(bf16[4,256,128]{2,1,0:T(8,128)(2,1)} %broadcast_in_dim.50), calls=%async_computation.7 | async-start | bytes 524288 | tf_op jit(solution)/shard_map/all_to_all | solution.py:18
  188.3 5.1 %all-to-all-done.7 = bf16[4,256,128]{2,1,0:T(8,128)(2,1)S(1)} async-done(((bf16[4,256,128]{2,1,0:T(8,128)(2,1)}), bf16[4,256,128]{2,1,0:T(8,128)(2,1)S(1)}, u32[]{:S(2)}, u32[]{:S(2)}) %all-to-all-start.7) | async-done | bytes 262176 | tf_op jit(solution)/shard_map/all_to_all | solution.py:18
  194.5 5.5 %all-to-all-start.8 = ((bf16[8,256,256]{2,1,0:T(8,128)(2,1)}), bf16[8,256,256]{2,1,0:T(8,128)(2,1)S(1)}, u32[]{:S(2)}, u32[]{:S(2)}) async-start(bf16[8,256,256]{2,1,0:T(8,128)(2,1)} %broadcast_in_dim.52), calls=%async_computation.8 | async-start | bytes 2097152 | tf_op jit(solution)/shard_map/all_to_all | solution.py:18
  200.1 35.2 %all-to-all-done.8 = bf16[8,256,256]{2,1,0:T(8,128)(2,1)S(1)} async-done(((bf16[8,256,256]{2,1,0:T(8,128)(2,1)}), bf16[8,256,256]{2,1,0:T(8,128)(2,1)S(1)}, u32[]{:S(2)}, u32[]{:S(2)}) %all-to-all-start.8) | async-done | bytes 1048608 | tf_op jit(solution)/shard_map/all_to_all | solution.py:18
  236.9 2.6 fusion.1
  240.7 3.2 %all-to-all-start.10 = ((f32[4,2,128]{2,1,0:T(2,128)}), f32[4,2,128]{2,1,0:T(2,128)S(1)}, u32[]{:S(2)}, u32[]{:S(2)}) async-start(f32[4,2,128]{2,1,0:T(2,128)} %compare_select_fusion.3), calls=%async_computation.10 | async-start | bytes 8192 | tf_op jit(solution)/shard_map/all_to_all | solution.py:95
  244.0 5.9 %fusion.16 = bf16[1024,128]{1,0:T(8,128)(2,1)} fusion(f32[1024,2048]{1,0:T(8,128)} %copy-done.1, f32[1024]{0:T(1024)S(1)} %get-tuple-element.15, s32[2048]{0:T(1024)S(1)} %bitcast.62, s32[1024]{0:T(1024)S(1)} %iota_add_fusion, bf16[2048,256]{1,0:T(8,128)(2,1)S(1)} %bitcast.52, f32[1024]{0:T(1024)S(1)} %compare_select_fusion.2), kind=kOutput, calls=%fused_computation.17 | convolution fusion | flops 547618816 | bytes 9195520 | tf_op jit(solution)/shard_map/dot_general | solution.py:88
  249.8 4.2 %all-to-all-start.9 = ((bf16[4,256,128]{2,1,0:T(8,128)(2,1)}), bf16[4,256,128]{2,1,0:T(8,128)(2,1)S(1)}, u32[]{:S(2)}, u32[]{:S(2)}) async-start(bf16[4,256,128]{2,1,0:T(8,128)(2,1)} %bitcast.13), calls=%async_computation.9 | async-start | bytes 524288 | tf_op jit(solution)/shard_map/all_to_all | solution.py:92
  254.1 5.5 %all-to-all-done.9 = bf16[4,256,128]{2,1,0:T(8,128)(2,1)S(1)} async-done(((bf16[4,256,128]{2,1,0:T(8,128)(2,1)}), bf16[4,256,128]{2,1,0:T(8,128)(2,1)S(1)}, u32[]{:S(2)}, u32[]{:S(2)}) %all-to-all-start.9) | async-done | bytes 262176 | tf_op jit(solution)/shard_map/all_to_all | solution.py:92
  259.8 22.1 %all_to_all.63 = bf16[2,128,128]{2,1,0:T(8,128)(2,1)S(1)} all-to-all(bf16[2,128,128]{2,1,0:T(8,128)(2,1)S(1)} %bitcast.57), channel_id=1, replica_groups=mesh['z'=8,'y'=4,'core'=2,'section'=2,'tp'=4] {'core'}, dimensions={0} | all-to-all | bytes 131072 | tf_op jit(solution)/shard_map/all_to_all | solution.py:101
  (64 shorter events, 16.7 us)
Async XLA Ops:
  0.0 35.0 %copy-start = (bf16[1024,512]{1,0:T(8,128)(2,1)S(1)}, bf16[1024,512]{1,0:T(8,128)(2,1)}, u32[]{:S(2)}) copy-start(bf16[1024,512]{1,0:T(8,128)(2,1)} %param.11) | copy-start | bytes 3145732
  0.0 57.0 %copy-start.2 = (bf16[64,256]{1,0:T(8,128)(2,1)S(1)}, bf16[64,256]{1,0:T(8,128)(2,1)}, u32[]{:S(2)}) copy-start(bf16[64,256]{1,0:T(8,128)(2,1)} %param.13) | copy-start | bytes 98308
  0.0 57.1 %copy-start.3 = (bf16[64,256]{1,0:T(8,128)(2,1)S(1)}, bf16[64,256]{1,0:T(8,128)(2,1)}, u32[]{:S(2)}) copy-start(bf16[64,256]{1,0:T(8,128)(2,1)} %param.14) | copy-start | bytes 98308
  0.0 57.2 %copy-start.4 = (bf16[64,256]{1,0:T(8,128)(2,1)S(1)}, bf16[64,256]{1,0:T(8,128)(2,1)}, u32[]{:S(2)}) copy-start(bf16[64,256]{1,0:T(8,128)(2,1)} %param.15) | copy-start | bytes 98308
  1.6 33.4 %all-to-all-start = ((bf16[8,128,128]{2,1,0:T(8,128)(2,1)}), bf16[8,128,128]{2,1,0:T(8,128)(2,1)S(1)}, u32[]{:S(2)}, u32[]{:S(2)}) async-start(bf16[8,128,128]{2,1,0:T(8,128)(2,1)} %broadcast_in_dim.42), calls=%async_computation | async-start | bytes 524288 | tf_op jit(solution)/shard_map/all_to_all | solution.py:18
  53.5 13.2 %all-to-all-start.2 = ((bf16[4,2,128,512]{3,2,1,0:T(8,128)(2,1)}), bf16[4,2,128,512]{3,2,1,0:T(8,128)(2,1)S(1)}, u32[]{:S(2)}, u32[]{:S(2)}) async-start(bf16[4,2,128,512]{3,2,1,0:T(8,128)(2,1)} %broadcast_in_dim.44), calls=%async_computation.2 | async-start | bytes 2097152 | tf_op jit(solution)/shard_map/all_to_all | solution.py:18
  66.7 13.9 %all-to-all-start.4 = ((bf16[2,64,384]{2,1,0:T(8,128)(2,1)}), bf16[2,64,384]{2,1,0:T(8,128)(2,1)S(1)}, u32[]{:S(2)}, u32[]{:S(2)}) async-start(bf16[2,64,384]{2,1,0:T(8,128)(2,1)} %reshape.180), calls=%async_computation.4 | async-start | bytes 196608 | tf_op jit(solution)/shard_map/all_to_all | solution.py:43
  137.0 6.9 %copy-start.5 = (bf16[4096]{0:T(1024)(128)(2,1)S(1)}, bf16[4096]{0:T(1024)(128)(2,1)}, u32[]{:S(2)}) copy-start(bf16[4096]{0:T(1024)(128)(2,1)} %param.12) | copy-start | bytes 24580
  139.2 40.5 %all-to-all-start.6 = ((bf16[4,8,128,384]{3,2,1,0:T(8,128)(2,1)}), bf16[4,8,128,384]{3,2,1,0:T(8,128)(2,1)}, u32[]{:S(2)}, u32[]{:S(2)}) async-start(bf16[4,8,128,384]{3,2,1,0:T(8,128)(2,1)} %broadcast_in_dim.49), calls=%async_computation.6 | async-start | bytes 6291456 | tf_op jit(solution)/shard_map/all_to_all | solution.py:18
  184.6 8.9 %all-to-all-start.7 = ((bf16[4,256,128]{2,1,0:T(8,128)(2,1)}), bf16[4,256,128]{2,1,0:T(8,128)(2,1)S(1)}, u32[]{:S(2)}, u32[]{:S(2)}) async-start(bf16[4,256,128]{2,1,0:T(8,128)(2,1)} %broadcast_in_dim.50), calls=%async_computation.7 | async-start | bytes 524288 | tf_op jit(solution)/shard_map/all_to_all | solution.py:18
  194.5 40.8 %all-to-all-start.8 = ((bf16[8,256,256]{2,1,0:T(8,128)(2,1)}), bf16[8,256,256]{2,1,0:T(8,128)(2,1)S(1)}, u32[]{:S(2)}, u32[]{:S(2)}) async-start(bf16[8,256,256]{2,1,0:T(8,128)(2,1)} %broadcast_in_dim.52), calls=%async_computation.8 | async-start | bytes 2097152 | tf_op jit(solution)/shard_map/all_to_all | solution.py:18
  236.9 3.2 %copy-start.1 = (f32[1024,2048]{1,0:T(8,128)}, f32[1024,2048]{1,0:T(8,128)S(1)}, u32[]{:S(2)}) copy-start(f32[1024,2048]{1,0:T(8,128)S(1)} %get-tuple-element.16) | copy-start | bytes 25165828
  240.7 9.1 %all-to-all-start.10 = ((f32[4,2,128]{2,1,0:T(2,128)}), f32[4,2,128]{2,1,0:T(2,128)S(1)}, u32[]{:S(2)}, u32[]{:S(2)}) async-start(f32[4,2,128]{2,1,0:T(2,128)} %compare_select_fusion.3), calls=%async_computation.10 | async-start | bytes 8192 | tf_op jit(solution)/shard_map/all_to_all | solution.py:95
  249.8 9.7 %all-to-all-start.9 = ((bf16[4,256,128]{2,1,0:T(8,128)(2,1)}), bf16[4,256,128]{2,1,0:T(8,128)(2,1)S(1)}, u32[]{:S(2)}, u32[]{:S(2)}) async-start(bf16[4,256,128]{2,1,0:T(8,128)(2,1)} %bitcast.13), calls=%async_computation.9 | async-start | bytes 524288 | tf_op jit(solution)/shard_map/all_to_all | solution.py:92

commit v2 on v1

v2 whole, which is shorter than its diff:
```python
import math

import jax
import jax.numpy as jnp
from jax import lax
from jax.experimental import pallas as pl
from jax.experimental.pallas import tpu as pltpu
from jax.sharding import Mesh, PartitionSpec as P

HD = 128
ROPE_BASE = 1000000.0
NORM_EPS = 1e-05
MASKED = -1e30

ZH, ZL, Y, CORES, SECTIONS, TP = 2, 4, 4, 2, 2, 4
F = ("section", "tp")
ROWS = 128
CHIP_ROWS = 2 * ROWS
SWAP = [(0, 1), (1, 0)]
VMEM = pl.BlockSpec(memory_space=pltpu.VMEM)
SMEM = pl.BlockSpec(memory_space=pltpu.SMEM)
LIMIT = 40 << 20


def swap(v, axis):
    return lax.ppermute(v, axis, SWAP)


def gather(v, axis, n):
    return lax.all_to_all(jnp.broadcast_to(v[None], (n, *v.shape)), axis, 0, 0, tiled=True)


def join_frames_kernel(pick, feats, proj, text, out):
    vision = jnp.zeros((ROWS, 512), jnp.float32)
    for s in range(SECTIONS):
        first = jnp.bitwise_xor(pick[0], s) * TP
        for t in range(TP):
            vision = vision + jnp.dot(
                feats[t, s], proj[first + t], preferred_element_type=jnp.float32
            )
    row = lax.broadcasted_iota(jnp.int32, (ROWS, 512), 0)
    joined = jnp.where(row < pick[1], vision, text[...].astype(jnp.float32))
    out[...] = joined.astype(jnp.bfloat16)


def project_kernel(
    flip, own_a, own_b, other_a, other_b, stored, gain, cosine, sine, q_out, kv_out, weight, sem
):
    copy = pltpu.make_async_copy(stored, weight, sem)
    copy.start()
    tiles = [(own, other, t) for own, other in ((own_a, other_a), (own_b, other_b)) for t in range(TP)]
    squares = jnp.zeros((CHIP_ROWS, 512), jnp.float32)
    for own, other, t in tiles:
        wide = jnp.concatenate([own[t], other[t]], axis=0).astype(jnp.float32)
        squares = squares + wide * wide
    mean_square = jnp.sum(squares, axis=-1, keepdims=True) * (1.0 / 4096)
    inverse = lax.rsqrt(mean_square + NORM_EPS)
    total = jnp.zeros((CHIP_ROWS, 3 * HD), jnp.float32)
    copy.wait()
    for i, (own, other, t) in enumerate(tiles):
        half = jnp.bitwise_xor(flip[0], i // TP)
        wide = jnp.concatenate([own[t], other[t]], axis=0).astype(jnp.float32)
        normed = (wide * inverse * gain[i : i + 1, :]).astype(jnp.bfloat16)
        block = jnp.concatenate(
            [weight[y, t * CORES + c, half] for y in range(Y) for c in range(CORES)], axis=0
        )
        total = total + jnp.dot(normed, block, preferred_element_type=jnp.float32)
    q = total[:, :HD]
    k = total[:, HD : 2 * HD]
    cos, sin = cosine[...], sine[...]
    q = (q * cos + pltpu.roll(q, HD // 2, 1) * sin).astype(jnp.bfloat16)
    for i in range(Y):
        q_out[i] = q
    kv_out[:, :HD] = (k * cos + pltpu.roll(k, HD // 2, 1) * sin).astype(jnp.bfloat16)
    kv_out[:, HD:] = total[:, 2 * HD :].astype(jnp.bfloat16)


def encode(level):
    lane = lax.broadcasted_iota(jnp.int32, (CHIP_ROWS, HD), 1)
    high = level.astype(jnp.bfloat16).astype(jnp.float32)
    rest = level - high
    middle = rest.astype(jnp.bfloat16).astype(jnp.float32)
    low = rest - middle
    coded = jnp.where(
        lane == 0, high, jnp.where(lane == 1, middle, jnp.where(lane == 2, low, 0.0))
    ).astype(jnp.bfloat16)
    pick = lax.broadcasted_iota(jnp.int32, (8, HD), 0) == lax.broadcasted_iota(jnp.int32, (8, HD), 1)
    pick = pick.astype(jnp.float32).astype(jnp.bfloat16)
    coded = lax.dot_general(
        pick, coded, (((1,), (1,)), ((), ())), preferred_element_type=jnp.float32
    )
    return jnp.concatenate([coded[:, :ROWS], coded[:, ROWS:]], axis=0).astype(jnp.bfloat16)


def decode(coded):
    shape = (ROWS, ROWS)
    eye = lax.broadcasted_iota(jnp.int32, shape, 0) == lax.broadcasted_iota(jnp.int32, shape, 1)
    eye = eye.astype(jnp.float32).astype(jnp.bfloat16)
    c = lax.dot_general(eye, coded, (((1,), (1,)), ((), ())), preferred_element_type=jnp.float32)
    return c[:, 0:1] + c[:, 1:2] + c[:, 2:3]


def attend_kernel(place, queries, kv, out, scores):
    zh, zl, me, core = place[0], place[1], place[2], place[3]
    shape = (CHIP_ROWS, CHIP_ROWS)
    turn = core * ROWS
    row = jnp.bitwise_xor(lax.broadcasted_iota(jnp.int32, shape, 0), turn)
    col = jnp.bitwise_xor(lax.broadcasted_iota(jnp.int32, shape, 1), turn)
    ahead = col - row
    scale = 1.0 / math.sqrt(HD)

    def one(y, carry):
        q = queries[y]
        first_q = (zh * ZL + zl) * (Y * CHIP_ROWS) + y * CHIP_ROWS
        peak = jnp.full(shape, MASKED, jnp.float32)
        for l in range(ZL):
            for h in range(ZH):
                first_k = (jnp.bitwise_xor(zh, h) * ZL + l) * (Y * CHIP_ROWS) + me * CHIP_ROWS
                s = lax.dot_general(
                    q,
                    kv[l, h, :, :HD],
                    (((1,), (1,)), ((), ())),
                    preferred_element_type=jnp.float32,
                )
                s = jnp.where(ahead <= first_q - first_k, s * scale, MASKED)
                scores[l * ZH + h] = s
                peak = jnp.maximum(peak, s)
        best = jnp.max(peak, axis=-1, keepdims=True)
        mass = jnp.zeros(shape, jnp.float32)
        part = jnp.zeros((CHIP_ROWS, HD), jnp.float32)
        for l in range(ZL):
            for h in range(ZH):
                w = jnp.exp(scores[l * ZH + h] - best)
                mass = mass + w
                part = part + jnp.dot(
                    w.astype(jnp.bfloat16), kv[l, h, :, HD:], preferred_element_type=jnp.float32
                )
        total = jnp.sum(mass, axis=-1, keepdims=True)
        level = jnp.where(best > 0.5 * MASKED, best + jnp.log(total), MASKED)
        coded = encode(level)
        part = (part / total).astype(jnp.bfloat16)
        for i in range(CORES):
            owner = y * CORES + jnp.bitwise_xor(core, i)
            out[owner, :ROWS, :] = part[i * ROWS : (i + 1) * ROWS]
            out[owner, ROWS:, :] = coded[i * 8 : (i + 1) * 8]
        return carry

    lax.fori_loop(0, Y, one, 0)


def merge_kernel(parts, out):
    for h in range(CORES):
        blocks = [parts[y * CORES + h] for y in range(Y)]
        levels = [decode(block[ROWS:, :]) for block in blocks]
        top = jnp.maximum(jnp.maximum(levels[0], levels[1]), jnp.maximum(levels[2], levels[3]))
        total = jnp.zeros_like(top)
        result = jnp.zeros((ROWS, HD), jnp.float32)
        for level, block in zip(levels, blocks):
            share = jnp.exp(level - top)
            total = total + share
            result = result + share * block[:ROWS, :].astype(jnp.float32)
        out[:, h * HD : (h + 1) * HD] = (result / total).astype(jnp.bfloat16)


def join_kernel(q, k, v, out, sems):
    copies = [
        pltpu.make_async_copy(w, out.at[:, i * 2 * HD : (i + 1) * 2 * HD], sems.at[i])
        for i, w in enumerate((q, k, v))
    ]
    for copy in copies:
        copy.start()
    for copy in copies:
        copy.wait()


def spread_kernel(own, partner, out):
    for h in range(CORES):
        for zr, w in enumerate((own, partner)):
            for i in range(3):
                block = w[:, (2 * i + h) * HD : (2 * i + h + 1) * HD]
                for l in range(ZL):
                    out[l * CORES + h, zr, :, i * HD : (i + 1) * HD] = block


def call(kernel, outs, n_scalars, n_arrays, flops, size, scratch=()):
    return pl.pallas_call(
        kernel,
        out_shape=outs,
        in_specs=[SMEM] * n_scalars + [VMEM] * n_arrays,
        out_specs=[VMEM] * len(outs),
        scratch_shapes=list(scratch),
        compiler_params=pltpu.CompilerParams(vmem_limit_bytes=LIMIT),
        cost_estimate=pl.CostEstimate(flops=flops, bytes_accessed=size, transcendentals=0),
    )


def shaped(*shape):
    return jax.ShapeDtypeStruct(shape, jnp.bfloat16)


def local(text, feats, count, proj, gain, q_weight, k_weight, v_weight):
    zh, zl, y = lax.axis_index("zh"), lax.axis_index("zl"), lax.axis_index("y")
    core, section = lax.axis_index("core"), lax.axis_index("section")

    turned = jnp.bitwise_xor(jnp.arange(CHIP_ROWS, dtype=jnp.int32), core * ROWS)
    position = ((zh * ZL + zl) * Y + y) * CHIP_ROWS + turned
    ladder = jnp.arange(HD // 2, dtype=jnp.float32) * 2.0 / HD
    angle = position.astype(jnp.float32)[:, None] * (ROPE_BASE ** (-ladder))[None, :]
    cosine = jnp.cos(angle)
    sine = jnp.sin(angle)
    cosine = jnp.concatenate([cosine, cosine], axis=-1)
    sine = jnp.concatenate([-sine, sine], axis=-1)
    gains = gain.astype(jnp.float32).reshape(SECTIONS, TP, 512)
    gains = jnp.where(section == 0, gains, gains[::-1]).reshape(8, 512)
    feats_b = swap(feats, "section")
    weight = pl.pallas_call(
        join_kernel,
        out_shape=shaped(64, 6 * HD),
        in_specs=[pl.BlockSpec(memory_space=pl.ANY)] * 3,
        out_specs=VMEM,
        scratch_shapes=[pltpu.SemaphoreType.DMA((3,))],
        cost_estimate=pl.CostEstimate(flops=0, bytes_accessed=200000, transcendentals=0),
    )(q_weight, k_weight, v_weight)
    weight_b = swap(weight, "zh")

    weight_b, feats_b = lax.optimization_barrier((weight_b, feats_b))
    (weight,) = call(spread_kernel, [shaped(ZL * CORES, ZH, 64, 3 * HD)], 0, 2, 1000, 1 << 20)(
        weight, weight_b
    )
    weight = lax.all_to_all(weight, ("zl", "core"), 0, 0, tiled=True)

    feats = lax.all_gather(jnp.stack([feats, feats_b]), "tp", axis=0)
    (joined,) = call(join_frames_kernel, [shaped(ROWS, 512)], 1, 3, 2 * ROWS * 1024 * 512, 2 << 20)(
        jnp.stack([section, count[0]]), feats, proj.reshape(8, HD, 512), text
    )

    weight, joined = lax.optimization_barrier((weight, joined))
    weight = lax.all_gather(weight, "y", axis=0)
    joined_b = swap(joined, "section")
    own_a = lax.all_gather(joined, "tp", axis=0)
    own_a, joined_b = lax.optimization_barrier((own_a, joined_b))
    other_a = swap(own_a, "core")
    own_b = gather(joined_b, "tp", TP)
    other_b = swap(own_b, "core")
    queries, kv = pl.pallas_call(
        project_kernel,
        out_shape=[shaped(Y, CHIP_ROWS, HD), shaped(CHIP_ROWS, 2 * HD)],
        in_specs=[SMEM] + [VMEM] * 4 + [pl.BlockSpec(memory_space=pltpu.HBM)] + [VMEM] * 3,
        out_specs=[VMEM, VMEM],
        scratch_shapes=[
            pltpu.VMEM((Y, ZL * CORES, ZH, 64, 3 * HD), jnp.bfloat16),
            pltpu.SemaphoreType.DMA,
        ],
        compiler_params=pltpu.CompilerParams(vmem_limit_bytes=LIMIT),
        cost_estimate=pl.CostEstimate(
            flops=2 * CHIP_ROWS * 4096 * 3 * HD, bytes_accessed=6 << 20, transcendentals=0
        ),
    )(
        jnp.bitwise_xor(zh, section).reshape(1),
        own_a,
        own_b,
        other_a,
        other_b,
        pltpu.with_memory_space_constraint(weight, pltpu.HBM),
        gains,
        cosine,
        sine,
    )

    kv_b = swap(kv, "zh")
    queries = lax.all_to_all(queries, "y", 0, 0, tiled=True)
    kv = gather(jnp.stack([kv, kv_b]), "zl", ZL)
    (parts,) = call(
        attend_kernel,
        [shaped(Y * CORES, ROWS + 8, HD)],
        1,
        2,
        4 * 1024 * 2048 * HD,
        2 << 20,
        [pltpu.VMEM((ZL * ZH, CHIP_ROWS, CHIP_ROWS), jnp.float32)],
    )(jnp.stack([zh, zl, y, core]), queries, kv)

    parts = lax.all_to_all(parts, ("y", "core"), 0, 0, tiled=True)
    (result,) = call(merge_kernel, [shaped(ROWS, 2 * HD)], 0, 1, 1 << 20, 1 << 20)(parts)
    return result


def solution(mesh):
    fine = Mesh(
        mesh.devices.reshape(ZH, ZL, Y, CORES, SECTIONS, TP),
        ("zh", "zl", "y", "core", "section", "tp"),
    )
    ctx = ("zh", "zl", "y", "core")
    in_specs = (P(ctx, F), P(ctx, F), P(ctx), P(None, F), P(), P(ctx, F), P(ctx, F), P(ctx, F))
    return jax.shard_map(
        local, mesh=fine, in_specs=in_specs, out_specs=P(ctx, F), check_vma=False
    )
```

time: 284 us -> 187 us (0.66)
  blocking collectives: 94.3 us -> 33.4 us
  waiting for transfers between devices: 93.8 us -> 54.3 us
  Pallas kernels: 0 us -> 14.4 us
  local copies, waits for them, and re-layouts: 18.1 us -> 4.62 us
  between operations: 1 us -> 14.2 us
  matrix products: 11.8 us -> 0 us
  starting transfers between devices: 55.5 us -> 63.7 us
  other arithmetic: 8.25 us -> 1.64 us
    all_to_all x4 -> x1, blocking collectives: 94.3 us -> 11.6 us  [local(): parts = lax.all_to_all(parts, ('y', 'core'), 0, 0, tiled=True)]
    all_to_all x8 -> x4, waiting for transfers between devices: 93.8 us -> 37.7 us  [the longest x2 31.1 us: gather(): lax.all_to_all(jnp.broadcast_to(v[None], (n, *v.shape)), axis, 0, 0, tile...]
    ppermute x0 -> x6, starting transfers between devices: none -> 37.3 us  [swap(): return lax.ppermute(v, axis, SWAP)]
    all_to_all x8 -> x4, starting transfers between devices: 55.5 us -> 26.4 us  [the longest x1 12.9 us: local(): weight = lax.all_to_all(weight, ('zl', 'core'), 0, 0, tiled=True)]
    all_gather x0 -> x2, blocking collectives: none -> 21.7 us  [the longest x1 11.6 us: local(): own_a = lax.all_gather(joined, 'tp', axis=0)]
    ppermute x0 -> x6, waiting for transfers between devices: none -> 15.4 us  [swap(): return lax.ppermute(v, axis, SWAP)]
    pallas_call x0 -> x6, Pallas kernels: none -> 14.4 us  [the longest x1 5.43 us: local(): call(attend_kernel, [shaped(Y * CORES, ROWS + 8, HD)], 1, 2, 4 * 1024 * 2...]
    dot_general x4 -> x0, matrix products: 11.8 us -> none  [the longest x1 5.85 us: local(): jnp.dot(weights.astype(jnp.bfloat16), kv[:, HD:], preferred_element_type=...]
  transfers between devices with their start and end apart: 8 -> 11, of which waited for: 7 -> 8; matrix products, arithmetic and copies ran while one was open for 7% -> 1% of each run, Pallas kernels for 0% -> 1%
where the time goes in v2:
time: 187 us; the launch traced here: 186 us
  starting transfers between devices  63.7 us (34%)
  waiting for transfers between devices  54.3 us (29%)
  blocking collectives  33.4 us (18%)
  Pallas kernels  14.4 us (8%)
  between operations  14.2 us (8%)
  local copies, waits for them, and re-layouts  4.62 us (2%)
    ppermute x6, starting transfers between devices, swap(): return lax.ppermute(v, axis, SWAP)  37.3 us
    all_to_all x2, waiting for transfers between devices, gather(): lax.all_to_all(jnp.broadcast_to(v[None], (n, *v.shape)), axis, 0, 0, tile...  31.1 us
    ppermute x6, waiting for transfers between devices, swap(): return lax.ppermute(v, axis, SWAP)  15.4 us
    all_to_all x1, starting transfers between devices, local(): weight = lax.all_to_all(weight, ('zl', 'core'), 0, 0, tiled=True)  12.9 us
    all_to_all x1, blocking collectives, local(): parts = lax.all_to_all(parts, ('y', 'core'), 0, 0, tiled=True)  11.6 us
    all_gather x1, blocking collectives, local(): own_a = lax.all_gather(joined, 'tp', axis=0)  11.6 us
    all_gather x1, blocking collectives, local(): feats = lax.all_gather(jnp.stack([feats, feats_b]), 'tp', axis=0)  10.1 us
    all_to_all x2, starting transfers between devices, gather(): lax.all_to_all(jnp.broadcast_to(v[None], (n, *v.shape)), axis, 0, 0, tile...  10.1 us
  transfers between devices with their start and end apart: 11, of which 8 were waited for; matrix products, arithmetic and copies ran while one was open for 1% of the time, Pallas kernels for 1%

profile of v2, /device:TPU:1, one launch (start us, length us, event | category | flops | bytes accessed | tf_op | source)
XLA Modules:
  0.0 186.2 jit_solution(10136511295040103862)
XLA Ops:
  6.5 1.5 shard_map.82.own
  8.1 9.6 %collective-permute-start = (bf16[64,768]{1,0:T(8,128)(2,1)}, bf16[64,768]{1,0:T(8,128)(2,1)S(1)}, u32[]{:S(2)}, u32[]{:S(2)}) collective-permute-start(bf16[64,768]{1,0:T(8,128)(2,1)} %shard_map.82.own), channel_id=1, source_target_pairs={{0,256},{256,0},{1,257},{257,1},{2,258},{258,2},{3,259},{259,3},{4... | collective-permute-start | bytes 294920 | tf_op jit(solution)/shard_map/ppermute | solution.py:26
  17.7 10.6 %collective-permute-start.1 = (bf16[128,128]{1,0:T(8,128)(2,1)}, bf16[128,128]{1,0:T(8,128)(2,1)S(1)}, u32[]{:S(2)}, u32[]{:S(2)}) collective-permute-start(bf16[128,128]{1,0:T(8,128)(2,1)} %param.9), channel_id=1, source_target_pairs={{0,4},{4,0},{1,5},{5,1},{2,6},{6,2},{3,7},{7,3},{8,12},{12,8},{9,1... | collective-permute-start | bytes 98312 | tf_op jit(solution)/shard_map/ppermute | solution.py:26
  28.4 3.2 %collective-permute-done.1 = bf16[128,128]{1,0:T(8,128)(2,1)S(1)} collective-permute-done((bf16[128,128]{1,0:T(8,128)(2,1)}, bf16[128,128]{1,0:T(8,128)(2,1)S(1)}, u32[]{:S(2)}, u32[]{:S(2)}) %collective-permute-start.1) | collective-permute-done | bytes 32800 | tf_op jit(solution)/shard_map/ppermute | solution.py:26
  33.5 12.9 %all-to-all-start = ((bf16[8,2,64,384]{3,2,1,0:T(8,128)(2,1)}), bf16[8,2,64,384]{3,2,1,0:T(8,128)(2,1)S(1)}, u32[]{:S(2)}, u32[]{:S(2)}) async-start(bf16[8,2,64,384]{3,2,1,0:T(8,128)(2,1)} %shard_map.83), calls=%async_computation | async-start | bytes 1572864 | tf_op jit(solution)/shard_map/all_to_all | solution.py:230
  47.9 10.1 %all-gather = bf16[8,128,128]{2,1,0:T(8,128)(2,1)S(1)} all-gather(bf16[2,128,128]{2,1,0:T(8,128)(2,1)S(1)} %pad_maximum_fusion.3), channel_id=2, replica_groups=mesh['zh'=2,'zl'=4,'y'=4,'core'=2,'section'=2,'tp'=4] {'tp'}, dimensions={0}, use_global_device_ids=true | all-gather | bytes 327680 | tf_op jit(solution)/shard_map/all_gather | solution.py:232
  59.9 6.6 %all-to-all-done = bf16[8,2,64,384]{3,2,1,0:T(8,128)(2,1)S(1)} async-done(((bf16[8,2,64,384]{3,2,1,0:T(8,128)(2,1)}), bf16[8,2,64,384]{3,2,1,0:T(8,128)(2,1)S(1)}, u32[]{:S(2)}, u32[]{:S(2)}) %all-to-all-start) | async-done | bytes 786464 | tf_op jit(solution)/shard_map/all_to_all | solution.py:230
  67.4 3.2 %collective-permute-start.2 = (bf16[128,512]{1,0:T(8,128)(2,1)S(1)}, bf16[128,512]{1,0:T(8,128)(2,1)S(1)}, u32[]{:S(2)}, u32[]{:S(2)}) collective-permute-start(bf16[128,512]{1,0:T(8,128)(2,1)S(1)} %shard_map.84), channel_id=1, source_target_pairs={{0,4},{4,0},{1,5},{5,1},{2,6},{6,2},{3,7},{7,3},{8,12},{12,8},{9,1... | collective-permute-start | bytes 393224 | tf_op jit(solution)/shard_map/ppermute | solution.py:26
  70.6 11.6 %all-gather.1 = bf16[512,512]{1,0:T(8,128)(2,1)S(1)} all-gather(bf16[128,512]{1,0:T(8,128)(2,1)S(1)} %shard_map.84), channel_id=3, replica_groups=mesh['zh'=2,'zl'=4,'y'=4,'core'=2,'section'=2,'tp'=4] {'tp'}, dimensions={0}, use_global_device_ids=true | all-gather | bytes 655360 | tf_op jit(solution)/shard_map/all_gather | solution.py:240
  82.2 3.4 %collective-permute-done.2 = bf16[128,512]{1,0:T(8,128)(2,1)S(1)} collective-permute-done((bf16[128,512]{1,0:T(8,128)(2,1)S(1)}, bf16[128,512]{1,0:T(8,128)(2,1)S(1)}, u32[]{:S(2)}, u32[]{:S(2)}) %collective-permute-start.2) | collective-permute-done | bytes 131104 | tf_op jit(solution)/shard_map/ppermute | solution.py:26
  86.4 5.6 %all-to-all-start.1 = ((bf16[4,128,512]{2,1,0:T(8,128)(2,1)}), bf16[4,128,512]{2,1,0:T(8,128)(2,1)S(1)}, u32[]{:S(2)}, u32[]{:S(2)}) async-start(bf16[4,128,512]{2,1,0:T(8,128)(2,1)} %broadcast_in_dim.4), calls=%async_computation.1 | async-start | bytes 1048576 | tf_op jit(solution)/shard_map/all_to_all | solution.py:30
  92.1 2.8 %collective-permute-start.3 = (bf16[4,128,512]{2,1,0:T(8,128)(2,1)S(1)}, bf16[4,128,512]{2,1,0:T(8,128)(2,1)S(1)}, u32[]{:S(2)}, u32[]{:S(2)}) collective-permute-start(bf16[4,128,512]{2,1,0:T(8,128)(2,1)S(1)} %bitcast.14), channel_id=1, source_target_pairs={{0,8},{8,0},{1,9},{9,1},{2,10},{10,2},{3,11},{11,3},{4,12},{12,4},... | collective-permute-start | bytes 1572872 | tf_op jit(solution)/shard_map/ppermute | solution.py:26
  94.9 5.9 %all-to-all-done.1.own_b = bf16[4,128,512]{2,1,0:T(8,128)(2,1)S(1)} async-done(((bf16[4,128,512]{2,1,0:T(8,128)(2,1)}), bf16[4,128,512]{2,1,0:T(8,128)(2,1)S(1)}, u32[]{:S(2)}, u32[]{:S(2)}) %all-to-all-start.1) | async-done | bytes 524320 | tf_op jit(solution)/shard_map/all_to_all | solution.py:30
  100.8 3.6 %collective-permute-start.4 = (bf16[4,128,512]{2,1,0:T(8,128)(2,1)S(1)}, bf16[4,128,512]{2,1,0:T(8,128)(2,1)S(1)}, u32[]{:S(2)}, u32[]{:S(2)}) collective-permute-start(bf16[4,128,512]{2,1,0:T(8,128)(2,1)S(1)} %all-to-all-done.1.own_b), channel_id=1, source_target_pairs={{0,8},{8,0},{1,9},{9,1},{2,10},{10,2},{3,11},{11,3},{4,12},{12,4},... | collective-permute-start | bytes 1572872 | tf_op jit(solution)/shard_map/ppermute | solution.py:26
  105.9 1.3 all-gather.5.cloned.1.call-done
  107.2 4.1 %shard_map.85 = (bf16[4,256,128]{2,1,0:T(8,128)(2,1)}, bf16[256,256]{1,0:T(8,128)(2,1)S(1)}) custom-call(s32[1]{0:T(128)} %bitcast.4.flip, bf16[4,128,512]{2,1,0:T(8,128)(2,1)S(1)} %bitcast.15, bf16[4,128,512]{2,1,0:T(8,128)(2,1)S(1)} %all-to-all-done.1.own_b, bf16[4,128,512]{2,1,0:T(8,128)(2,1)S(1)} %collective-permute-done.3.other_a, ...), custom_call_target="tpu_custom_call" | custom-call | flops 805306368 | bytes 6291456 | tf_op jit(solution)/shard_map/pallas_call | solution.py:245
  111.3 7.4 %collective-permute-start.5 = (bf16[256,256]{1,0:T(8,128)(2,1)S(1)}, bf16[256,256]{1,0:T(8,128)(2,1)S(1)}, u32[]{:S(2)}, u32[]{:S(2)}) collective-permute-start(bf16[256,256]{1,0:T(8,128)(2,1)S(1)} %get-tuple-element.20), channel_id=1, source_target_pairs={{0,256},{256,0},{1,257},{257,1},{2,258},{258,2},{3,259},{259,3},{4... | collective-permute-start | bytes 393224 | tf_op jit(solution)/shard_map/ppermute | solution.py:26
  118.7 3.4 %all-to-all-start.2 = ((bf16[4,256,128]{2,1,0:T(8,128)(2,1)}), bf16[4,256,128]{2,1,0:T(8,128)(2,1)S(1)}, u32[]{:S(2)}, u32[]{:S(2)}) async-start(bf16[4,256,128]{2,1,0:T(8,128)(2,1)} %get-tuple-element.19), calls=%async_computation.2 | async-start | bytes 524288 | tf_op jit(solution)/shard_map/all_to_all | solution.py:271
  122.1 8.0 %collective-permute-done.5 = bf16[256,256]{1,0:T(8,128)(2,1)S(1)} collective-permute-done((bf16[256,256]{1,0:T(8,128)(2,1)S(1)}, bf16[256,256]{1,0:T(8,128)(2,1)S(1)}, u32[]{:S(2)}, u32[]{:S(2)}) %collective-permute-start.5) | collective-permute-done | bytes 131104 | tf_op jit(solution)/shard_map/ppermute | solution.py:26
  131.2 4.5 %all-to-all-start.3 = ((bf16[4,2,256,256]{3,2,1,0:T(8,128)(2,1)}), bf16[4,2,256,256]{3,2,1,0:T(8,128)(2,1)S(1)}, u32[]{:S(2)}, u32[]{:S(2)}) async-start(bf16[4,2,256,256]{3,2,1,0:T(8,128)(2,1)} %broadcast_in_dim.5), calls=%async_computation.3 | async-start | bytes 2097152 | tf_op jit(solution)/shard_map/all_to_all | solution.py:30
  135.7 25.2 %all-to-all-done.3.kv = bf16[4,2,256,256]{3,2,1,0:T(8,128)(2,1)S(1)} async-done(((bf16[4,2,256,256]{3,2,1,0:T(8,128)(2,1)}), bf16[4,2,256,256]{3,2,1,0:T(8,128)(2,1)S(1)}, u32[]{:S(2)}, u32[]{:S(2)}) %all-to-all-start.3) | async-done | bytes 1048608 | tf_op jit(solution)/shard_map/all_to_all | solution.py:30
  160.9 5.4 %shard_map.86 = bf16[8,136,128]{2,1,0:T(8,128)(2,1)S(1)} custom-call(s32[4]{0:T(128)S(1)} %pad_add_fusion.place, bf16[4,256,128]{2,1,0:T(8,128)(2,1)S(1)} %all-to-all-done.2.queries, bf16[4,2,256,256]{3,2,1,0:T(8,128)(2,1)S(1)} %all-to-all-done.3.kv), custom_call_target="tpu_custom_call" | custom-call | flops 1073741824 | bytes 2097152 | tf_op jit(solution)/shard_map/pallas_call | solution.py:273
  166.3 11.6 %all_to_all.25.parts = bf16[8,136,128]{2,1,0:T(8,128)(2,1)S(1)} all-to-all(bf16[8,136,128]{2,1,0:T(8,128)(2,1)S(1)} %shard_map.86), channel_id=1, replica_groups=mesh['zh'=2,'zl'=4,'y'=4,'core'=2,'section'=2,'tp'=4] {'y','core'}, dimensions={0} | all-to-all | bytes 557056 | tf_op jit(solution)/shard_map/all_to_all | solution.py:283
  178.0 1.4 shard_map.87
  (31 shorter events, 9.0 us)
Async XLA Ops:
  6.5 51.5 %copy-start = (bf16[1024,512]{1,0:T(8,128)(2,1)S(1)}, bf16[1024,512]{1,0:T(8,128)(2,1)}, u32[]{:S(2)}) copy-start(bf16[1024,512]{1,0:T(8,128)(2,1)} %param.11) | copy-start | bytes 3145732
  8.1 23.5 %collective-permute-start = (bf16[64,768]{1,0:T(8,128)(2,1)}, bf16[64,768]{1,0:T(8,128)(2,1)S(1)}, u32[]{:S(2)}, u32[]{:S(2)}) collective-permute-start(bf16[64,768]{1,0:T(8,128)(2,1)} %shard_map.82.own), channel_id=1, source_target_pairs={{0,256},{256,0},{1,257},{257,1},{2,258},{258,2},{3,259},{259,3},{4... | collective-permute-start | bytes 294920 | tf_op jit(solution)/shard_map/ppermute | solution.py:26
  17.7 13.8 %collective-permute-start.1 = (bf16[128,128]{1,0:T(8,128)(2,1)}, bf16[128,128]{1,0:T(8,128)(2,1)S(1)}, u32[]{:S(2)}, u32[]{:S(2)}) collective-permute-start(bf16[128,128]{1,0:T(8,128)(2,1)} %param.9), channel_id=1, source_target_pairs={{0,4},{4,0},{1,5},{5,1},{2,6},{6,2},{3,7},{7,3},{8,12},{12,8},{9,1... | collective-permute-start | bytes 98312 | tf_op jit(solution)/shard_map/ppermute | solution.py:26
  31.6 0.9 copy-start.1
  33.5 58.6 %copy-start.4 = (bf16[4096]{0:T(1024)(128)(2,1)S(1)}, bf16[4096]{0:T(1024)(128)(2,1)}, u32[]{:S(2)}) copy-start(bf16[4096]{0:T(1024)(128)(2,1)} %param.12) | copy-start | bytes 24580
  33.5 33.0 %all-to-all-start = ((bf16[8,2,64,384]{3,2,1,0:T(8,128)(2,1)}), bf16[8,2,64,384]{3,2,1,0:T(8,128)(2,1)S(1)}, u32[]{:S(2)}, u32[]{:S(2)}) async-start(bf16[8,2,64,384]{3,2,1,0:T(8,128)(2,1)} %shard_map.83), calls=%async_computation | async-start | bytes 1572864 | tf_op jit(solution)/shard_map/all_to_all | solution.py:230
  46.4 60.8 %all-gather.5.cloned.1.call-start = ((), (), s32[]{:S(2)}) async-start(), calls=%async_computation.5 | async-start | bytes 3932160 | tf_op jit(solution)/shard_map/all_gather | solution.py:238
  58.0 0.9 copy-start.2
  66.5 0.9 copy-start.3
  67.4 18.2 %collective-permute-start.2 = (bf16[128,512]{1,0:T(8,128)(2,1)S(1)}, bf16[128,512]{1,0:T(8,128)(2,1)S(1)}, u32[]{:S(2)}, u32[]{:S(2)}) collective-permute-start(bf16[128,512]{1,0:T(8,128)(2,1)S(1)} %shard_map.84), channel_id=1, source_target_pairs={{0,4},{4,0},{1,5},{5,1},{2,6},{6,2},{3,7},{7,3},{8,12},{12,8},{9,1... | collective-permute-start | bytes 393224 | tf_op jit(solution)/shard_map/ppermute | solution.py:26
  86.4 14.3 %all-to-all-start.1 = ((bf16[4,128,512]{2,1,0:T(8,128)(2,1)}), bf16[4,128,512]{2,1,0:T(8,128)(2,1)S(1)}, u32[]{:S(2)}, u32[]{:S(2)}) async-start(bf16[4,128,512]{2,1,0:T(8,128)(2,1)} %broadcast_in_dim.4), calls=%async_computation.1 | async-start | bytes 1048576 | tf_op jit(solution)/shard_map/all_to_all | solution.py:30
  92.1 13.0 %collective-permute-start.3 = (bf16[4,128,512]{2,1,0:T(8,128)(2,1)S(1)}, bf16[4,128,512]{2,1,0:T(8,128)(2,1)S(1)}, u32[]{:S(2)}, u32[]{:S(2)}) collective-permute-start(bf16[4,128,512]{2,1,0:T(8,128)(2,1)S(1)} %bitcast.14), channel_id=1, source_target_pairs={{0,8},{8,0},{1,9},{9,1},{2,10},{10,2},{3,11},{11,3},{4,12},{12,4},... | collective-permute-start | bytes 1572872 | tf_op jit(solution)/shard_map/ppermute | solution.py:26
  100.8 5.2 %collective-permute-start.4 = (bf16[4,128,512]{2,1,0:T(8,128)(2,1)S(1)}, bf16[4,128,512]{2,1,0:T(8,128)(2,1)S(1)}, u32[]{:S(2)}, u32[]{:S(2)}) collective-permute-start(bf16[4,128,512]{2,1,0:T(8,128)(2,1)S(1)} %all-to-all-done.1.own_b), channel_id=1, source_target_pairs={{0,8},{8,0},{1,9},{9,1},{2,10},{10,2},{3,11},{11,3},{4,12},{12,4},... | collective-permute-start | bytes 1572872 | tf_op jit(solution)/shard_map/ppermute | solution.py:26
  111.3 18.8 %collective-permute-start.5 = (bf16[256,256]{1,0:T(8,128)(2,1)S(1)}, bf16[256,256]{1,0:T(8,128)(2,1)S(1)}, u32[]{:S(2)}, u32[]{:S(2)}) collective-permute-start(bf16[256,256]{1,0:T(8,128)(2,1)S(1)} %get-tuple-element.20), channel_id=1, source_target_pairs={{0,256},{256,0},{1,257},{257,1},{2,258},{258,2},{3,259},{259,3},{4... | collective-permute-start | bytes 393224 | tf_op jit(solution)/shard_map/ppermute | solution.py:26
  118.7 11.5 %all-to-all-start.2 = ((bf16[4,256,128]{2,1,0:T(8,128)(2,1)}), bf16[4,256,128]{2,1,0:T(8,128)(2,1)S(1)}, u32[]{:S(2)}, u32[]{:S(2)}) async-start(bf16[4,256,128]{2,1,0:T(8,128)(2,1)} %get-tuple-element.19), calls=%async_computation.2 | async-start | bytes 524288 | tf_op jit(solution)/shard_map/all_to_all | solution.py:271
  131.2 29.7 %all-to-all-start.3 = ((bf16[4,2,256,256]{3,2,1,0:T(8,128)(2,1)}), bf16[4,2,256,256]{3,2,1,0:T(8,128)(2,1)S(1)}, u32[]{:S(2)}, u32[]{:S(2)}) async-start(bf16[4,2,256,256]{3,2,1,0:T(8,128)(2,1)} %broadcast_in_dim.5), calls=%async_computation.3 | async-start | bytes 2097152 | tf_op jit(solution)/shard_map/all_to_all | solution.py:30
Sparse Core Ops, SparseCore 0:
  67.5 39.6 all-gather.4

commit v3 on v2

--- a/solution.py
+++ b/solution.py
@@ -44,10 +44,16 @@
 
 
 def project_kernel(
-    flip, own_a, own_b, other_a, other_b, stored, gain, cosine, sine, q_out, kv_out, weight, sem
+    flip, own_a, own_b, other_a, other_b, stored, gain, cosine, sine, q_out, kv_out, lines_out, weight, sem
 ):
-    copy = pltpu.make_async_copy(stored, weight, sem)
-    copy.start()
+    copies = [
+        pltpu.make_async_copy(
+            stored.at[:, t * CORES : (t + 1) * CORES], weight.at[:, t * CORES : (t + 1) * CORES], sem.at[t]
+        )
+        for t in range(TP)
+    ]
+    for copy in copies:
+        copy.start()
     tiles = [(own, other, t) for own, other in ((own_a, other_a), (own_b, other_b)) for t in range(TP)]
     squares = jnp.zeros((CHIP_ROWS, 512), jnp.float32)
     for own, other, t in tiles:
@@ -56,8 +62,9 @@
     mean_square = jnp.sum(squares, axis=-1, keepdims=True) * (1.0 / 4096)
     inverse = lax.rsqrt(mean_square + NORM_EPS)
     total = jnp.zeros((CHIP_ROWS, 3 * HD), jnp.float32)
-    copy.wait()
     for i, (own, other, t) in enumerate(tiles):
+        if i < TP:
+            copies[i].wait()
         half = jnp.bitwise_xor(flip[0], i // TP)
         wide = jnp.concatenate([own[t], other[t]], axis=0).astype(jnp.float32)
         normed = (wide * inverse * gain[i : i + 1, :]).astype(jnp.bfloat16)
@@ -68,11 +75,14 @@
     q = total[:, :HD]
     k = total[:, HD : 2 * HD]
     cos, sin = cosine[...], sine[...]
-    q = (q * cos + pltpu.roll(q, HD // 2, 1) * sin).astype(jnp.bfloat16)
-    for i in range(Y):
-        q_out[i] = q
-    kv_out[:, :HD] = (k * cos + pltpu.roll(k, HD // 2, 1) * sin).astype(jnp.bfloat16)
-    kv_out[:, HD:] = total[:, 2 * HD :].astype(jnp.bfloat16)
+    q_out[...] = (q * cos + pltpu.roll(q, HD // 2, 1) * sin).astype(jnp.bfloat16)
+    k = (k * cos + pltpu.roll(k, HD // 2, 1) * sin).astype(jnp.bfloat16)
+    v = total[:, 2 * HD :].astype(jnp.bfloat16)
+    kv_out[:, :HD] = k
+    kv_out[:, HD:] = v
+    for i in range(ZL):
+        lines_out[i, :, :HD] = k
+        lines_out[i, :, HD:] = v
 
 
 def encode(level):
@@ -100,52 +110,81 @@
     return c[:, 0:1] + c[:, 1:2] + c[:, 2:3]
 
 
-def attend_kernel(place, queries, kv, out, scores):
-    zh, zl, me, core = place[0], place[1], place[2], place[3]
+def attend(q, kv, scores, mask):
+    shape = (CHIP_ROWS, CHIP_ROWS)
+    scale = 1.0 / math.sqrt(HD)
+    peak = jnp.full(shape, MASKED, jnp.float32)
+    for l in range(ZL):
+        s = lax.dot_general(
+            q, kv[l, :, :HD], (((1,), (1,)), ((), ())), preferred_element_type=jnp.float32
+        )
+        s = mask(l, s * scale)
+        scores[l] = s
+        peak = jnp.maximum(peak, s)
+    best = jnp.max(peak, axis=-1, keepdims=True)
+    mass = jnp.zeros(shape, jnp.float32)
+    part = jnp.zeros((CHIP_ROWS, HD), jnp.float32)
+    for l in range(ZL):
+        w = jnp.exp(scores[l] - best)
+        mass = mass + w
+        part = part + jnp.dot(
+            w.astype(jnp.bfloat16), kv[l, :, HD:], preferred_element_type=jnp.float32
+        )
+    total = jnp.sum(mass, axis=-1, keepdims=True)
+    return part / total, jnp.where(best > 0.5 * MASKED, best + jnp.log(total), MASKED)
+
+
+def attend_own_kernel(place, queries, kv, parts, levels, scores):
+    zl, me, core = place[1], place[2], place[3]
     shape = (CHIP_ROWS, CHIP_ROWS)
     turn = core * ROWS
     row = jnp.bitwise_xor(lax.broadcasted_iota(jnp.int32, shape, 0), turn)
     col = jnp.bitwise_xor(lax.broadcasted_iota(jnp.int32, shape, 1), turn)
     ahead = col - row
-    scale = 1.0 / math.sqrt(HD)
-
-    def one(y, carry):
-        q = queries[y]
-        first_q = (zh * ZL + zl) * (Y * CHIP_ROWS) + y * CHIP_ROWS
-        peak = jnp.full(shape, MASKED, jnp.float32)
-        for l in range(ZL):
-            for h in range(ZH):
-                first_k = (jnp.bitwise_xor(zh, h) * ZL + l) * (Y * CHIP_ROWS) + me * CHIP_ROWS
-                s = lax.dot_general(
-                    q,
-                    kv[l, h, :, :HD],
-                    (((1,), (1,)), ((), ())),
-                    preferred_element_type=jnp.float32,
-                )
-                s = jnp.where(ahead <= first_q - first_k, s * scale, MASKED)
-                scores[l * ZH + h] = s
-                peak = jnp.maximum(peak, s)
-        best = jnp.max(peak, axis=-1, keepdims=True)
-        mass = jnp.zeros(shape, jnp.float32)
-        part = jnp.zeros((CHIP_ROWS, HD), jnp.float32)
-        for l in range(ZL):
-            for h in range(ZH):
-                w = jnp.exp(scores[l * ZH + h] - best)
-                mass = mass + w
-                part = part + jnp.dot(
-                    w.astype(jnp.bfloat16), kv[l, h, :, HD:], preferred_element_type=jnp.float32
-                )
-        total = jnp.sum(mass, axis=-1, keepdims=True)
-        level = jnp.where(best > 0.5 * MASKED, best + jnp.log(total), MASKED)
+
+    def one(pair, carry):
+        for i in range(2):
+            y = pair * 2 + i
+
+            def mask(l, s):
+                return jnp.where(ahead <= ((zl - l) * Y + y - me) * CHIP_ROWS, s, MASKED)
+
+            part, level = attend(queries[y], kv, scores.at[i], mask)
+            parts[y] = part
+            levels[y] = jnp.broadcast_to(level, (CHIP_ROWS, HD))
+        return carry
+
+    lax.fori_loop(0, Y // 2, one, 0)
+
+
+def attend_rest_kernel(place, queries, kv, parts, levels, out, scores):
+    def put(y, part, level):
         coded = encode(level)
-        part = (part / total).astype(jnp.bfloat16)
+        part = part.astype(jnp.bfloat16)
         for i in range(CORES):
-            owner = y * CORES + jnp.bitwise_xor(core, i)
+            owner = y * CORES + jnp.bitwise_xor(place[3], i)
             out[owner, :ROWS, :] = part[i * ROWS : (i + 1) * ROWS]
             out[owner, ROWS:, :] = coded[i * 8 : (i + 1) * 8]
-        return carry
-
-    lax.fori_loop(0, Y, one, 0)
+
+    @pl.when(place[0] == 0)
+    def _():
+        for y in range(Y):
+            put(y, parts[y], levels[y, :, 0:1])
+
+    @pl.when(place[0] != 0)
+    def _():
+        def one(pair, carry):
+            for i in range(2):
+                y = pair * 2 + i
+                part, level = attend(queries[y], kv, scores.at[i], lambda l, s: s)
+                before = levels[y, :, 0:1]
+                top = jnp.maximum(level, before)
+                new, old = jnp.exp(level - top), jnp.exp(before - top)
+                total = new + old
+                put(y, (part * new + parts[y] * old) / total, top + jnp.log(total))
+            return carry
+
+        lax.fori_loop(0, Y // 2, one, 0)
 
 
 def merge_kernel(parts, out):
@@ -242,14 +281,18 @@
     other_a = swap(own_a, "core")
     own_b = gather(joined_b, "tp", TP)
     other_b = swap(own_b, "core")
-    queries, kv = pl.pallas_call(
+    queries, kv, lines = pl.pallas_call(
         project_kernel,
-        out_shape=[shaped(Y, CHIP_ROWS, HD), shaped(CHIP_ROWS, 2 * HD)],
+        out_shape=[
+            shaped(CHIP_ROWS, HD),
+            shaped(CHIP_ROWS, 2 * HD),
+            shaped(ZL, CHIP_ROWS, 2 * HD),
+        ],
         in_specs=[SMEM] + [VMEM] * 4 + [pl.BlockSpec(memory_space=pltpu.HBM)] + [VMEM] * 3,
-        out_specs=[VMEM, VMEM],
+        out_specs=[VMEM] * 3,
         scratch_shapes=[
             pltpu.VMEM((Y, ZL * CORES, ZH, 64, 3 * HD), jnp.bfloat16),
-            pltpu.SemaphoreType.DMA,
+            pltpu.SemaphoreType.DMA((TP,)),
         ],
         compiler_params=pltpu.CompilerParams(vmem_limit_bytes=LIMIT),
         cost_estimate=pl.CostEstimate(
@@ -268,17 +311,20 @@
     )
 
     kv_b = swap(kv, "zh")
-    queries = lax.all_to_all(queries, "y", 0, 0, tiled=True)
-    kv = gather(jnp.stack([kv, kv_b]), "zl", ZL)
+    kv_a = lax.all_to_all(lines, "zl", 0, 0, tiled=True)
+    queries = lax.all_gather(queries, "y", axis=0)
+    kv_a, kv_b, queries = lax.optimization_barrier((kv_a, kv_b, queries))
+    place = jnp.stack([zh, zl, y, core])
+    scores = [pltpu.VMEM((2, ZL, CHIP_ROWS, CHIP_ROWS), jnp.float32)]
+    state = [jax.ShapeDtypeStruct((Y, CHIP_ROWS, HD), jnp.float32)] * 2
+    flops = 4 * 1024 * 1024 * HD
+    parts, levels = call(attend_own_kernel, state, 1, 2, flops, 2 << 20, scores)(
+        place, queries, kv_a
+    )
+    kv_b = gather(kv_b, "zl", ZL)
     (parts,) = call(
-        attend_kernel,
-        [shaped(Y * CORES, ROWS + 8, HD)],
-        1,
-        2,
-        4 * 1024 * 2048 * HD,
-        2 << 20,
-        [pltpu.VMEM((ZL * ZH, CHIP_ROWS, CHIP_ROWS), jnp.float32)],
-    )(jnp.stack([zh, zl, y, core]), queries, kv)
+        attend_rest_kernel, [shaped(Y * CORES, ROWS + 8, HD)], 1, 4, flops, 2 << 20, scores
+    )(place, queries, kv_b, parts, levels)
 
     parts = lax.all_to_all(parts, ("y", "core"), 0, 0, tiled=True)
     (result,) = call(merge_kernel, [shaped(ROWS, 2 * HD)], 0, 1, 1 << 20, 1 << 20)(parts)

time: 187 us -> 178 us (0.952)
  waiting for transfers between devices: 54.3 us -> 34.7 us
  blocking collectives: 33.4 us -> 43.1 us
  starting transfers between devices: 63.7 us -> 67.1 us
    all_to_all x2, waiting for transfers between devices: 31.1 us -> 16.8 us  [gather(): lax.all_to_all(jnp.broadcast_to(v[None], (n, *v.shape)), axis, 0, 0, tile...]
    all_gather x0 -> x1, blocking collectives: none -> 9.67 us  [local(): queries = lax.all_gather(queries, 'y', axis=0)]
    ppermute x6, waiting for transfers between devices: 15.4 us -> 7.39 us  [swap(): return lax.ppermute(v, axis, SWAP)]
    all_to_all x1, waiting for transfers between devices: 0.01 us -> 2.58 us  [local(): kv_a = lax.all_to_all(lines, 'zl', 0, 0, tiled=True)]
    all_to_all x2, starting transfers between devices: 10.1 us -> 12.4 us  [gather(): lax.all_to_all(jnp.broadcast_to(v[None], (n, *v.shape)), axis, 0, 0, tile...]
    pallas_call x2 -> x3, Pallas kernels: 9.51 us -> 7.86 us  [the longest x1 3.94 us: local(): pl.pallas_call(project_kernel, out_shape=[shaped(CHIP_ROWS, HD), shaped(C...]
  transfers between devices with their start and end apart: 11 -> 11, of which waited for: 8 -> 8; matrix products, arithmetic and copies ran while one was open for 1% -> 1% of each run, Pallas kernels for 1% -> 2%
where the time goes in v3:
time: 178 us
  starting transfers between devices  67.1 us (38%)
  blocking collectives  43.1 us (24%)
  waiting for transfers between devices  34.7 us (19%)
  between operations  14.2 us (8%)
  Pallas kernels  12.7 us (7%)
  local copies, waits for them, and re-layouts  4.41 us (2%)
    ppermute x6, starting transfers between devices, swap(): return lax.ppermute(v, axis, SWAP)  37.3 us
    all_to_all x2, waiting for transfers between devices, gather(): lax.all_to_all(jnp.broadcast_to(v[None], (n, *v.shape)), axis, 0, 0, tile...  16.8 us
    all_to_all x1, starting transfers between devices, local(): weight = lax.all_to_all(weight, ('zl', 'core'), 0, 0, tiled=True)  12.9 us
    all_to_all x2, starting transfers between devices, gather(): lax.all_to_all(jnp.broadcast_to(v[None], (n, *v.shape)), axis, 0, 0, tile...  12.4 us
    all_to_all x1, blocking collectives, local(): parts = lax.all_to_all(parts, ('y', 'core'), 0, 0, tiled=True)  11.7 us
    all_gather x1, blocking collectives, local(): own_a = lax.all_gather(joined, 'tp', axis=0)  11.6 us
    all_gather x1, blocking collectives, local(): feats = lax.all_gather(jnp.stack([feats, feats_b]), 'tp', axis=0)  10.1 us
    all_gather x1, blocking collectives, local(): queries = lax.all_gather(queries, 'y', axis=0)  9.67 us
  transfers between devices with their start and end apart: 11, of which 8 were waited for; matrix products, arithmetic and copies ran while one was open for 1% of the time, Pallas kernels for 2%

profile of v3, /device:TPU:1, one launch (start us, length us, event | category | flops | bytes accessed | tf_op | source)
XLA Modules:
  0.0 177.7 jit_solution(14103601818999975414)
XLA Ops:
  6.5 1.5 shard_map.82.own
  8.1 9.6 %collective-permute-start = (bf16[64,768]{1,0:T(8,128)(2,1)}, bf16[64,768]{1,0:T(8,128)(2,1)S(1)}, u32[]{:S(2)}, u32[]{:S(2)}) collective-permute-start(bf16[64,768]{1,0:T(8,128)(2,1)} %shard_map.82.own), channel_id=1, source_target_pairs={{0,256},{256,0},{1,257},{257,1},{2,258},{258,2},{3,259},{259,3},{4... | collective-permute-start | bytes 294920 | tf_op jit(solution)/shard_map/ppermute | solution.py:26
  17.7 10.6 %collective-permute-start.1 = (bf16[128,128]{1,0:T(8,128)(2,1)}, bf16[128,128]{1,0:T(8,128)(2,1)S(1)}, u32[]{:S(2)}, u32[]{:S(2)}) collective-permute-start(bf16[128,128]{1,0:T(8,128)(2,1)} %param.9), channel_id=1, source_target_pairs={{0,4},{4,0},{1,5},{5,1},{2,6},{6,2},{3,7},{7,3},{8,12},{12,8},{9,1... | collective-permute-start | bytes 98312 | tf_op jit(solution)/shard_map/ppermute | solution.py:26
  28.4 3.2 %collective-permute-done.1 = bf16[128,128]{1,0:T(8,128)(2,1)S(1)} collective-permute-done((bf16[128,128]{1,0:T(8,128)(2,1)}, bf16[128,128]{1,0:T(8,128)(2,1)S(1)}, u32[]{:S(2)}, u32[]{:S(2)}) %collective-permute-start.1) | collective-permute-done | bytes 32800 | tf_op jit(solution)/shard_map/ppermute | solution.py:26
  33.5 12.9 %all-to-all-start = ((bf16[8,2,64,384]{3,2,1,0:T(8,128)(2,1)}), bf16[8,2,64,384]{3,2,1,0:T(8,128)(2,1)S(1)}, u32[]{:S(2)}, u32[]{:S(2)}) async-start(bf16[8,2,64,384]{3,2,1,0:T(8,128)(2,1)} %shard_map.83), calls=%async_computation | async-start | bytes 1572864 | tf_op jit(solution)/shard_map/all_to_all | solution.py:269
  47.9 10.1 %all-gather = bf16[8,128,128]{2,1,0:T(8,128)(2,1)S(1)} all-gather(bf16[2,128,128]{2,1,0:T(8,128)(2,1)S(1)} %pad_maximum_fusion.2), channel_id=2, replica_groups=mesh['zh'=2,'zl'=4,'y'=4,'core'=2,'section'=2,'tp'=4] {'tp'}, dimensions={0}, use_global_device_ids=true | all-gather | bytes 327680 | tf_op jit(solution)/shard_map/all_gather | solution.py:271
  59.9 6.6 %all-to-all-done = bf16[8,2,64,384]{3,2,1,0:T(8,128)(2,1)S(1)} async-done(((bf16[8,2,64,384]{3,2,1,0:T(8,128)(2,1)}), bf16[8,2,64,384]{3,2,1,0:T(8,128)(2,1)S(1)}, u32[]{:S(2)}, u32[]{:S(2)}) %all-to-all-start) | async-done | bytes 786464 | tf_op jit(solution)/shard_map/all_to_all | solution.py:269
  67.4 3.2 %collective-permute-start.2 = (bf16[128,512]{1,0:T(8,128)(2,1)S(1)}, bf16[128,512]{1,0:T(8,128)(2,1)S(1)}, u32[]{:S(2)}, u32[]{:S(2)}) collective-permute-start(bf16[128,512]{1,0:T(8,128)(2,1)S(1)} %shard_map.84), channel_id=1, source_target_pairs={{0,4},{4,0},{1,5},{5,1},{2,6},{6,2},{3,7},{7,3},{8,12},{12,8},{9,1... | collective-permute-start | bytes 393224 | tf_op jit(solution)/shard_map/ppermute | solution.py:26
  70.6 11.6 %all-gather.1 = bf16[512,512]{1,0:T(8,128)(2,1)S(1)} all-gather(bf16[128,512]{1,0:T(8,128)(2,1)S(1)} %shard_map.84), channel_id=3, replica_groups=mesh['zh'=2,'zl'=4,'y'=4,'core'=2,'section'=2,'tp'=4] {'tp'}, dimensions={0}, use_global_device_ids=true | all-gather | bytes 655360 | tf_op jit(solution)/shard_map/all_gather | solution.py:279
  82.2 3.4 %collective-permute-done.2 = bf16[128,512]{1,0:T(8,128)(2,1)S(1)} collective-permute-done((bf16[128,512]{1,0:T(8,128)(2,1)S(1)}, bf16[128,512]{1,0:T(8,128)(2,1)S(1)}, u32[]{:S(2)}, u32[]{:S(2)}) %collective-permute-start.2) | collective-permute-done | bytes 131104 | tf_op jit(solution)/shard_map/ppermute | solution.py:26
  86.4 5.6 %all-to-all-start.1 = ((bf16[4,128,512]{2,1,0:T(8,128)(2,1)}), bf16[4,128,512]{2,1,0:T(8,128)(2,1)S(1)}, u32[]{:S(2)}, u32[]{:S(2)}) async-start(bf16[4,128,512]{2,1,0:T(8,128)(2,1)} %broadcast_in_dim.4), calls=%async_computation.1 | async-start | bytes 1048576 | tf_op jit(solution)/shard_map/all_to_all | solution.py:30
  92.1 2.8 %collective-permute-start.3 = (bf16[4,128,512]{2,1,0:T(8,128)(2,1)S(1)}, bf16[4,128,512]{2,1,0:T(8,128)(2,1)S(1)}, u32[]{:S(2)}, u32[]{:S(2)}) collective-permute-start(bf16[4,128,512]{2,1,0:T(8,128)(2,1)S(1)} %bitcast.13), channel_id=1, source_target_pairs={{0,8},{8,0},{1,9},{9,1},{2,10},{10,2},{3,11},{11,3},{4,12},{12,4},... | collective-permute-start | bytes 1572872 | tf_op jit(solution)/shard_map/ppermute | solution.py:26
  94.9 5.9 %all-to-all-done.1.own_b = bf16[4,128,512]{2,1,0:T(8,128)(2,1)S(1)} async-done(((bf16[4,128,512]{2,1,0:T(8,128)(2,1)}), bf16[4,128,512]{2,1,0:T(8,128)(2,1)S(1)}, u32[]{:S(2)}, u32[]{:S(2)}) %all-to-all-start.1) | async-done | bytes 524320 | tf_op jit(solution)/shard_map/all_to_all | solution.py:30
  100.8 3.6 %collective-permute-start.4 = (bf16[4,128,512]{2,1,0:T(8,128)(2,1)S(1)}, bf16[4,128,512]{2,1,0:T(8,128)(2,1)S(1)}, u32[]{:S(2)}, u32[]{:S(2)}) collective-permute-start(bf16[4,128,512]{2,1,0:T(8,128)(2,1)S(1)} %all-to-all-done.1.own_b), channel_id=1, source_target_pairs={{0,8},{8,0},{1,9},{9,1},{2,10},{10,2},{3,11},{11,3},{4,12},{12,4},... | collective-permute-start | bytes 1572872 | tf_op jit(solution)/shard_map/ppermute | solution.py:26
  107.2 3.9 %shard_map.85 = (bf16[256,128]{1,0:T(8,128)(2,1)S(1)}, bf16[256,256]{1,0:T(8,128)(2,1)S(1)}, bf16[4,256,256]{2,1,0:T(8,128)(2,1)}) custom-call(s32[1]{0:T(128)} %bitcast.4.flip, bf16[4,128,512]{2,1,0:T(8,128)(2,1)S(1)} %bitcast.14, bf16[4,128,512]{2,1,0:T(8,128)(2,1)S(1)} %all-to-all-done.1.own_b, bf16[4,128,512]{2,1,0:T(8,128)(2,1)S(1)} %collective-permute-done.3.other_a, ...), custom_call_target="tpu_custom_call" | custom-call | flops 805306368 | bytes 6291456 | tf_op jit(solution)/shard_map/pallas_call | solution.py:284
  111.2 4.5 %all-to-all-start.2 = ((bf16[4,256,256]{2,1,0:T(8,128)(2,1)}), bf16[4,256,256]{2,1,0:T(8,128)(2,1)S(1)}, u32[]{:S(2)}, u32[]{:S(2)}) async-start(bf16[4,256,256]{2,1,0:T(8,128)(2,1)} %get-tuple-element.25), calls=%async_computation.2 | async-start | bytes 1048576 | tf_op jit(solution)/shard_map/all_to_all | solution.py:314
  115.7 7.3 %collective-permute-start.5 = (bf16[256,256]{1,0:T(8,128)(2,1)S(1)}, bf16[256,256]{1,0:T(8,128)(2,1)S(1)}, u32[]{:S(2)}, u32[]{:S(2)}) collective-permute-start(bf16[256,256]{1,0:T(8,128)(2,1)S(1)} %get-tuple-element.26), channel_id=1, source_target_pairs={{0,256},{256,0},{1,257},{257,1},{2,258},{258,2},{3,259},{259,3},{4... | collective-permute-start | bytes 393224 | tf_op jit(solution)/shard_map/ppermute | solution.py:26
  123.0 9.7 %all-gather.3 = bf16[1024,128]{1,0:T(8,128)(2,1)S(1)} all-gather(bf16[256,128]{1,0:T(8,128)(2,1)S(1)} %get-tuple-element.27), channel_id=5, replica_groups=mesh['zh'=2,'zl'=4,'y'=4,'core'=2,'section'=2,'tp'=4] {'y'}, dimensions={0}, use_global_device_ids=true | all-gather | bytes 327680 | tf_op jit(solution)/shard_map/all_gather | solution.py:315
  132.7 2.6 %all-to-all-done.2.kv = bf16[4,256,256]{2,1,0:T(8,128)(2,1)S(1)} async-done(((bf16[4,256,256]{2,1,0:T(8,128)(2,1)}), bf16[4,256,256]{2,1,0:T(8,128)(2,1)S(1)}, u32[]{:S(2)}, u32[]{:S(2)}) %all-to-all-start.2) | async-done | bytes 524320 | tf_op jit(solution)/shard_map/all_to_all | solution.py:314
  136.1 6.7 %all-to-all-start.3 = ((bf16[4,256,256]{2,1,0:T(8,128)(2,1)}), bf16[4,256,256]{2,1,0:T(8,128)(2,1)S(1)}, u32[]{:S(2)}, u32[]{:S(2)}) async-start(bf16[4,256,256]{2,1,0:T(8,128)(2,1)} %broadcast_in_dim.5), calls=%async_computation.3 | async-start | bytes 1048576 | tf_op jit(solution)/shard_map/all_to_all | solution.py:30
  142.9 3.0 %shard_map.86 = (f32[4,256,128]{2,1,0:T(8,128)S(1)}, f32[4,256,128]{2,1,0:T(8,128)S(1)}) custom-call(s32[4]{0:T(128)S(1)} %pad_add_fusion.place, bf16[4,256,128]{2,1,0:T(8,128)(2,1)S(1)} %bitcast.15, bf16[4,256,256]{2,1,0:T(8,128)(2,1)S(1)} %all-to-all-done.2.kv), custom_call_target="tpu_custom_call" | custom-call | flops 536870912 | bytes 2097152 | tf_op jit(solution)/shard_map/pallas_call | solution.py:321
  145.9 10.9 %all-to-all-done.3.kv = bf16[4,256,256]{2,1,0:T(8,128)(2,1)S(1)} async-done(((bf16[4,256,256]{2,1,0:T(8,128)(2,1)}), bf16[4,256,256]{2,1,0:T(8,128)(2,1)S(1)}, u32[]{:S(2)}, u32[]{:S(2)}) %all-to-all-start.3) | async-done | bytes 524320 | tf_op jit(solution)/shard_map/all_to_all | solution.py:30
  157.8 11.7 %all_to_all.25.parts = bf16[8,136,128]{2,1,0:T(8,128)(2,1)S(1)} all-to-all(bf16[8,136,128]{2,1,0:T(8,128)(2,1)S(1)} %shard_map.87), channel_id=1, replica_groups=mesh['zh'=2,'zl'=4,'y'=4,'core'=2,'section'=2,'tp'=4] {'y','core'}, dimensions={0} | all-to-all | bytes 557056 | tf_op jit(solution)/shard_map/all_to_all | solution.py:329
  169.5 1.4 shard_map.88
  (32 shorter events, 11.0 us)
Async XLA Ops:
  6.5 51.5 %copy-start = (bf16[1024,512]{1,0:T(8,128)(2,1)S(1)}, bf16[1024,512]{1,0:T(8,128)(2,1)}, u32[]{:S(2)}) copy-start(bf16[1024,512]{1,0:T(8,128)(2,1)} %param.11) | copy-start | bytes 3145732
  8.1 23.5 %collective-permute-start = (bf16[64,768]{1,0:T(8,128)(2,1)}, bf16[64,768]{1,0:T(8,128)(2,1)S(1)}, u32[]{:S(2)}, u32[]{:S(2)}) collective-permute-start(bf16[64,768]{1,0:T(8,128)(2,1)} %shard_map.82.own), channel_id=1, source_target_pairs={{0,256},{256,0},{1,257},{257,1},{2,258},{258,2},{3,259},{259,3},{4... | collective-permute-start | bytes 294920 | tf_op jit(solution)/shard_map/ppermute | solution.py:26
  17.7 13.8 %collective-permute-start.1 = (bf16[128,128]{1,0:T(8,128)(2,1)}, bf16[128,128]{1,0:T(8,128)(2,1)S(1)}, u32[]{:S(2)}, u32[]{:S(2)}) collective-permute-start(bf16[128,128]{1,0:T(8,128)(2,1)} %param.9), channel_id=1, source_target_pairs={{0,4},{4,0},{1,5},{5,1},{2,6},{6,2},{3,7},{7,3},{8,12},{12,8},{9,1... | collective-permute-start | bytes 98312 | tf_op jit(solution)/shard_map/ppermute | solution.py:26
  31.6 0.9 copy-start.1
  33.4 58.6 %copy-start.4 = (bf16[4096]{0:T(1024)(128)(2,1)S(1)}, bf16[4096]{0:T(1024)(128)(2,1)}, u32[]{:S(2)}) copy-start(bf16[4096]{0:T(1024)(128)(2,1)} %param.12) | copy-start | bytes 24580
  33.5 33.0 %all-to-all-start = ((bf16[8,2,64,384]{3,2,1,0:T(8,128)(2,1)}), bf16[8,2,64,384]{3,2,1,0:T(8,128)(2,1)S(1)}, u32[]{:S(2)}, u32[]{:S(2)}) async-start(bf16[8,2,64,384]{3,2,1,0:T(8,128)(2,1)} %shard_map.83), calls=%async_computation | async-start | bytes 1572864 | tf_op jit(solution)/shard_map/all_to_all | solution.py:269
  46.4 60.8 %all-gather.6.cloned.1.call-start = ((), (), s32[]{:S(2)}) async-start(), calls=%async_computation.5 | async-start | bytes 3932160 | tf_op jit(solution)/shard_map/all_gather | solution.py:277
  58.0 0.9 copy-start.2
  66.5 0.9 copy-start.3
  67.4 18.2 %collective-permute-start.2 = (bf16[128,512]{1,0:T(8,128)(2,1)S(1)}, bf16[128,512]{1,0:T(8,128)(2,1)S(1)}, u32[]{:S(2)}, u32[]{:S(2)}) collective-permute-start(bf16[128,512]{1,0:T(8,128)(2,1)S(1)} %shard_map.84), channel_id=1, source_target_pairs={{0,4},{4,0},{1,5},{5,1},{2,6},{6,2},{3,7},{7,3},{8,12},{12,8},{9,1... | collective-permute-start | bytes 393224 | tf_op jit(solution)/shard_map/ppermute | solution.py:26
  86.4 14.3 %all-to-all-start.1 = ((bf16[4,128,512]{2,1,0:T(8,128)(2,1)}), bf16[4,128,512]{2,1,0:T(8,128)(2,1)S(1)}, u32[]{:S(2)}, u32[]{:S(2)}) async-start(bf16[4,128,512]{2,1,0:T(8,128)(2,1)} %broadcast_in_dim.4), calls=%async_computation.1 | async-start | bytes 1048576 | tf_op jit(solution)/shard_map/all_to_all | solution.py:30
  92.1 13.0 %collective-permute-start.3 = (bf16[4,128,512]{2,1,0:T(8,128)(2,1)S(1)}, bf16[4,128,512]{2,1,0:T(8,128)(2,1)S(1)}, u32[]{:S(2)}, u32[]{:S(2)}) collective-permute-start(bf16[4,128,512]{2,1,0:T(8,128)(2,1)S(1)} %bitcast.13), channel_id=1, source_target_pairs={{0,8},{8,0},{1,9},{9,1},{2,10},{10,2},{3,11},{11,3},{4,12},{12,4},... | collective-permute-start | bytes 1572872 | tf_op jit(solution)/shard_map/ppermute | solution.py:26
  100.8 5.2 %collective-permute-start.4 = (bf16[4,128,512]{2,1,0:T(8,128)(2,1)S(1)}, bf16[4,128,512]{2,1,0:T(8,128)(2,1)S(1)}, u32[]{:S(2)}, u32[]{:S(2)}) collective-permute-start(bf16[4,128,512]{2,1,0:T(8,128)(2,1)S(1)} %all-to-all-done.1.own_b), channel_id=1, source_target_pairs={{0,8},{8,0},{1,9},{9,1},{2,10},{10,2},{3,11},{11,3},{4,12},{12,4},... | collective-permute-start | bytes 1572872 | tf_op jit(solution)/shard_map/ppermute | solution.py:26
  111.2 24.1 %all-to-all-start.2 = ((bf16[4,256,256]{2,1,0:T(8,128)(2,1)}), bf16[4,256,256]{2,1,0:T(8,128)(2,1)S(1)}, u32[]{:S(2)}, u32[]{:S(2)}) async-start(bf16[4,256,256]{2,1,0:T(8,128)(2,1)} %get-tuple-element.25), calls=%async_computation.2 | async-start | bytes 1048576 | tf_op jit(solution)/shard_map/all_to_all | solution.py:314
  115.7 17.0 %collective-permute-start.5 = (bf16[256,256]{1,0:T(8,128)(2,1)S(1)}, bf16[256,256]{1,0:T(8,128)(2,1)S(1)}, u32[]{:S(2)}, u32[]{:S(2)}) collective-permute-start(bf16[256,256]{1,0:T(8,128)(2,1)S(1)} %get-tuple-element.26), channel_id=1, source_target_pairs={{0,256},{256,0},{1,257},{257,1},{2,258},{258,2},{3,259},{259,3},{4... | collective-permute-start | bytes 393224 | tf_op jit(solution)/shard_map/ppermute | solution.py:26
  136.1 20.7 %all-to-all-start.3 = ((bf16[4,256,256]{2,1,0:T(8,128)(2,1)}), bf16[4,256,256]{2,1,0:T(8,128)(2,1)S(1)}, u32[]{:S(2)}, u32[]{:S(2)}) async-start(bf16[4,256,256]{2,1,0:T(8,128)(2,1)} %broadcast_in_dim.5), calls=%async_computation.3 | async-start | bytes 1048576 | tf_op jit(solution)/shard_map/all_to_all | solution.py:30
Sparse Core Ops, SparseCore 0:
  67.5 39.6 all-gather.5

commit v4 on v3

--- a/solution.py
+++ b/solution.py
@@ -48,7 +48,9 @@
 ):
     copies = [
         pltpu.make_async_copy(
-            stored.at[:, t * CORES : (t + 1) * CORES], weight.at[:, t * CORES : (t + 1) * CORES], sem.at[t]
+            stored.at[:, :, t * CORES : (t + 1) * CORES],
+            weight.at[:, :, t * CORES : (t + 1) * CORES],
+            sem.at[t],
         )
         for t in range(TP)
     ]
@@ -69,7 +71,7 @@
         wide = jnp.concatenate([own[t], other[t]], axis=0).astype(jnp.float32)
         normed = (wide * inverse * gain[i : i + 1, :]).astype(jnp.bfloat16)
         block = jnp.concatenate(
-            [weight[y, t * CORES + c, half] for y in range(Y) for c in range(CORES)], axis=0
+            [weight[y, half, t * CORES + c] for y in range(Y) for c in range(CORES)], axis=0
         )
         total = total + jnp.dot(normed, block, preferred_element_type=jnp.float32)
     q = total[:, :HD]
@@ -201,24 +203,24 @@
         out[:, h * HD : (h + 1) * HD] = (result / total).astype(jnp.bfloat16)
 
 
-def join_kernel(q, k, v, out, sems):
+def spread_kernel(w, out):
+    for h in range(CORES):
+        for i in range(3):
+            block = w[:, (2 * i + h) * HD : (2 * i + h + 1) * HD]
+            for l in range(ZL):
+                out[l * CORES + h, :, i * HD : (i + 1) * HD] = block
+
+
+def join_kernel(q, k, v, joined, out, sems):
     copies = [
-        pltpu.make_async_copy(w, out.at[:, i * 2 * HD : (i + 1) * 2 * HD], sems.at[i])
+        pltpu.make_async_copy(w, joined.at[:, i * 2 * HD : (i + 1) * 2 * HD], sems.at[i])
         for i, w in enumerate((q, k, v))
     ]
     for copy in copies:
         copy.start()
     for copy in copies:
         copy.wait()
-
-
-def spread_kernel(own, partner, out):
-    for h in range(CORES):
-        for zr, w in enumerate((own, partner)):
-            for i in range(3):
-                block = w[:, (2 * i + h) * HD : (2 * i + h + 1) * HD]
-                for l in range(ZL):
-                    out[l * CORES + h, zr, :, i * HD : (i + 1) * HD] = block
+    spread_kernel(joined, out)
 
 
 def call(kernel, outs, n_scalars, n_arrays, flops, size, scratch=()):
@@ -252,29 +254,27 @@
     gains = gain.astype(jnp.float32).reshape(SECTIONS, TP, 512)
     gains = jnp.where(section == 0, gains, gains[::-1]).reshape(8, 512)
     feats_b = swap(feats, "section")
-    weight = pl.pallas_call(
+    weight, spread = pl.pallas_call(
         join_kernel,
-        out_shape=shaped(64, 6 * HD),
+        out_shape=[shaped(64, 6 * HD), shaped(ZL * CORES, 64, 3 * HD)],
         in_specs=[pl.BlockSpec(memory_space=pl.ANY)] * 3,
-        out_specs=VMEM,
+        out_specs=[VMEM] * 2,
         scratch_shapes=[pltpu.SemaphoreType.DMA((3,))],
-        cost_estimate=pl.CostEstimate(flops=0, bytes_accessed=200000, transcendentals=0),
+        cost_estimate=pl.CostEstimate(flops=0, bytes_accessed=800000, transcendentals=0),
     )(q_weight, k_weight, v_weight)
     weight_b = swap(weight, "zh")
-
-    weight_b, feats_b = lax.optimization_barrier((weight_b, feats_b))
-    (weight,) = call(spread_kernel, [shaped(ZL * CORES, ZH, 64, 3 * HD)], 0, 2, 1000, 1 << 20)(
-        weight, weight_b
-    )
-    weight = lax.all_to_all(weight, ("zl", "core"), 0, 0, tiled=True)
+    weight_a = lax.all_to_all(spread, ("zl", "core"), 0, 0, tiled=True)
+    weight_a, weight_b, feats_b = lax.optimization_barrier((weight_a, weight_b, feats_b))
+    (spread,) = call(spread_kernel, [shaped(ZL * CORES, 64, 3 * HD)], 0, 1, 1000, 1 << 20)(weight_b)
+    weight_b = lax.all_to_all(spread, ("zl", "core"), 0, 0, tiled=True)
 
     feats = lax.all_gather(jnp.stack([feats, feats_b]), "tp", axis=0)
     (joined,) = call(join_frames_kernel, [shaped(ROWS, 512)], 1, 3, 2 * ROWS * 1024 * 512, 2 << 20)(
         jnp.stack([section, count[0]]), feats, proj.reshape(8, HD, 512), text
     )
 
-    weight, joined = lax.optimization_barrier((weight, joined))
-    weight = lax.all_gather(weight, "y", axis=0)
+    weight_b, joined = lax.optimization_barrier((weight_b, joined))
+    weight = lax.all_gather(jnp.stack([weight_a, weight_b]), "y", axis=0)
     joined_b = swap(joined, "section")
     own_a = lax.all_gather(joined, "tp", axis=0)
     own_a, joined_b = lax.optimization_barrier((own_a, joined_b))
@@ -291,7 +291,7 @@
         in_specs=[SMEM] + [VMEM] * 4 + [pl.BlockSpec(memory_space=pltpu.HBM)] + [VMEM] * 3,
         out_specs=[VMEM] * 3,
         scratch_shapes=[
-            pltpu.VMEM((Y, ZL * CORES, ZH, 64, 3 * HD), jnp.bfloat16),
+            pltpu.VMEM((Y, ZH, ZL * CORES, 64, 3 * HD), jnp.bfloat16),
             pltpu.SemaphoreType.DMA((TP,)),
         ],
         compiler_params=pltpu.CompilerParams(vmem_limit_bytes=LIMIT),

time: 178 us -> 180 us (1.011)
  starting transfers between devices: 67.1 us -> 79.8 us
  waiting for transfers between devices: 34.7 us -> 26.6 us
  blocking collectives: 43.1 us -> 41 us
  local copies, waits for them, and re-layouts: 4.41 us -> 2.61 us
    ppermute x6, starting transfers between devices: 37.3 us -> 45.4 us  [swap(): return lax.ppermute(v, axis, SWAP)]
    all_to_all x1 -> x2, waiting for transfers between devices: 6.59 us -> 0.01 us  [the longest x1 0.01 us: local(): weight_a = lax.all_to_all(spread, ('zl', 'core'), 0, 0, tiled=True)]
    all_to_all x1 -> x2, starting transfers between devices: 12.9 us -> 18.9 us  [the longest x1 10.2 us: local(): weight_a = lax.all_to_all(spread, ('zl', 'core'), 0, 0, tiled=True)]
    all_to_all x2, waiting for transfers between devices: 16.8 us -> 10.9 us  [gather(): lax.all_to_all(jnp.broadcast_to(v[None], (n, *v.shape)), axis, 0, 0, tile...]
    all_gather x1, waiting for transfers between devices: 1.28 us -> 6.68 us  [local(): weight = lax.all_gather(jnp.stack([weight_a, weight_b]), 'y', axis=0)]
  transfers between devices with their start and end apart: 11 -> 12, of which waited for: 8 -> 5; matrix products, arithmetic and copies ran while one was open for 1% -> 1% of each run, Pallas kernels for 2% -> 2%
where the time goes in v4:
time: 180 us
  starting transfers between devices  79.8 us (44%)
  blocking collectives  41 us (23%)
  waiting for transfers between devices  26.6 us (15%)
  between operations  14.2 us (8%)
  Pallas kernels  12.7 us (7%)
  local copies, waits for them, and re-layouts  2.61 us (1%)
  other arithmetic  2.59 us (1%)
    ppermute x6, starting transfers between devices, swap(): return lax.ppermute(v, axis, SWAP)  45.4 us
    all_to_all x1, blocking collectives, local(): parts = lax.all_to_all(parts, ('y', 'core'), 0, 0, tiled=True)  11.7 us
    all_to_all x2, waiting for transfers between devices, gather(): lax.all_to_all(jnp.broadcast_to(v[None], (n, *v.shape)), axis, 0, 0, tile...  10.9 us
    all_to_all x2, starting transfers between devices, gather(): lax.all_to_all(jnp.broadcast_to(v[None], (n, *v.shape)), axis, 0, 0, tile...  10.9 us
    all_to_all x1, starting transfers between devices, local(): weight_a = lax.all_to_all(spread, ('zl', 'core'), 0, 0, tiled=True)  10.2 us
    all_gather x1, blocking collectives, local(): own_a = lax.all_gather(joined, 'tp', axis=0)  10.2 us
    all_gather x1, blocking collectives, local(): queries = lax.all_gather(queries, 'y', axis=0)  9.67 us
    all_gather x1, blocking collectives, local(): feats = lax.all_gather(jnp.stack([feats, feats_b]), 'tp', axis=0)  9.51 us
  transfers between devices with their start and end apart: 12, of which 5 were waited for; matrix products, arithmetic and copies ran while one was open for 1% of the time, Pallas kernels for 2%

profile of v4, /device:TPU:1, one launch (start us, length us, event | category | flops | bytes accessed | tf_op | source)
XLA Modules:
  0.0 179.5 jit_solution(17568746077695903844)
XLA Ops:
  6.5 1.7 shard_map.82
  8.2 10.2 %all-to-all-start = ((bf16[8,64,384]{2,1,0:T(8,128)(2,1)}), bf16[8,64,384]{2,1,0:T(8,128)(2,1)S(1)}, u32[]{:S(2)}, u32[]{:S(2)}) async-start(bf16[8,64,384]{2,1,0:T(8,128)(2,1)} %get-tuple-element.22), calls=%async_computation | async-start | bytes 786432 | tf_op jit(solution)/shard_map/all_to_all | solution.py:266
  18.5 6.0 %collective-permute-start = (bf16[64,768]{1,0:T(8,128)(2,1)}, bf16[64,768]{1,0:T(8,128)(2,1)S(1)}, u32[]{:S(2)}, u32[]{:S(2)}) collective-permute-start(bf16[64,768]{1,0:T(8,128)(2,1)} %get-tuple-element.23), channel_id=1, source_target_pairs={{0,256},{256,0},{1,257},{257,1},{2,258},{258,2},{3,259},{259,3},{4... | collective-permute-start | bytes 294920 | tf_op jit(solution)/shard_map/ppermute | solution.py:26
  24.5 8.1 %collective-permute-start.1 = (bf16[128,128]{1,0:T(8,128)(2,1)}, bf16[128,128]{1,0:T(8,128)(2,1)S(1)}, u32[]{:S(2)}, u32[]{:S(2)}) collective-permute-start(bf16[128,128]{1,0:T(8,128)(2,1)} %param.9), channel_id=1, source_target_pairs={{0,4},{4,0},{1,5},{5,1},{2,6},{6,2},{3,7},{7,3},{8,12},{12,8},{9,1... | collective-permute-start | bytes 98312 | tf_op jit(solution)/shard_map/ppermute | solution.py:26
  32.6 5.6 %collective-permute-done.1 = bf16[128,128]{1,0:T(8,128)(2,1)S(1)} collective-permute-done((bf16[128,128]{1,0:T(8,128)(2,1)}, bf16[128,128]{1,0:T(8,128)(2,1)S(1)}, u32[]{:S(2)}, u32[]{:S(2)}) %collective-permute-start.1) | collective-permute-done | bytes 32800 | tf_op jit(solution)/shard_map/ppermute | solution.py:26
  39.0 8.7 %all-to-all-start.1 = ((bf16[8,64,384]{2,1,0:T(8,128)(2,1)}), bf16[8,64,384]{2,1,0:T(8,128)(2,1)S(1)}, u32[]{:S(2)}, u32[]{:S(2)}) async-start(bf16[8,64,384]{2,1,0:T(8,128)(2,1)} %shard_map.83), calls=%async_computation.1 | async-start | bytes 786432 | tf_op jit(solution)/shard_map/all_to_all | solution.py:269
  49.2 9.5 %all-gather = bf16[8,128,128]{2,1,0:T(8,128)(2,1)S(1)} all-gather(bf16[2,128,128]{2,1,0:T(8,128)(2,1)S(1)} %pad_maximum_fusion.3), channel_id=2, replica_groups=mesh['zh'=2,'zl'=4,'y'=4,'core'=2,'section'=2,'tp'=4] {'tp'}, dimensions={0}, use_global_device_ids=true | all-gather | bytes 327680 | tf_op jit(solution)/shard_map/all_gather | solution.py:271
  60.6 1.0 pad_maximum_fusion
  61.6 8.8 %collective-permute-start.2 = (bf16[128,512]{1,0:T(8,128)(2,1)S(1)}, bf16[128,512]{1,0:T(8,128)(2,1)S(1)}, u32[]{:S(2)}, u32[]{:S(2)}) collective-permute-start(bf16[128,512]{1,0:T(8,128)(2,1)S(1)} %shard_map.84), channel_id=1, source_target_pairs={{0,4},{4,0},{1,5},{5,1},{2,6},{6,2},{3,7},{7,3},{8,12},{12,8},{9,1... | collective-permute-start | bytes 393224 | tf_op jit(solution)/shard_map/ppermute | solution.py:26
  70.4 10.2 %all-gather.1 = bf16[512,512]{1,0:T(8,128)(2,1)S(1)} all-gather(bf16[128,512]{1,0:T(8,128)(2,1)S(1)} %shard_map.84), channel_id=3, replica_groups=mesh['zh'=2,'zl'=4,'y'=4,'core'=2,'section'=2,'tp'=4] {'tp'}, dimensions={0}, use_global_device_ids=true | all-gather | bytes 655360 | tf_op jit(solution)/shard_map/all_gather | solution.py:279
  81.4 4.1 %all-to-all-start.2 = ((bf16[4,128,512]{2,1,0:T(8,128)(2,1)}), bf16[4,128,512]{2,1,0:T(8,128)(2,1)S(1)}, u32[]{:S(2)}, u32[]{:S(2)}) async-start(bf16[4,128,512]{2,1,0:T(8,128)(2,1)} %broadcast_in_dim.4), calls=%async_computation.2 | async-start | bytes 1048576 | tf_op jit(solution)/shard_map/all_to_all | solution.py:30
  85.6 7.3 %collective-permute-start.3 = (bf16[4,128,512]{2,1,0:T(8,128)(2,1)S(1)}, bf16[4,128,512]{2,1,0:T(8,128)(2,1)S(1)}, u32[]{:S(2)}, u32[]{:S(2)}) collective-permute-start(bf16[4,128,512]{2,1,0:T(8,128)(2,1)S(1)} %bitcast.15), channel_id=1, source_target_pairs={{0,8},{8,0},{1,9},{9,1},{2,10},{10,2},{3,11},{11,3},{4,12},{12,4},... | collective-permute-start | bytes 1572872 | tf_op jit(solution)/shard_map/ppermute | solution.py:26
  92.9 7.9 %collective-permute-start.4 = (bf16[4,128,512]{2,1,0:T(8,128)(2,1)S(1)}, bf16[4,128,512]{2,1,0:T(8,128)(2,1)S(1)}, u32[]{:S(2)}, u32[]{:S(2)}) collective-permute-start(bf16[4,128,512]{2,1,0:T(8,128)(2,1)S(1)} %all-to-all-done.2.own_b), channel_id=1, source_target_pairs={{0,8},{8,0},{1,9},{9,1},{2,10},{10,2},{3,11},{11,3},{4,12},{12,4},... | collective-permute-start | bytes 1572872 | tf_op jit(solution)/shard_map/ppermute | solution.py:26
  102.3 6.7 %all-gather.6.cloned.1.call-done = bf16[8,8,64,384]{3,2,1,0:T(8,128)(2,1)} async-done(((bf16[2,8,64,384]{3,2,1,0:T(8,128)(2,1)}), bf16[8,8,64,384]{3,2,1,0:T(8,128)(2,1)}) %all-gather.6.cloned.1.call-update) | async-done | bytes 3145744 | tf_op jit(solution)/shard_map/all_gather | solution.py:277
  109.0 4.0 %shard_map.85 = (bf16[256,128]{1,0:T(8,128)(2,1)S(1)}, bf16[256,256]{1,0:T(8,128)(2,1)S(1)}, bf16[4,256,256]{2,1,0:T(8,128)(2,1)}) custom-call(s32[1]{0:T(128)} %bitcast.4.flip, bf16[4,128,512]{2,1,0:T(8,128)(2,1)S(1)} %bitcast.16, bf16[4,128,512]{2,1,0:T(8,128)(2,1)S(1)} %all-to-all-done.2.own_b, bf16[4,128,512]{2,1,0:T(8,128)(2,1)S(1)} %collective-permute-done.3.other_a, ...), custom_call_target="tpu_custom_call" | custom-call | flops 805306368 | bytes 6291456 | tf_op jit(solution)/shard_map/pallas_call | solution.py:284
  113.0 4.5 %all-to-all-start.3 = ((bf16[4,256,256]{2,1,0:T(8,128)(2,1)}), bf16[4,256,256]{2,1,0:T(8,128)(2,1)S(1)}, u32[]{:S(2)}, u32[]{:S(2)}) async-start(bf16[4,256,256]{2,1,0:T(8,128)(2,1)} %get-tuple-element.31), calls=%async_computation.3 | async-start | bytes 1048576 | tf_op jit(solution)/shard_map/all_to_all | solution.py:314
  117.5 7.4 %collective-permute-start.5 = (bf16[256,256]{1,0:T(8,128)(2,1)S(1)}, bf16[256,256]{1,0:T(8,128)(2,1)S(1)}, u32[]{:S(2)}, u32[]{:S(2)}) collective-permute-start(bf16[256,256]{1,0:T(8,128)(2,1)S(1)} %get-tuple-element.32), channel_id=1, source_target_pairs={{0,256},{256,0},{1,257},{257,1},{2,258},{258,2},{3,259},{259,3},{4... | collective-permute-start | bytes 393224 | tf_op jit(solution)/shard_map/ppermute | solution.py:26
  124.9 9.7 %all-gather.3 = bf16[1024,128]{1,0:T(8,128)(2,1)S(1)} all-gather(bf16[256,128]{1,0:T(8,128)(2,1)S(1)} %get-tuple-element.33), channel_id=5, replica_groups=mesh['zh'=2,'zl'=4,'y'=4,'core'=2,'section'=2,'tp'=4] {'y'}, dimensions={0}, use_global_device_ids=true | all-gather | bytes 327680 | tf_op jit(solution)/shard_map/all_gather | solution.py:315
  134.6 2.6 %all-to-all-done.3.kv = bf16[4,256,256]{2,1,0:T(8,128)(2,1)S(1)} async-done(((bf16[4,256,256]{2,1,0:T(8,128)(2,1)}), bf16[4,256,256]{2,1,0:T(8,128)(2,1)S(1)}, u32[]{:S(2)}, u32[]{:S(2)}) %all-to-all-start.3) | async-done | bytes 524320 | tf_op jit(solution)/shard_map/all_to_all | solution.py:314
  138.0 6.7 %all-to-all-start.4 = ((bf16[4,256,256]{2,1,0:T(8,128)(2,1)}), bf16[4,256,256]{2,1,0:T(8,128)(2,1)S(1)}, u32[]{:S(2)}, u32[]{:S(2)}) async-start(bf16[4,256,256]{2,1,0:T(8,128)(2,1)} %broadcast_in_dim.5), calls=%async_computation.4 | async-start | bytes 1048576 | tf_op jit(solution)/shard_map/all_to_all | solution.py:30
  144.8 3.0 %shard_map.86 = (f32[4,256,128]{2,1,0:T(8,128)S(1)}, f32[4,256,128]{2,1,0:T(8,128)S(1)}) custom-call(s32[4]{0:T(128)S(1)} %pad_add_fusion.place, bf16[4,256,128]{2,1,0:T(8,128)(2,1)S(1)} %bitcast.17, bf16[4,256,256]{2,1,0:T(8,128)(2,1)S(1)} %all-to-all-done.3.kv), custom_call_target="tpu_custom_call" | custom-call | flops 536870912 | bytes 2097152 | tf_op jit(solution)/shard_map/pallas_call | solution.py:321
  147.7 10.9 %all-to-all-done.4.kv = bf16[4,256,256]{2,1,0:T(8,128)(2,1)S(1)} async-done(((bf16[4,256,256]{2,1,0:T(8,128)(2,1)}), bf16[4,256,256]{2,1,0:T(8,128)(2,1)S(1)}, u32[]{:S(2)}, u32[]{:S(2)}) %all-to-all-start.4) | async-done | bytes 524320 | tf_op jit(solution)/shard_map/all_to_all | solution.py:30
  159.6 11.7 %all_to_all.30.parts = bf16[8,136,128]{2,1,0:T(8,128)(2,1)S(1)} all-to-all(bf16[8,136,128]{2,1,0:T(8,128)(2,1)S(1)} %shard_map.87), channel_id=1, replica_groups=mesh['zh'=2,'zl'=4,'y'=4,'core'=2,'section'=2,'tp'=4] {'y','core'}, dimensions={0} | all-to-all | bytes 557056 | tf_op jit(solution)/shard_map/all_to_all | solution.py:329
  171.3 1.4 shard_map.88
  (31 shorter events, 7.8 us)
Async XLA Ops:
  6.5 52.1 %copy-start = (bf16[1024,512]{1,0:T(8,128)(2,1)S(1)}, bf16[1024,512]{1,0:T(8,128)(2,1)}, u32[]{:S(2)}) copy-start(bf16[1024,512]{1,0:T(8,128)(2,1)} %param.11) | copy-start | bytes 3145732
  8.2 29.9 %all-to-all-start = ((bf16[8,64,384]{2,1,0:T(8,128)(2,1)}), bf16[8,64,384]{2,1,0:T(8,128)(2,1)S(1)}, u32[]{:S(2)}, u32[]{:S(2)}) async-start(bf16[8,64,384]{2,1,0:T(8,128)(2,1)} %get-tuple-element.22), calls=%async_computation | async-start | bytes 786432 | tf_op jit(solution)/shard_map/all_to_all | solution.py:266
  18.5 19.7 %collective-permute-start = (bf16[64,768]{1,0:T(8,128)(2,1)}, bf16[64,768]{1,0:T(8,128)(2,1)S(1)}, u32[]{:S(2)}, u32[]{:S(2)}) collective-permute-start(bf16[64,768]{1,0:T(8,128)(2,1)} %get-tuple-element.23), channel_id=1, source_target_pairs={{0,256},{256,0},{1,257},{257,1},{2,258},{258,2},{3,259},{259,3},{4... | collective-permute-start | bytes 294920 | tf_op jit(solution)/shard_map/ppermute | solution.py:26
  24.5 13.7 %collective-permute-start.1 = (bf16[128,128]{1,0:T(8,128)(2,1)}, bf16[128,128]{1,0:T(8,128)(2,1)S(1)}, u32[]{:S(2)}, u32[]{:S(2)}) collective-permute-start(bf16[128,128]{1,0:T(8,128)(2,1)} %param.9), channel_id=1, source_target_pairs={{0,4},{4,0},{1,5},{5,1},{2,6},{6,2},{3,7},{7,3},{8,12},{12,8},{9,1... | collective-permute-start | bytes 98312 | tf_op jit(solution)/shard_map/ppermute | solution.py:26
  39.0 21.6 %all-to-all-start.1 = ((bf16[8,64,384]{2,1,0:T(8,128)(2,1)}), bf16[8,64,384]{2,1,0:T(8,128)(2,1)S(1)}, u32[]{:S(2)}, u32[]{:S(2)}) async-start(bf16[8,64,384]{2,1,0:T(8,128)(2,1)} %shard_map.83), calls=%async_computation.1 | async-start | bytes 786432 | tf_op jit(solution)/shard_map/all_to_all | solution.py:269
  47.7 61.3 %all-gather.6.cloned.1.call-start = ((), (), s32[]{:S(2)}) async-start(), calls=%async_computation.6 | async-start | bytes 3932160 | tf_op jit(solution)/shard_map/all_gather | solution.py:277
  58.7 0.9 copy-start.1
  59.6 25.9 %copy-start.2 = (bf16[4096]{0:T(1024)(128)(2,1)S(1)}, bf16[4096]{0:T(1024)(128)(2,1)}, u32[]{:S(2)}) copy-start(bf16[4096]{0:T(1024)(128)(2,1)} %param.12) | copy-start | bytes 24580
  61.6 19.0 %collective-permute-start.2 = (bf16[128,512]{1,0:T(8,128)(2,1)S(1)}, bf16[128,512]{1,0:T(8,128)(2,1)S(1)}, u32[]{:S(2)}, u32[]{:S(2)}) collective-permute-start(bf16[128,512]{1,0:T(8,128)(2,1)S(1)} %shard_map.84), channel_id=1, source_target_pairs={{0,4},{4,0},{1,5},{5,1},{2,6},{6,2},{3,7},{7,3},{8,12},{12,8},{9,1... | collective-permute-start | bytes 393224 | tf_op jit(solution)/shard_map/ppermute | solution.py:26
  81.4 11.5 %all-to-all-start.2 = ((bf16[4,128,512]{2,1,0:T(8,128)(2,1)}), bf16[4,128,512]{2,1,0:T(8,128)(2,1)S(1)}, u32[]{:S(2)}, u32[]{:S(2)}) async-start(bf16[4,128,512]{2,1,0:T(8,128)(2,1)} %broadcast_in_dim.4), calls=%async_computation.2 | async-start | bytes 1048576 | tf_op jit(solution)/shard_map/all_to_all | solution.py:30
  85.6 16.0 %collective-permute-start.3 = (bf16[4,128,512]{2,1,0:T(8,128)(2,1)S(1)}, bf16[4,128,512]{2,1,0:T(8,128)(2,1)S(1)}, u32[]{:S(2)}, u32[]{:S(2)}) collective-permute-start(bf16[4,128,512]{2,1,0:T(8,128)(2,1)S(1)} %bitcast.15), channel_id=1, source_target_pairs={{0,8},{8,0},{1,9},{9,1},{2,10},{10,2},{3,11},{11,3},{4,12},{12,4},... | collective-permute-start | bytes 1572872 | tf_op jit(solution)/shard_map/ppermute | solution.py:26
  92.9 9.5 %collective-permute-start.4 = (bf16[4,128,512]{2,1,0:T(8,128)(2,1)S(1)}, bf16[4,128,512]{2,1,0:T(8,128)(2,1)S(1)}, u32[]{:S(2)}, u32[]{:S(2)}) collective-permute-start(bf16[4,128,512]{2,1,0:T(8,128)(2,1)S(1)} %all-to-all-done.2.own_b), channel_id=1, source_target_pairs={{0,8},{8,0},{1,9},{9,1},{2,10},{10,2},{3,11},{11,3},{4,12},{12,4},... | collective-permute-start | bytes 1572872 | tf_op jit(solution)/shard_map/ppermute | solution.py:26
  113.0 24.1 %all-to-all-start.3 = ((bf16[4,256,256]{2,1,0:T(8,128)(2,1)}), bf16[4,256,256]{2,1,0:T(8,128)(2,1)S(1)}, u32[]{:S(2)}, u32[]{:S(2)}) async-start(bf16[4,256,256]{2,1,0:T(8,128)(2,1)} %get-tuple-element.31), calls=%async_computation.3 | async-start | bytes 1048576 | tf_op jit(solution)/shard_map/all_to_all | solution.py:314
  117.5 17.0 %collective-permute-start.5 = (bf16[256,256]{1,0:T(8,128)(2,1)S(1)}, bf16[256,256]{1,0:T(8,128)(2,1)S(1)}, u32[]{:S(2)}, u32[]{:S(2)}) collective-permute-start(bf16[256,256]{1,0:T(8,128)(2,1)S(1)} %get-tuple-element.32), channel_id=1, source_target_pairs={{0,256},{256,0},{1,257},{257,1},{2,258},{258,2},{3,259},{259,3},{4... | collective-permute-start | bytes 393224 | tf_op jit(solution)/shard_map/ppermute | solution.py:26
  138.0 20.7 %all-to-all-start.4 = ((bf16[4,256,256]{2,1,0:T(8,128)(2,1)}), bf16[4,256,256]{2,1,0:T(8,128)(2,1)S(1)}, u32[]{:S(2)}, u32[]{:S(2)}) async-start(bf16[4,256,256]{2,1,0:T(8,128)(2,1)} %broadcast_in_dim.5), calls=%async_computation.4 | async-start | bytes 1048576 | tf_op jit(solution)/shard_map/all_to_all | solution.py:30
Sparse Core Ops, SparseCore 0:
  61.7 47.2 all-gather.5

commit v5 on v4

--- a/solution.py
+++ b/solution.py
@@ -264,16 +264,14 @@
     )(q_weight, k_weight, v_weight)
     weight_b = swap(weight, "zh")
     weight_a = lax.all_to_all(spread, ("zl", "core"), 0, 0, tiled=True)
-    weight_a, weight_b, feats_b = lax.optimization_barrier((weight_a, weight_b, feats_b))
-    (spread,) = call(spread_kernel, [shaped(ZL * CORES, 64, 3 * HD)], 0, 1, 1000, 1 << 20)(weight_b)
-    weight_b = lax.all_to_all(spread, ("zl", "core"), 0, 0, tiled=True)
-
     feats = lax.all_gather(jnp.stack([feats, feats_b]), "tp", axis=0)
     (joined,) = call(join_frames_kernel, [shaped(ROWS, 512)], 1, 3, 2 * ROWS * 1024 * 512, 2 << 20)(
         jnp.stack([section, count[0]]), feats, proj.reshape(8, HD, 512), text
     )
 
-    weight_b, joined = lax.optimization_barrier((weight_b, joined))
+    weight_a, weight_b, joined = lax.optimization_barrier((weight_a, weight_b, joined))
+    (spread,) = call(spread_kernel, [shaped(ZL * CORES, 64, 3 * HD)], 0, 1, 1000, 1 << 20)(weight_b)
+    weight_b = lax.all_to_all(spread, ("zl", "core"), 0, 0, tiled=True)
     weight = lax.all_gather(jnp.stack([weight_a, weight_b]), "y", axis=0)
     joined_b = swap(joined, "section")
     own_a = lax.all_gather(joined, "tp", axis=0)

time: 180 us -> 185 us (1.028)
  blocking collectives: 41 us -> 65.8 us
  starting transfers between devices: 79.8 us -> 57.7 us
    all_to_all x0 -> x1, blocking collectives: none -> 22.5 us  [local(): weight_b = lax.all_to_all(spread, ('zl', 'core'), 0, 0, tiled=True)]
    ppermute x6, starting transfers between devices: 45.4 us -> 32.7 us  [swap(): return lax.ppermute(v, axis, SWAP)]
    all_to_all x1 -> x0, starting transfers between devices: 8.7 us -> none  [local(): weight_b = lax.all_to_all(spread, ('zl', 'core'), 0, 0, tiled=True)]
    all_to_all x2, waiting for transfers between devices: 10.9 us -> 16.9 us  [gather(): lax.all_to_all(jnp.broadcast_to(v[None], (n, *v.shape)), axis, 0, 0, tile...]
    all_gather x1, waiting for transfers between devices: 6.68 us -> 3.46 us  [local(): weight = lax.all_gather(jnp.stack([weight_a, weight_b]), 'y', axis=0)]
  transfers between devices with their start and end apart: 12 -> 11, of which waited for: 5 -> 7; matrix products, arithmetic and copies ran while one was open for 1% -> 1% of each run, Pallas kernels for 2% -> 2%
where the time goes in v5:
time: 185 us
  blocking collectives  65.8 us (36%)
  starting transfers between devices  57.7 us (31%)
  waiting for transfers between devices  28.4 us (15%)
  between operations  14.2 us (8%)
  Pallas kernels  11.9 us (6%)
  local copies, waits for them, and re-layouts  3.86 us (2%)
  other arithmetic  2.59 us (1%)
    ppermute x6, starting transfers between devices, swap(): return lax.ppermute(v, axis, SWAP)  32.7 us
    all_to_all x1, blocking collectives, local(): weight_b = lax.all_to_all(spread, ('zl', 'core'), 0, 0, tiled=True)  22.5 us
    all_to_all x2, waiting for transfers between devices, gather(): lax.all_to_all(jnp.broadcast_to(v[None], (n, *v.shape)), axis, 0, 0, tile...  16.9 us
    all_to_all x1, blocking collectives, local(): parts = lax.all_to_all(parts, ('y', 'core'), 0, 0, tiled=True)  11.7 us
    all_gather x1, blocking collectives, local(): own_a = lax.all_gather(joined, 'tp', axis=0)  11.4 us
    all_gather x1, blocking collectives, local(): feats = lax.all_gather(jnp.stack([feats, feats_b]), 'tp', axis=0)  10.6 us
    all_to_all x1, starting transfers between devices, local(): weight_a = lax.all_to_all(spread, ('zl', 'core'), 0, 0, tiled=True)  10.2 us
    all_to_all x2, starting transfers between devices, gather(): lax.all_to_all(jnp.broadcast_to(v[None], (n, *v.shape)), axis, 0, 0, tile...  10.2 us
  transfers between devices with their start and end apart: 11, of which 7 were waited for; matrix products, arithmetic and copies ran while one was open for 1% of the time, Pallas kernels for 2%

profile of v5, /device:TPU:1, one launch (start us, length us, event | category | flops | bytes accessed | tf_op | source)
XLA Modules:
  0.0 184.5 jit_solution(456943569396674549)
XLA Ops:
  6.5 1.6 shard_map.82
  8.2 10.2 %all-to-all-start = ((bf16[8,64,384]{2,1,0:T(8,128)(2,1)}), bf16[8,64,384]{2,1,0:T(8,128)(2,1)S(1)}, u32[]{:S(2)}, u32[]{:S(2)}) async-start(bf16[8,64,384]{2,1,0:T(8,128)(2,1)} %get-tuple-element.20), calls=%async_computation | async-start | bytes 786432 | tf_op jit(solution)/shard_map/all_to_all | solution.py:266
  18.4 10.1 %collective-permute-start.1 = (bf16[128,128]{1,0:T(8,128)(2,1)}, bf16[128,128]{1,0:T(8,128)(2,1)S(1)}, u32[]{:S(2)}, u32[]{:S(2)}) collective-permute-start(bf16[128,128]{1,0:T(8,128)(2,1)} %param.9), channel_id=1, source_target_pairs={{0,4},{4,0},{1,5},{5,1},{2,6},{6,2},{3,7},{7,3},{8,12},{12,8},{9,1... | collective-permute-start | bytes 98312 | tf_op jit(solution)/shard_map/ppermute | solution.py:26
  28.5 4.0 %collective-permute-start = (bf16[64,768]{1,0:T(8,128)(2,1)}, bf16[64,768]{1,0:T(8,128)(2,1)S(1)}, u32[]{:S(2)}, u32[]{:S(2)}) collective-permute-start(bf16[64,768]{1,0:T(8,128)(2,1)} %get-tuple-element.21), channel_id=1, source_target_pairs={{0,256},{256,0},{1,257},{257,1},{2,258},{258,2},{3,259},{259,3},{4... | collective-permute-start | bytes 294920 | tf_op jit(solution)/shard_map/ppermute | solution.py:26
  33.2 1.6 collective-permute-done.1
  35.6 10.6 %all-gather = bf16[8,128,128]{2,1,0:T(8,128)(2,1)S(1)} all-gather(bf16[2,128,128]{2,1,0:T(8,128)(2,1)S(1)} %pad_maximum_fusion.3), channel_id=2, replica_groups=mesh['zh'=2,'zl'=4,'y'=4,'core'=2,'section'=2,'tp'=4] {'tp'}, dimensions={0}, use_global_device_ids=true | all-gather | bytes 327680 | tf_op jit(solution)/shard_map/all_gather | solution.py:267
  49.4 22.5 %all_to_all.30 = bf16[8,64,384]{2,1,0:T(8,128)(2,1)S(1)} all-to-all(bf16[8,64,384]{2,1,0:T(8,128)(2,1)S(1)} %shard_map.84), channel_id=1, replica_groups=mesh['zh'=2,'zl'=4,'y'=4,'core'=2,'section'=2,'tp'=4] {'zl','core'}, dimensions={0} | all-to-all | bytes 786432 | tf_op jit(solution)/shard_map/all_to_all | solution.py:274
  72.9 5.0 %collective-permute-start.2 = (bf16[128,512]{1,0:T(8,128)(2,1)S(1)}, bf16[128,512]{1,0:T(8,128)(2,1)S(1)}, u32[]{:S(2)}, u32[]{:S(2)}) collective-permute-start(bf16[128,512]{1,0:T(8,128)(2,1)S(1)} %shard_map.83), channel_id=1, source_target_pairs={{0,4},{4,0},{1,5},{5,1},{2,6},{6,2},{3,7},{7,3},{8,12},{12,8},{9,1... | collective-permute-start | bytes 393224 | tf_op jit(solution)/shard_map/ppermute | solution.py:26
  77.9 11.4 %all-gather.1 = bf16[512,512]{1,0:T(8,128)(2,1)S(1)} all-gather(bf16[128,512]{1,0:T(8,128)(2,1)S(1)} %shard_map.83), channel_id=3, replica_groups=mesh['zh'=2,'zl'=4,'y'=4,'core'=2,'section'=2,'tp'=4] {'tp'}, dimensions={0}, use_global_device_ids=true | all-gather | bytes 655360 | tf_op jit(solution)/shard_map/all_gather | solution.py:277
  89.3 3.1 %collective-permute-done.2 = bf16[128,512]{1,0:T(8,128)(2,1)S(1)} collective-permute-done((bf16[128,512]{1,0:T(8,128)(2,1)S(1)}, bf16[128,512]{1,0:T(8,128)(2,1)S(1)}, u32[]{:S(2)}, u32[]{:S(2)}) %collective-permute-start.2) | collective-permute-done | bytes 131104 | tf_op jit(solution)/shard_map/ppermute | solution.py:26
  93.2 3.5 %all-to-all-start.1 = ((bf16[4,128,512]{2,1,0:T(8,128)(2,1)}), bf16[4,128,512]{2,1,0:T(8,128)(2,1)S(1)}, u32[]{:S(2)}, u32[]{:S(2)}) async-start(bf16[4,128,512]{2,1,0:T(8,128)(2,1)} %broadcast_in_dim.4), calls=%async_computation.1 | async-start | bytes 1048576 | tf_op jit(solution)/shard_map/all_to_all | solution.py:30
  96.8 2.7 %collective-permute-start.3 = (bf16[4,128,512]{2,1,0:T(8,128)(2,1)S(1)}, bf16[4,128,512]{2,1,0:T(8,128)(2,1)S(1)}, u32[]{:S(2)}, u32[]{:S(2)}) collective-permute-start(bf16[4,128,512]{2,1,0:T(8,128)(2,1)S(1)} %bitcast.15), channel_id=1, source_target_pairs={{0,8},{8,0},{1,9},{9,1},{2,10},{10,2},{3,11},{11,3},{4,12},{12,4},... | collective-permute-start | bytes 1572872 | tf_op jit(solution)/shard_map/ppermute | solution.py:26
  99.5 5.9 %all-to-all-done.1.own_b = bf16[4,128,512]{2,1,0:T(8,128)(2,1)S(1)} async-done(((bf16[4,128,512]{2,1,0:T(8,128)(2,1)}), bf16[4,128,512]{2,1,0:T(8,128)(2,1)S(1)}, u32[]{:S(2)}, u32[]{:S(2)}) %all-to-all-start.1) | async-done | bytes 524320 | tf_op jit(solution)/shard_map/all_to_all | solution.py:30
  105.4 3.6 %collective-permute-start.4 = (bf16[4,128,512]{2,1,0:T(8,128)(2,1)S(1)}, bf16[4,128,512]{2,1,0:T(8,128)(2,1)S(1)}, u32[]{:S(2)}, u32[]{:S(2)}) collective-permute-start(bf16[4,128,512]{2,1,0:T(8,128)(2,1)S(1)} %all-to-all-done.1.own_b), channel_id=1, source_target_pairs={{0,8},{8,0},{1,9},{9,1},{2,10},{10,2},{3,11},{11,3},{4,12},{12,4},... | collective-permute-start | bytes 1572872 | tf_op jit(solution)/shard_map/ppermute | solution.py:26
  110.6 3.5 %all-gather.6.cloned.1.call-done = bf16[8,8,64,384]{3,2,1,0:T(8,128)(2,1)} async-done(((bf16[2,8,64,384]{3,2,1,0:T(8,128)(2,1)}), bf16[8,8,64,384]{3,2,1,0:T(8,128)(2,1)}) %all-gather.6.cloned.1.call-update) | async-done | bytes 3145744 | tf_op jit(solution)/shard_map/all_gather | solution.py:275
  114.0 4.0 %shard_map.85 = (bf16[256,128]{1,0:T(8,128)(2,1)S(1)}, bf16[256,256]{1,0:T(8,128)(2,1)S(1)}, bf16[4,256,256]{2,1,0:T(8,128)(2,1)}) custom-call(s32[1]{0:T(128)} %bitcast.4.flip, bf16[4,128,512]{2,1,0:T(8,128)(2,1)S(1)} %bitcast.16, bf16[4,128,512]{2,1,0:T(8,128)(2,1)S(1)} %all-to-all-done.1.own_b, bf16[4,128,512]{2,1,0:T(8,128)(2,1)S(1)} %collective-permute-done.3.other_a, ...), custom_call_target="tpu_custom_call" | custom-call | flops 805306368 | bytes 6291456 | tf_op jit(solution)/shard_map/pallas_call | solution.py:282
  118.0 4.5 %all-to-all-start.3 = ((bf16[4,256,256]{2,1,0:T(8,128)(2,1)}), bf16[4,256,256]{2,1,0:T(8,128)(2,1)S(1)}, u32[]{:S(2)}, u32[]{:S(2)}) async-start(bf16[4,256,256]{2,1,0:T(8,128)(2,1)} %get-tuple-element.27), calls=%async_computation.3 | async-start | bytes 1048576 | tf_op jit(solution)/shard_map/all_to_all | solution.py:312
  122.5 7.4 %collective-permute-start.5 = (bf16[256,256]{1,0:T(8,128)(2,1)S(1)}, bf16[256,256]{1,0:T(8,128)(2,1)S(1)}, u32[]{:S(2)}, u32[]{:S(2)}) collective-permute-start(bf16[256,256]{1,0:T(8,128)(2,1)S(1)} %get-tuple-element.28), channel_id=1, source_target_pairs={{0,256},{256,0},{1,257},{257,1},{2,258},{258,2},{3,259},{259,3},{4... | collective-permute-start | bytes 393224 | tf_op jit(solution)/shard_map/ppermute | solution.py:26
  129.9 9.7 %all-gather.3 = bf16[1024,128]{1,0:T(8,128)(2,1)S(1)} all-gather(bf16[256,128]{1,0:T(8,128)(2,1)S(1)} %get-tuple-element.29), channel_id=5, replica_groups=mesh['zh'=2,'zl'=4,'y'=4,'core'=2,'section'=2,'tp'=4] {'y'}, dimensions={0}, use_global_device_ids=true | all-gather | bytes 327680 | tf_op jit(solution)/shard_map/all_gather | solution.py:313
  139.6 2.6 %all-to-all-done.3.kv = bf16[4,256,256]{2,1,0:T(8,128)(2,1)S(1)} async-done(((bf16[4,256,256]{2,1,0:T(8,128)(2,1)}), bf16[4,256,256]{2,1,0:T(8,128)(2,1)S(1)}, u32[]{:S(2)}, u32[]{:S(2)}) %all-to-all-start.3) | async-done | bytes 524320 | tf_op jit(solution)/shard_map/all_to_all | solution.py:312
  143.0 6.7 %all-to-all-start.4 = ((bf16[4,256,256]{2,1,0:T(8,128)(2,1)}), bf16[4,256,256]{2,1,0:T(8,128)(2,1)S(1)}, u32[]{:S(2)}, u32[]{:S(2)}) async-start(bf16[4,256,256]{2,1,0:T(8,128)(2,1)} %broadcast_in_dim.5), calls=%async_computation.4 | async-start | bytes 1048576 | tf_op jit(solution)/shard_map/all_to_all | solution.py:30
  149.8 3.0 %shard_map.86 = (f32[4,256,128]{2,1,0:T(8,128)S(1)}, f32[4,256,128]{2,1,0:T(8,128)S(1)}) custom-call(s32[4]{0:T(128)S(1)} %pad_add_fusion.place, bf16[4,256,128]{2,1,0:T(8,128)(2,1)S(1)} %bitcast.17, bf16[4,256,256]{2,1,0:T(8,128)(2,1)S(1)} %all-to-all-done.3.kv), custom_call_target="tpu_custom_call" | custom-call | flops 536870912 | bytes 2097152 | tf_op jit(solution)/shard_map/pallas_call | solution.py:319
  152.8 10.9 %all-to-all-done.4.kv = bf16[4,256,256]{2,1,0:T(8,128)(2,1)S(1)} async-done(((bf16[4,256,256]{2,1,0:T(8,128)(2,1)}), bf16[4,256,256]{2,1,0:T(8,128)(2,1)S(1)}, u32[]{:S(2)}, u32[]{:S(2)}) %all-to-all-start.4) | async-done | bytes 524320 | tf_op jit(solution)/shard_map/all_to_all | solution.py:30
  164.7 11.7 %all_to_all.31.parts = bf16[8,136,128]{2,1,0:T(8,128)(2,1)S(1)} all-to-all(bf16[8,136,128]{2,1,0:T(8,128)(2,1)S(1)} %shard_map.87), channel_id=1, replica_groups=mesh['zh'=2,'zl'=4,'y'=4,'core'=2,'section'=2,'tp'=4] {'y','core'}, dimensions={0} | all-to-all | bytes 557056 | tf_op jit(solution)/shard_map/all_to_all | solution.py:327
  (30 shorter events, 10.6 us)
Async XLA Ops:
  8.2 41.2 %all-to-all-start = ((bf16[8,64,384]{2,1,0:T(8,128)(2,1)}), bf16[8,64,384]{2,1,0:T(8,128)(2,1)S(1)}, u32[]{:S(2)}, u32[]{:S(2)}) async-start(bf16[8,64,384]{2,1,0:T(8,128)(2,1)} %get-tuple-element.20), calls=%async_computation | async-start | bytes 786432 | tf_op jit(solution)/shard_map/all_to_all | solution.py:266
  18.4 95.6 %all-gather.6.cloned.1.call-start = ((), (), s32[]{:S(2)}) async-start(), calls=%async_computation.6 | async-start | bytes 3932160 | tf_op jit(solution)/shard_map/all_gather | solution.py:275
  18.4 16.4 %collective-permute-start.1 = (bf16[128,128]{1,0:T(8,128)(2,1)}, bf16[128,128]{1,0:T(8,128)(2,1)S(1)}, u32[]{:S(2)}, u32[]{:S(2)}) collective-permute-start(bf16[128,128]{1,0:T(8,128)(2,1)} %param.9), channel_id=1, source_target_pairs={{0,4},{4,0},{1,5},{5,1},{2,6},{6,2},{3,7},{7,3},{8,12},{12,8},{9,1... | collective-permute-start | bytes 98312 | tf_op jit(solution)/shard_map/ppermute | solution.py:26
  28.5 20.9 %collective-permute-start = (bf16[64,768]{1,0:T(8,128)(2,1)}, bf16[64,768]{1,0:T(8,128)(2,1)S(1)}, u32[]{:S(2)}, u32[]{:S(2)}) collective-permute-start(bf16[64,768]{1,0:T(8,128)(2,1)} %get-tuple-element.21), channel_id=1, source_target_pairs={{0,256},{256,0},{1,257},{257,1},{2,258},{258,2},{3,259},{259,3},{4... | collective-permute-start | bytes 294920 | tf_op jit(solution)/shard_map/ppermute | solution.py:26
  46.2 1.2 copy-start
  47.5 0.9 copy-start.1
  49.3 47.4 %copy-start.2 = (bf16[4096]{0:T(1024)(128)(2,1)S(1)}, bf16[4096]{0:T(1024)(128)(2,1)}, u32[]{:S(2)}) copy-start(bf16[4096]{0:T(1024)(128)(2,1)} %param.12) | copy-start | bytes 24580
  72.9 19.5 %collective-permute-start.2 = (bf16[128,512]{1,0:T(8,128)(2,1)S(1)}, bf16[128,512]{1,0:T(8,128)(2,1)S(1)}, u32[]{:S(2)}, u32[]{:S(2)}) collective-permute-start(bf16[128,512]{1,0:T(8,128)(2,1)S(1)} %shard_map.83), channel_id=1, source_target_pairs={{0,4},{4,0},{1,5},{5,1},{2,6},{6,2},{3,7},{7,3},{8,12},{12,8},{9,1... | collective-permute-start | bytes 393224 | tf_op jit(solution)/shard_map/ppermute | solution.py:26
  93.2 12.2 %all-to-all-start.1 = ((bf16[4,128,512]{2,1,0:T(8,128)(2,1)}), bf16[4,128,512]{2,1,0:T(8,128)(2,1)S(1)}, u32[]{:S(2)}, u32[]{:S(2)}) async-start(bf16[4,128,512]{2,1,0:T(8,128)(2,1)} %broadcast_in_dim.4), calls=%async_computation.1 | async-start | bytes 1048576 | tf_op jit(solution)/shard_map/all_to_all | solution.py:30
  96.8 13.0 %collective-permute-start.3 = (bf16[4,128,512]{2,1,0:T(8,128)(2,1)S(1)}, bf16[4,128,512]{2,1,0:T(8,128)(2,1)S(1)}, u32[]{:S(2)}, u32[]{:S(2)}) collective-permute-start(bf16[4,128,512]{2,1,0:T(8,128)(2,1)S(1)} %bitcast.15), channel_id=1, source_target_pairs={{0,8},{8,0},{1,9},{9,1},{2,10},{10,2},{3,11},{11,3},{4,12},{12,4},... | collective-permute-start | bytes 1572872 | tf_op jit(solution)/shard_map/ppermute | solution.py:26
  105.4 5.1 %collective-permute-start.4 = (bf16[4,128,512]{2,1,0:T(8,128)(2,1)S(1)}, bf16[4,128,512]{2,1,0:T(8,128)(2,1)S(1)}, u32[]{:S(2)}, u32[]{:S(2)}) collective-permute-start(bf16[4,128,512]{2,1,0:T(8,128)(2,1)S(1)} %all-to-all-done.1.own_b), channel_id=1, source_target_pairs={{0,8},{8,0},{1,9},{9,1},{2,10},{10,2},{3,11},{11,3},{4,12},{12,4},... | collective-permute-start | bytes 1572872 | tf_op jit(solution)/shard_map/ppermute | solution.py:26
  118.0 24.1 %all-to-all-start.3 = ((bf16[4,256,256]{2,1,0:T(8,128)(2,1)}), bf16[4,256,256]{2,1,0:T(8,128)(2,1)S(1)}, u32[]{:S(2)}, u32[]{:S(2)}) async-start(bf16[4,256,256]{2,1,0:T(8,128)(2,1)} %get-tuple-element.27), calls=%async_computation.3 | async-start | bytes 1048576 | tf_op jit(solution)/shard_map/all_to_all | solution.py:312
  122.5 17.0 %collective-permute-start.5 = (bf16[256,256]{1,0:T(8,128)(2,1)S(1)}, bf16[256,256]{1,0:T(8,128)(2,1)S(1)}, u32[]{:S(2)}, u32[]{:S(2)}) collective-permute-start(bf16[256,256]{1,0:T(8,128)(2,1)S(1)} %get-tuple-element.28), channel_id=1, source_target_pairs={{0,256},{256,0},{1,257},{257,1},{2,258},{258,2},{3,259},{259,3},{4... | collective-permute-start | bytes 393224 | tf_op jit(solution)/shard_map/ppermute | solution.py:26
  143.0 20.7 %all-to-all-start.4 = ((bf16[4,256,256]{2,1,0:T(8,128)(2,1)}), bf16[4,256,256]{2,1,0:T(8,128)(2,1)S(1)}, u32[]{:S(2)}, u32[]{:S(2)}) async-start(bf16[4,256,256]{2,1,0:T(8,128)(2,1)} %broadcast_in_dim.5), calls=%async_computation.4 | async-start | bytes 1048576 | tf_op jit(solution)/shard_map/all_to_all | solution.py:30
Sparse Core Ops, SparseCore 0:
  73.0 40.9 all-gather.5

commit v6 on v3

--- a/solution.py
+++ b/solution.py
@@ -102,14 +102,6 @@
     return jnp.concatenate([coded[:, :ROWS], coded[:, ROWS:]], axis=0).astype(jnp.bfloat16)
 
 
-def decode(coded):
-    shape = (ROWS, ROWS)
-    eye = lax.broadcasted_iota(jnp.int32, shape, 0) == lax.broadcasted_iota(jnp.int32, shape, 1)
-    eye = eye.astype(jnp.float32).astype(jnp.bfloat16)
-    c = lax.dot_general(eye, coded, (((1,), (1,)), ((), ())), preferred_element_type=jnp.float32)
-    return c[:, 0:1] + c[:, 1:2] + c[:, 2:3]
-
-
 def attend(q, kv, scores, mask):
     shape = (CHIP_ROWS, CHIP_ROWS)
     scale = 1.0 / math.sqrt(HD)
@@ -173,32 +165,33 @@
 
     @pl.when(place[0] != 0)
     def _():
-        def one(pair, carry):
-            for i in range(2):
-                y = pair * 2 + i
-                part, level = attend(queries[y], kv, scores.at[i], lambda l, s: s)
-                before = levels[y, :, 0:1]
-                top = jnp.maximum(level, before)
-                new, old = jnp.exp(level - top), jnp.exp(before - top)
-                total = new + old
-                put(y, (part * new + parts[y] * old) / total, top + jnp.log(total))
-            return carry
-
-        lax.fori_loop(0, Y // 2, one, 0)
+        for y in range(Y):
+            part, level = attend(queries[y], kv, scores.at[y], lambda l, s: s)
+            before = levels[y, :, 0:1]
+            top = jnp.maximum(level, before)
+            new, old = jnp.exp(level - top), jnp.exp(before - top)
+            total = new + old
+            put(y, (part * new + parts[y] * old) / total, top + jnp.log(total))
 
 
 def merge_kernel(parts, out):
+    shares = []
     for h in range(CORES):
-        blocks = [parts[y * CORES + h] for y in range(Y)]
-        levels = [decode(block[ROWS:, :]) for block in blocks]
-        top = jnp.maximum(jnp.maximum(levels[0], levels[1]), jnp.maximum(levels[2], levels[3]))
-        total = jnp.zeros_like(top)
+        levels = []
+        for y in range(Y):
+            coded = parts[y * CORES + h, ROWS:, :].astype(jnp.float32)
+            levels.append(coded[0:1] + coded[1:2] + coded[2:3])
+        levels = jnp.concatenate(levels, axis=0)
+        share = jnp.exp(levels - jnp.max(levels, axis=0, keepdims=True))
+        shares.append(share / jnp.sum(share, axis=0, keepdims=True))
+    shares = jnp.transpose(jnp.concatenate(shares * (ROWS // (CORES * Y)), axis=0))
+    for h in range(CORES):
         result = jnp.zeros((ROWS, HD), jnp.float32)
-        for level, block in zip(levels, blocks):
-            share = jnp.exp(level - top)
-            total = total + share
-            result = result + share * block[:ROWS, :].astype(jnp.float32)
-        out[:, h * HD : (h + 1) * HD] = (result / total).astype(jnp.bfloat16)
+        for y in range(Y):
+            lane = h * Y + y
+            block = parts[y * CORES + h, :ROWS, :].astype(jnp.float32)
+            result = result + shares[:, lane : lane + 1] * block
+        out[:, h * HD : (h + 1) * HD] = result.astype(jnp.bfloat16)
 
 
 def join_kernel(q, k, v, out, sems):
@@ -279,7 +272,7 @@
     own_a = lax.all_gather(joined, "tp", axis=0)
     own_a, joined_b = lax.optimization_barrier((own_a, joined_b))
     other_a = swap(own_a, "core")
-    own_b = gather(joined_b, "tp", TP)
+    own_b = lax.all_gather(joined_b, "tp", axis=0)
     other_b = swap(own_b, "core")
     queries, kv, lines = pl.pallas_call(
         project_kernel,
@@ -315,7 +308,7 @@
     queries = lax.all_gather(queries, "y", axis=0)
     kv_a, kv_b, queries = lax.optimization_barrier((kv_a, kv_b, queries))
     place = jnp.stack([zh, zl, y, core])
-    scores = [pltpu.VMEM((2, ZL, CHIP_ROWS, CHIP_ROWS), jnp.float32)]
+    scores = [pltpu.VMEM((Y, ZL, CHIP_ROWS, CHIP_ROWS), jnp.float32)]
     state = [jax.ShapeDtypeStruct((Y, CHIP_ROWS, HD), jnp.float32)] * 2
     flops = 4 * 1024 * 1024 * HD
     parts, levels = call(attend_own_kernel, state, 1, 2, flops, 2 << 20, scores)(

time: 178 us -> 178 us (level)
  blocking collectives: 43.1 us -> 56.2 us
  starting transfers between devices: 67.1 us -> 60.2 us
  waiting for transfers between devices: 34.7 us -> 29.1 us
    all_gather x0 -> x1, blocking collectives: none -> 13 us  [local(): own_b = lax.all_gather(joined_b, 'tp', axis=0)]
    all_to_all x2 -> x1, starting transfers between devices: 12.4 us -> 5.92 us  [gather(): lax.all_to_all(jnp.broadcast_to(v[None], (n, *v.shape)), axis, 0, 0, tile...]
    all_to_all x2 -> x1, waiting for transfers between devices: 16.8 us -> 10.9 us  [gather(): lax.all_to_all(jnp.broadcast_to(v[None], (n, *v.shape)), axis, 0, 0, tile...]
  transfers between devices with their start and end apart: 11 -> 10, of which waited for: 8 -> 7; matrix products, arithmetic and copies ran while one was open for 1% -> 1% of each run, Pallas kernels for 2% -> 2%
where the time goes in v6:
time: 178 us; the launch traced here: 177 us
  starting transfers between devices  60.2 us (34%)
  blocking collectives  56.2 us (32%)
  waiting for transfers between devices  29.1 us (16%)
  between operations  14.2 us (8%)
  Pallas kernels  12.3 us (7%)
  local copies, waits for them, and re-layouts  3.55 us (2%)
    ppermute x6, starting transfers between devices, swap(): return lax.ppermute(v, axis, SWAP)  36.3 us
    all_gather x1, blocking collectives, local(): own_b = lax.all_gather(joined_b, 'tp', axis=0)  13 us
    all_to_all x1, starting transfers between devices, local(): weight = lax.all_to_all(weight, ('zl', 'core'), 0, 0, tiled=True)  12.8 us
    all_to_all x1, blocking collectives, local(): parts = lax.all_to_all(parts, ('y', 'core'), 0, 0, tiled=True)  11.7 us
    all_gather x1, blocking collectives, local(): own_a = lax.all_gather(joined, 'tp', axis=0)  11.6 us
    all_to_all x1, waiting for transfers between devices, gather(): lax.all_to_all(jnp.broadcast_to(v[None], (n, *v.shape)), axis, 0, 0, tile...  10.9 us
    all_gather x1, blocking collectives, local(): feats = lax.all_gather(jnp.stack([feats, feats_b]), 'tp', axis=0)  10.1 us
    all_gather x1, blocking collectives, local(): queries = lax.all_gather(queries, 'y', axis=0)  9.8 us
  transfers between devices with their start and end apart: 10, of which 7 were waited for; matrix products, arithmetic and copies ran while one was open for 1% of the time, Pallas kernels for 2%

profile of v6, /device:TPU:1, one launch (start us, length us, event | category | flops | bytes accessed | tf_op | source)
XLA Modules:
  0.0 177.2 jit_solution(7382632931142998619)
XLA Ops:
  6.5 1.5 shard_map.82.own
  8.1 9.6 %collective-permute-start = (bf16[64,768]{1,0:T(8,128)(2,1)}, bf16[64,768]{1,0:T(8,128)(2,1)S(1)}, u32[]{:S(2)}, u32[]{:S(2)}) collective-permute-start(bf16[64,768]{1,0:T(8,128)(2,1)} %shard_map.82.own), channel_id=1, source_target_pairs={{0,256},{256,0},{1,257},{257,1},{2,258},{258,2},{3,259},{259,3},{4... | collective-permute-start | bytes 294920 | tf_op jit(solution)/shard_map/ppermute | solution.py:26
  17.7 10.6 %collective-permute-start.1 = (bf16[128,128]{1,0:T(8,128)(2,1)}, bf16[128,128]{1,0:T(8,128)(2,1)S(1)}, u32[]{:S(2)}, u32[]{:S(2)}) collective-permute-start(bf16[128,128]{1,0:T(8,128)(2,1)} %param.9), channel_id=1, source_target_pairs={{0,4},{4,0},{1,5},{5,1},{2,6},{6,2},{3,7},{7,3},{8,12},{12,8},{9,1... | collective-permute-start | bytes 98312 | tf_op jit(solution)/shard_map/ppermute | solution.py:26
  28.4 3.2 %collective-permute-done.1 = bf16[128,128]{1,0:T(8,128)(2,1)S(1)} collective-permute-done((bf16[128,128]{1,0:T(8,128)(2,1)}, bf16[128,128]{1,0:T(8,128)(2,1)S(1)}, u32[]{:S(2)}, u32[]{:S(2)}) %collective-permute-start.1) | collective-permute-done | bytes 32800 | tf_op jit(solution)/shard_map/ppermute | solution.py:26
  33.5 12.8 %all-to-all-start = ((bf16[8,2,64,384]{3,2,1,0:T(8,128)(2,1)}), bf16[8,2,64,384]{3,2,1,0:T(8,128)(2,1)S(1)}, u32[]{:S(2)}, u32[]{:S(2)}) async-start(bf16[8,2,64,384]{3,2,1,0:T(8,128)(2,1)} %shard_map.83), calls=%async_computation | async-start | bytes 1572864 | tf_op jit(solution)/shard_map/all_to_all | solution.py:262
  47.7 10.1 %all-gather = bf16[8,128,128]{2,1,0:T(8,128)(2,1)S(1)} all-gather(bf16[2,128,128]{2,1,0:T(8,128)(2,1)S(1)} %pad_maximum_fusion.2), channel_id=2, replica_groups=mesh['zh'=2,'zl'=4,'y'=4,'core'=2,'section'=2,'tp'=4] {'tp'}, dimensions={0}, use_global_device_ids=true | all-gather | bytes 327680 | tf_op jit(solution)/shard_map/all_gather | solution.py:264
  59.7 6.6 %all-to-all-done = bf16[8,2,64,384]{3,2,1,0:T(8,128)(2,1)S(1)} async-done(((bf16[8,2,64,384]{3,2,1,0:T(8,128)(2,1)}), bf16[8,2,64,384]{3,2,1,0:T(8,128)(2,1)S(1)}, u32[]{:S(2)}, u32[]{:S(2)}) %all-to-all-start) | async-done | bytes 786464 | tf_op jit(solution)/shard_map/all_to_all | solution.py:262
  67.3 3.2 %collective-permute-start.2 = (bf16[128,512]{1,0:T(8,128)(2,1)S(1)}, bf16[128,512]{1,0:T(8,128)(2,1)S(1)}, u32[]{:S(2)}, u32[]{:S(2)}) collective-permute-start(bf16[128,512]{1,0:T(8,128)(2,1)S(1)} %shard_map.84), channel_id=1, source_target_pairs={{0,4},{4,0},{1,5},{5,1},{2,6},{6,2},{3,7},{7,3},{8,12},{12,8},{9,1... | collective-permute-start | bytes 393224 | tf_op jit(solution)/shard_map/ppermute | solution.py:26
  70.6 11.6 %all-gather.1 = bf16[512,512]{1,0:T(8,128)(2,1)S(1)} all-gather(bf16[128,512]{1,0:T(8,128)(2,1)S(1)} %shard_map.84), channel_id=3, replica_groups=mesh['zh'=2,'zl'=4,'y'=4,'core'=2,'section'=2,'tp'=4] {'tp'}, dimensions={0}, use_global_device_ids=true | all-gather | bytes 655360 | tf_op jit(solution)/shard_map/all_gather | solution.py:272
  82.1 3.4 %collective-permute-done.2 = bf16[128,512]{1,0:T(8,128)(2,1)S(1)} collective-permute-done((bf16[128,512]{1,0:T(8,128)(2,1)S(1)}, bf16[128,512]{1,0:T(8,128)(2,1)S(1)}, u32[]{:S(2)}, u32[]{:S(2)}) %collective-permute-start.2) | collective-permute-done | bytes 131104 | tf_op jit(solution)/shard_map/ppermute | solution.py:26
  85.5 13.0 %all-gather.2 = bf16[512,512]{1,0:T(8,128)(2,1)S(1)} all-gather(bf16[128,512]{1,0:T(8,128)(2,1)S(1)} %collective-permute-done.2), channel_id=4, replica_groups=mesh['zh'=2,'zl'=4,'y'=4,'core'=2,'section'=2,'tp'=4] {'tp'}, dimensions={0}, use_global_device_ids=true | all-gather | bytes 655360 | tf_op jit(solution)/shard_map/all_gather | solution.py:275
  98.6 4.2 %collective-permute-start.4 = (bf16[4,128,512]{2,1,0:T(8,128)(2,1)S(1)}, bf16[4,128,512]{2,1,0:T(8,128)(2,1)S(1)}, u32[]{:S(2)}, u32[]{:S(2)}) collective-permute-start(bf16[4,128,512]{2,1,0:T(8,128)(2,1)S(1)} %bitcast.16), channel_id=1, source_target_pairs={{0,8},{8,0},{1,9},{9,1},{2,10},{10,2},{3,11},{11,3},{4,12},{12,4},... | collective-permute-start | bytes 1572872 | tf_op jit(solution)/shard_map/ppermute | solution.py:26
  102.8 1.9 %collective-permute-start.3 = (bf16[4,128,512]{2,1,0:T(8,128)(2,1)S(1)}, bf16[4,128,512]{2,1,0:T(8,128)(2,1)S(1)}, u32[]{:S(2)}, u32[]{:S(2)}) collective-permute-start(bf16[4,128,512]{2,1,0:T(8,128)(2,1)S(1)} %bitcast.14), channel_id=1, source_target_pairs={{0,8},{8,0},{1,9},{9,1},{2,10},{10,2},{3,11},{11,3},{4,12},{12,4},... | collective-permute-start | bytes 1572872 | tf_op jit(solution)/shard_map/ppermute | solution.py:26
  105.4 1.2 collective-permute-done.3.other_a
  107.1 3.9 %shard_map.85 = (bf16[256,128]{1,0:T(8,128)(2,1)S(1)}, bf16[256,256]{1,0:T(8,128)(2,1)S(1)}, bf16[4,256,256]{2,1,0:T(8,128)(2,1)}) custom-call(s32[1]{0:T(128)} %bitcast.4.flip, bf16[4,128,512]{2,1,0:T(8,128)(2,1)S(1)} %bitcast.15, bf16[4,128,512]{2,1,0:T(8,128)(2,1)S(1)} %bitcast.17, bf16[4,128,512]{2,1,0:T(8,128)(2,1)S(1)} %collective-permute-done.3.other_a, ...), custom_call_target="tpu_custom_call" | custom-call | flops 805306368 | bytes 6291456 | tf_op jit(solution)/shard_map/pallas_call | solution.py:277
  111.0 5.2 %all-to-all-start.1 = ((bf16[4,256,256]{2,1,0:T(8,128)(2,1)}), bf16[4,256,256]{2,1,0:T(8,128)(2,1)S(1)}, u32[]{:S(2)}, u32[]{:S(2)}) async-start(bf16[4,256,256]{2,1,0:T(8,128)(2,1)} %get-tuple-element.25), calls=%async_computation.1 | async-start | bytes 1048576 | tf_op jit(solution)/shard_map/all_to_all | solution.py:307
  116.2 6.7 %collective-permute-start.5 = (bf16[256,256]{1,0:T(8,128)(2,1)S(1)}, bf16[256,256]{1,0:T(8,128)(2,1)S(1)}, u32[]{:S(2)}, u32[]{:S(2)}) collective-permute-start(bf16[256,256]{1,0:T(8,128)(2,1)S(1)} %get-tuple-element.26), channel_id=1, source_target_pairs={{0,256},{256,0},{1,257},{257,1},{2,258},{258,2},{3,259},{259,3},{4... | collective-permute-start | bytes 393224 | tf_op jit(solution)/shard_map/ppermute | solution.py:26
  122.9 9.8 %all-gather.4 = bf16[1024,128]{1,0:T(8,128)(2,1)S(1)} all-gather(bf16[256,128]{1,0:T(8,128)(2,1)S(1)} %get-tuple-element.27), channel_id=6, replica_groups=mesh['zh'=2,'zl'=4,'y'=4,'core'=2,'section'=2,'tp'=4] {'y'}, dimensions={0}, use_global_device_ids=true | all-gather | bytes 327680 | tf_op jit(solution)/shard_map/all_gather | solution.py:308
  132.7 3.3 %all-to-all-done.1.kv = bf16[4,256,256]{2,1,0:T(8,128)(2,1)S(1)} async-done(((bf16[4,256,256]{2,1,0:T(8,128)(2,1)}), bf16[4,256,256]{2,1,0:T(8,128)(2,1)S(1)}, u32[]{:S(2)}, u32[]{:S(2)}) %all-to-all-start.1) | async-done | bytes 524320 | tf_op jit(solution)/shard_map/all_to_all | solution.py:307
  136.8 5.9 %all-to-all-start.2 = ((bf16[4,256,256]{2,1,0:T(8,128)(2,1)}), bf16[4,256,256]{2,1,0:T(8,128)(2,1)S(1)}, u32[]{:S(2)}, u32[]{:S(2)}) async-start(bf16[4,256,256]{2,1,0:T(8,128)(2,1)} %broadcast_in_dim.2), calls=%async_computation.2 | async-start | bytes 1048576 | tf_op jit(solution)/shard_map/all_to_all | solution.py:30
  142.8 3.0 %shard_map.86 = (f32[4,256,128]{2,1,0:T(8,128)S(1)}, f32[4,256,128]{2,1,0:T(8,128)S(1)}) custom-call(s32[4]{0:T(128)S(1)} %pad_add_fusion.place, bf16[4,256,128]{2,1,0:T(8,128)(2,1)S(1)} %bitcast.18, bf16[4,256,256]{2,1,0:T(8,128)(2,1)S(1)} %all-to-all-done.1.kv), custom_call_target="tpu_custom_call" | custom-call | flops 536870912 | bytes 2097152 | tf_op jit(solution)/shard_map/pallas_call | solution.py:314
  145.8 10.9 %all-to-all-done.2.kv = bf16[4,256,256]{2,1,0:T(8,128)(2,1)S(1)} async-done(((bf16[4,256,256]{2,1,0:T(8,128)(2,1)}), bf16[4,256,256]{2,1,0:T(8,128)(2,1)S(1)}, u32[]{:S(2)}, u32[]{:S(2)}) %all-to-all-start.2) | async-done | bytes 524320 | tf_op jit(solution)/shard_map/all_to_all | solution.py:30
  157.7 11.7 %all_to_all.20.parts = bf16[8,136,128]{2,1,0:T(8,128)(2,1)S(1)} all-to-all(bf16[8,136,128]{2,1,0:T(8,128)(2,1)S(1)} %shard_map.87), channel_id=1, replica_groups=mesh['zh'=2,'zl'=4,'y'=4,'core'=2,'section'=2,'tp'=4] {'y','core'}, dimensions={0} | all-to-all | bytes 557056 | tf_op jit(solution)/shard_map/all_to_all | solution.py:322
  169.3 1.0 shard_map.88
  (30 shorter events, 8.6 us)
Async XLA Ops:
  6.5 51.3 %copy-start = (bf16[1024,512]{1,0:T(8,128)(2,1)S(1)}, bf16[1024,512]{1,0:T(8,128)(2,1)}, u32[]{:S(2)}) copy-start(bf16[1024,512]{1,0:T(8,128)(2,1)} %param.11) | copy-start | bytes 3145732
  8.1 23.5 %collective-permute-start = (bf16[64,768]{1,0:T(8,128)(2,1)}, bf16[64,768]{1,0:T(8,128)(2,1)S(1)}, u32[]{:S(2)}, u32[]{:S(2)}) collective-permute-start(bf16[64,768]{1,0:T(8,128)(2,1)} %shard_map.82.own), channel_id=1, source_target_pairs={{0,256},{256,0},{1,257},{257,1},{2,258},{258,2},{3,259},{259,3},{4... | collective-permute-start | bytes 294920 | tf_op jit(solution)/shard_map/ppermute | solution.py:26
  17.7 13.8 %collective-permute-start.1 = (bf16[128,128]{1,0:T(8,128)(2,1)}, bf16[128,128]{1,0:T(8,128)(2,1)S(1)}, u32[]{:S(2)}, u32[]{:S(2)}) collective-permute-start(bf16[128,128]{1,0:T(8,128)(2,1)} %param.9), channel_id=1, source_target_pairs={{0,4},{4,0},{1,5},{5,1},{2,6},{6,2},{3,7},{7,3},{8,12},{12,8},{9,1... | collective-permute-start | bytes 98312 | tf_op jit(solution)/shard_map/ppermute | solution.py:26
  31.6 0.9 copy-start.1
  32.5 34.8 %copy-start.4 = (bf16[4096]{0:T(1024)(128)(2,1)S(1)}, bf16[4096]{0:T(1024)(128)(2,1)}, u32[]{:S(2)}) copy-start(bf16[4096]{0:T(1024)(128)(2,1)} %param.12) | copy-start | bytes 24580
  33.5 32.9 %all-to-all-start = ((bf16[8,2,64,384]{3,2,1,0:T(8,128)(2,1)}), bf16[8,2,64,384]{3,2,1,0:T(8,128)(2,1)S(1)}, u32[]{:S(2)}, u32[]{:S(2)}) async-start(bf16[8,2,64,384]{3,2,1,0:T(8,128)(2,1)} %shard_map.83), calls=%async_computation | async-start | bytes 1572864 | tf_op jit(solution)/shard_map/all_to_all | solution.py:262
  46.2 60.8 %all-gather.7.cloned.1.call-start = ((), (), s32[]{:S(2)}) async-start(), calls=%async_computation.4 | async-start | bytes 3932160 | tf_op jit(solution)/shard_map/all_gather | solution.py:270
  57.9 0.9 copy-start.2
  66.3 0.9 copy-start.3
  67.3 18.2 %collective-permute-start.2 = (bf16[128,512]{1,0:T(8,128)(2,1)S(1)}, bf16[128,512]{1,0:T(8,128)(2,1)S(1)}, u32[]{:S(2)}, u32[]{:S(2)}) collective-permute-start(bf16[128,512]{1,0:T(8,128)(2,1)S(1)} %shard_map.84), channel_id=1, source_target_pairs={{0,4},{4,0},{1,5},{5,1},{2,6},{6,2},{3,7},{7,3},{8,12},{12,8},{9,1... | collective-permute-start | bytes 393224 | tf_op jit(solution)/shard_map/ppermute | solution.py:26
  98.6 6.8 %collective-permute-start.4 = (bf16[4,128,512]{2,1,0:T(8,128)(2,1)S(1)}, bf16[4,128,512]{2,1,0:T(8,128)(2,1)S(1)}, u32[]{:S(2)}, u32[]{:S(2)}) collective-permute-start(bf16[4,128,512]{2,1,0:T(8,128)(2,1)S(1)} %bitcast.16), channel_id=1, source_target_pairs={{0,8},{8,0},{1,9},{9,1},{2,10},{10,2},{3,11},{11,3},{4,12},{12,4},... | collective-permute-start | bytes 1572872 | tf_op jit(solution)/shard_map/ppermute | solution.py:26
  102.8 3.8 %collective-permute-start.3 = (bf16[4,128,512]{2,1,0:T(8,128)(2,1)S(1)}, bf16[4,128,512]{2,1,0:T(8,128)(2,1)S(1)}, u32[]{:S(2)}, u32[]{:S(2)}) collective-permute-start(bf16[4,128,512]{2,1,0:T(8,128)(2,1)S(1)} %bitcast.14), channel_id=1, source_target_pairs={{0,8},{8,0},{1,9},{9,1},{2,10},{10,2},{3,11},{11,3},{4,12},{12,4},... | collective-permute-start | bytes 1572872 | tf_op jit(solution)/shard_map/ppermute | solution.py:26
  111.0 25.0 %all-to-all-start.1 = ((bf16[4,256,256]{2,1,0:T(8,128)(2,1)}), bf16[4,256,256]{2,1,0:T(8,128)(2,1)S(1)}, u32[]{:S(2)}, u32[]{:S(2)}) async-start(bf16[4,256,256]{2,1,0:T(8,128)(2,1)} %get-tuple-element.25), calls=%async_computation.1 | async-start | bytes 1048576 | tf_op jit(solution)/shard_map/all_to_all | solution.py:307
  116.2 16.5 %collective-permute-start.5 = (bf16[256,256]{1,0:T(8,128)(2,1)S(1)}, bf16[256,256]{1,0:T(8,128)(2,1)S(1)}, u32[]{:S(2)}, u32[]{:S(2)}) collective-permute-start(bf16[256,256]{1,0:T(8,128)(2,1)S(1)} %get-tuple-element.26), channel_id=1, source_target_pairs={{0,256},{256,0},{1,257},{257,1},{2,258},{258,2},{3,259},{259,3},{4... | collective-permute-start | bytes 393224 | tf_op jit(solution)/shard_map/ppermute | solution.py:26
  136.8 19.9 %all-to-all-start.2 = ((bf16[4,256,256]{2,1,0:T(8,128)(2,1)}), bf16[4,256,256]{2,1,0:T(8,128)(2,1)S(1)}, u32[]{:S(2)}, u32[]{:S(2)}) async-start(bf16[4,256,256]{2,1,0:T(8,128)(2,1)} %broadcast_in_dim.2), calls=%async_computation.2 | async-start | bytes 1048576 | tf_op jit(solution)/shard_map/all_to_all | solution.py:30
Sparse Core Ops, SparseCore 0:
  67.4 39.6 all-gather.6

commit v7 on v6

--- a/solution.py
+++ b/solution.py
@@ -48,7 +48,9 @@
 ):
     copies = [
         pltpu.make_async_copy(
-            stored.at[:, t * CORES : (t + 1) * CORES], weight.at[:, t * CORES : (t + 1) * CORES], sem.at[t]
+            stored.at[:, :, t * CORES : (t + 1) * CORES],
+            weight.at[:, :, t * CORES : (t + 1) * CORES],
+            sem.at[t],
         )
         for t in range(TP)
     ]
@@ -69,7 +71,7 @@
         wide = jnp.concatenate([own[t], other[t]], axis=0).astype(jnp.float32)
         normed = (wide * inverse * gain[i : i + 1, :]).astype(jnp.bfloat16)
         block = jnp.concatenate(
-            [weight[y, t * CORES + c, half] for y in range(Y) for c in range(CORES)], axis=0
+            [weight[y, half, t * CORES + c] for y in range(Y) for c in range(CORES)], axis=0
         )
         total = total + jnp.dot(normed, block, preferred_element_type=jnp.float32)
     q = total[:, :HD]
@@ -194,24 +196,24 @@
         out[:, h * HD : (h + 1) * HD] = result.astype(jnp.bfloat16)
 
 
-def join_kernel(q, k, v, out, sems):
+def spread_kernel(w, out):
+    for h in range(CORES):
+        for i in range(3):
+            block = w[:, (2 * i + h) * HD : (2 * i + h + 1) * HD]
+            for l in range(ZL):
+                out[l * CORES + h, :, i * HD : (i + 1) * HD] = block
+
+
+def join_kernel(q, k, v, joined, out, sems):
     copies = [
-        pltpu.make_async_copy(w, out.at[:, i * 2 * HD : (i + 1) * 2 * HD], sems.at[i])
+        pltpu.make_async_copy(w, joined.at[:, i * 2 * HD : (i + 1) * 2 * HD], sems.at[i])
         for i, w in enumerate((q, k, v))
     ]
     for copy in copies:
         copy.start()
     for copy in copies:
         copy.wait()
-
-
-def spread_kernel(own, partner, out):
-    for h in range(CORES):
-        for zr, w in enumerate((own, partner)):
-            for i in range(3):
-                block = w[:, (2 * i + h) * HD : (2 * i + h + 1) * HD]
-                for l in range(ZL):
-                    out[l * CORES + h, zr, :, i * HD : (i + 1) * HD] = block
+    spread_kernel(joined, out)
 
 
 def call(kernel, outs, n_scalars, n_arrays, flops, size, scratch=()):
@@ -245,29 +247,27 @@
     gains = gain.astype(jnp.float32).reshape(SECTIONS, TP, 512)
     gains = jnp.where(section == 0, gains, gains[::-1]).reshape(8, 512)
     feats_b = swap(feats, "section")
-    weight = pl.pallas_call(
+    weight, spread = pl.pallas_call(
         join_kernel,
-        out_shape=shaped(64, 6 * HD),
+        out_shape=[shaped(64, 6 * HD), shaped(ZL * CORES, 64, 3 * HD)],
         in_specs=[pl.BlockSpec(memory_space=pl.ANY)] * 3,
-        out_specs=VMEM,
+        out_specs=[VMEM] * 2,
         scratch_shapes=[pltpu.SemaphoreType.DMA((3,))],
-        cost_estimate=pl.CostEstimate(flops=0, bytes_accessed=200000, transcendentals=0),
+        cost_estimate=pl.CostEstimate(flops=0, bytes_accessed=800000, transcendentals=0),
     )(q_weight, k_weight, v_weight)
     weight_b = swap(weight, "zh")
-
-    weight_b, feats_b = lax.optimization_barrier((weight_b, feats_b))
-    (weight,) = call(spread_kernel, [shaped(ZL * CORES, ZH, 64, 3 * HD)], 0, 2, 1000, 1 << 20)(
-        weight, weight_b
-    )
-    weight = lax.all_to_all(weight, ("zl", "core"), 0, 0, tiled=True)
+    weight_a = lax.all_to_all(spread, ("zl", "core"), 0, 0, tiled=True)
+    weight_a, weight_b, feats_b = lax.optimization_barrier((weight_a, weight_b, feats_b))
+    (spread,) = call(spread_kernel, [shaped(ZL * CORES, 64, 3 * HD)], 0, 1, 1000, 1 << 20)(weight_b)
+    weight_b = lax.all_to_all(spread, ("zl", "core"), 0, 0, tiled=True)
 
     feats = lax.all_gather(jnp.stack([feats, feats_b]), "tp", axis=0)
+    weight_b, feats = lax.optimization_barrier((weight_b, feats))
+    weight = lax.all_gather(jnp.stack([weight_a, weight_b]), "y", axis=0)
     (joined,) = call(join_frames_kernel, [shaped(ROWS, 512)], 1, 3, 2 * ROWS * 1024 * 512, 2 << 20)(
         jnp.stack([section, count[0]]), feats, proj.reshape(8, HD, 512), text
     )
 
-    weight, joined = lax.optimization_barrier((weight, joined))
-    weight = lax.all_gather(weight, "y", axis=0)
     joined_b = swap(joined, "section")
     own_a = lax.all_gather(joined, "tp", axis=0)
     own_a, joined_b = lax.optimization_barrier((own_a, joined_b))
@@ -284,7 +284,7 @@
         in_specs=[SMEM] + [VMEM] * 4 + [pl.BlockSpec(memory_space=pltpu.HBM)] + [VMEM] * 3,
         out_specs=[VMEM] * 3,
         scratch_shapes=[
-            pltpu.VMEM((Y, ZL * CORES, ZH, 64, 3 * HD), jnp.bfloat16),
+            pltpu.VMEM((Y, ZH, ZL * CORES, 64, 3 * HD), jnp.bfloat16),
             pltpu.SemaphoreType.DMA((TP,)),
         ],
         compiler_params=pltpu.CompilerParams(vmem_limit_bytes=LIMIT),

time: 178 us -> 177 us (level)
  waiting for transfers between devices: 29.1 us -> 22 us
  starting transfers between devices: 60.2 us -> 67 us
  local copies, waits for them, and re-layouts: 3.55 us -> 0.88 us
    all_to_all x1 -> x2, starting transfers between devices: 12.8 us -> 18.9 us  [the longest x1 10.2 us: local(): weight_a = lax.all_to_all(spread, ('zl', 'core'), 0, 0, tiled=True)]
    all_to_all x1 -> x2, waiting for transfers between devices: 6.6 us -> 1.41 us  [the longest x1 1.41 us: local(): weight_b = lax.all_to_all(spread, ('zl', 'core'), 0, 0, tiled=True)]
    unnamed x10 -> x6, local copies, waits for them, and re-layouts: 2.69 us -> 0.01 us
    all_gather x1, blocking collectives: 13 us -> 15.6 us  [local(): own_b = lax.all_gather(joined_b, 'tp', axis=0)]
  transfers between devices with their start and end apart: 10 -> 11, of which waited for: 7 -> 6; matrix products, arithmetic and copies ran while one was open for 1% -> 1% of each run, Pallas kernels for 2% -> 2%
where the time goes in v7:
time: 177 us
  starting transfers between devices  67 us (38%)
  blocking collectives  57.6 us (33%)
  waiting for transfers between devices  22 us (12%)
  between operations  14.2 us (8%)
  Pallas kernels  12.4 us (7%)
  other arithmetic  2.59 us (1%)
    ppermute x6, starting transfers between devices, swap(): return lax.ppermute(v, axis, SWAP)  36.7 us
    all_gather x1, blocking collectives, local(): own_b = lax.all_gather(joined_b, 'tp', axis=0)  15.6 us
    all_to_all x1, blocking collectives, local(): parts = lax.all_to_all(parts, ('y', 'core'), 0, 0, tiled=True)  11.7 us
    all_gather x1, blocking collectives, local(): own_a = lax.all_gather(joined, 'tp', axis=0)  11.1 us
    all_to_all x1, waiting for transfers between devices, gather(): lax.all_to_all(jnp.broadcast_to(v[None], (n, *v.shape)), axis, 0, 0, tile...  10.9 us
    all_to_all x1, starting transfers between devices, local(): weight_a = lax.all_to_all(spread, ('zl', 'core'), 0, 0, tiled=True)  10.2 us
    all_gather x1, blocking collectives, local(): queries = lax.all_gather(queries, 'y', axis=0)  9.67 us
    all_gather x1, blocking collectives, local(): feats = lax.all_gather(jnp.stack([feats, feats_b]), 'tp', axis=0)  9.51 us
  transfers between devices with their start and end apart: 11, of which 6 were waited for; matrix products, arithmetic and copies ran while one was open for 1% of the time, Pallas kernels for 2%

profile of v7, /device:TPU:1, one launch (start us, length us, event | category | flops | bytes accessed | tf_op | source)
XLA Modules:
  0.0 176.6 jit_solution(3431696628613917037)
XLA Ops:
  6.5 1.7 shard_map.82
  8.3 10.2 %all-to-all-start = ((bf16[8,64,384]{2,1,0:T(8,128)(2,1)}), bf16[8,64,384]{2,1,0:T(8,128)(2,1)S(1)}, u32[]{:S(2)}, u32[]{:S(2)}) async-start(bf16[8,64,384]{2,1,0:T(8,128)(2,1)} %get-tuple-element.22), calls=%async_computation | async-start | bytes 786432 | tf_op jit(solution)/shard_map/all_to_all | solution.py:259
  18.5 6.0 %collective-permute-start = (bf16[64,768]{1,0:T(8,128)(2,1)}, bf16[64,768]{1,0:T(8,128)(2,1)S(1)}, u32[]{:S(2)}, u32[]{:S(2)}) collective-permute-start(bf16[64,768]{1,0:T(8,128)(2,1)} %get-tuple-element.23), channel_id=1, source_target_pairs={{0,256},{256,0},{1,257},{257,1},{2,258},{258,2},{3,259},{259,3},{4... | collective-permute-start | bytes 294920 | tf_op jit(solution)/shard_map/ppermute | solution.py:26
  24.5 8.1 %collective-permute-start.1 = (bf16[128,128]{1,0:T(8,128)(2,1)}, bf16[128,128]{1,0:T(8,128)(2,1)S(1)}, u32[]{:S(2)}, u32[]{:S(2)}) collective-permute-start(bf16[128,128]{1,0:T(8,128)(2,1)} %param.9), channel_id=1, source_target_pairs={{0,4},{4,0},{1,5},{5,1},{2,6},{6,2},{3,7},{7,3},{8,12},{12,8},{9,1... | collective-permute-start | bytes 98312 | tf_op jit(solution)/shard_map/ppermute | solution.py:26
  32.6 5.6 %collective-permute-done.1 = bf16[128,128]{1,0:T(8,128)(2,1)S(1)} collective-permute-done((bf16[128,128]{1,0:T(8,128)(2,1)}, bf16[128,128]{1,0:T(8,128)(2,1)S(1)}, u32[]{:S(2)}, u32[]{:S(2)}) %collective-permute-start.1) | collective-permute-done | bytes 32800 | tf_op jit(solution)/shard_map/ppermute | solution.py:26
  39.0 8.7 %all-to-all-start.1 = ((bf16[8,64,384]{2,1,0:T(8,128)(2,1)}), bf16[8,64,384]{2,1,0:T(8,128)(2,1)S(1)}, u32[]{:S(2)}, u32[]{:S(2)}) async-start(bf16[8,64,384]{2,1,0:T(8,128)(2,1)} %shard_map.83), calls=%async_computation.1 | async-start | bytes 786432 | tf_op jit(solution)/shard_map/all_to_all | solution.py:262
  48.5 9.5 %all-gather = bf16[8,128,128]{2,1,0:T(8,128)(2,1)S(1)} all-gather(bf16[2,128,128]{2,1,0:T(8,128)(2,1)S(1)} %pad_maximum_fusion.3), channel_id=2, replica_groups=mesh['zh'=2,'zl'=4,'y'=4,'core'=2,'section'=2,'tp'=4] {'tp'}, dimensions={0}, use_global_device_ids=true | all-gather | bytes 327680 | tf_op jit(solution)/shard_map/all_gather | solution.py:264
  58.0 1.4 all-to-all-done.1
  62.2 8.3 %collective-permute-start.2 = (bf16[128,512]{1,0:T(8,128)(2,1)S(1)}, bf16[128,512]{1,0:T(8,128)(2,1)S(1)}, u32[]{:S(2)}, u32[]{:S(2)}) collective-permute-start(bf16[128,512]{1,0:T(8,128)(2,1)S(1)} %shard_map.84), channel_id=1, source_target_pairs={{0,4},{4,0},{1,5},{5,1},{2,6},{6,2},{3,7},{7,3},{8,12},{12,8},{9,1... | collective-permute-start | bytes 393224 | tf_op jit(solution)/shard_map/ppermute | solution.py:26
  70.5 11.1 %all-gather.1 = bf16[512,512]{1,0:T(8,128)(2,1)S(1)} all-gather(bf16[128,512]{1,0:T(8,128)(2,1)S(1)} %shard_map.84), channel_id=3, replica_groups=mesh['zh'=2,'zl'=4,'y'=4,'core'=2,'section'=2,'tp'=4] {'tp'}, dimensions={0}, use_global_device_ids=true | all-gather | bytes 655360 | tf_op jit(solution)/shard_map/all_gather | solution.py:272
  81.6 15.6 %all-gather.2 = bf16[512,512]{1,0:T(8,128)(2,1)S(1)} all-gather(bf16[128,512]{1,0:T(8,128)(2,1)S(1)} %collective-permute-done.2), channel_id=4, replica_groups=mesh['zh'=2,'zl'=4,'y'=4,'core'=2,'section'=2,'tp'=4] {'tp'}, dimensions={0}, use_global_device_ids=true | all-gather | bytes 655360 | tf_op jit(solution)/shard_map/all_gather | solution.py:275
  97.2 5.1 %collective-permute-start.4 = (bf16[4,128,512]{2,1,0:T(8,128)(2,1)S(1)}, bf16[4,128,512]{2,1,0:T(8,128)(2,1)S(1)}, u32[]{:S(2)}, u32[]{:S(2)}) collective-permute-start(bf16[4,128,512]{2,1,0:T(8,128)(2,1)S(1)} %bitcast.18), channel_id=1, source_target_pairs={{0,8},{8,0},{1,9},{9,1},{2,10},{10,2},{3,11},{11,3},{4,12},{12,4},... | collective-permute-start | bytes 1572872 | tf_op jit(solution)/shard_map/ppermute | solution.py:26
  102.3 1.9 %collective-permute-start.3 = (bf16[4,128,512]{2,1,0:T(8,128)(2,1)S(1)}, bf16[4,128,512]{2,1,0:T(8,128)(2,1)S(1)}, u32[]{:S(2)}, u32[]{:S(2)}) collective-permute-start(bf16[4,128,512]{2,1,0:T(8,128)(2,1)S(1)} %bitcast.16), channel_id=1, source_target_pairs={{0,8},{8,0},{1,9},{9,1},{2,10},{10,2},{3,11},{11,3},{4,12},{12,4},... | collective-permute-start | bytes 1572872 | tf_op jit(solution)/shard_map/ppermute | solution.py:26
  105.0 1.2 collective-permute-done.3.other_a
  106.4 3.9 %shard_map.85 = (bf16[256,128]{1,0:T(8,128)(2,1)S(1)}, bf16[256,256]{1,0:T(8,128)(2,1)S(1)}, bf16[4,256,256]{2,1,0:T(8,128)(2,1)}) custom-call(s32[1]{0:T(128)} %bitcast.4.flip, bf16[4,128,512]{2,1,0:T(8,128)(2,1)S(1)} %bitcast.17, bf16[4,128,512]{2,1,0:T(8,128)(2,1)S(1)} %bitcast.19, bf16[4,128,512]{2,1,0:T(8,128)(2,1)S(1)} %collective-permute-done.3.other_a, ...), custom_call_target="tpu_custom_call" | custom-call | flops 805306368 | bytes 6291456 | tf_op jit(solution)/shard_map/pallas_call | solution.py:277
  110.4 4.6 %all-to-all-start.2 = ((bf16[4,256,256]{2,1,0:T(8,128)(2,1)}), bf16[4,256,256]{2,1,0:T(8,128)(2,1)S(1)}, u32[]{:S(2)}, u32[]{:S(2)}) async-start(bf16[4,256,256]{2,1,0:T(8,128)(2,1)} %get-tuple-element.31), calls=%async_computation.2 | async-start | bytes 1048576 | tf_op jit(solution)/shard_map/all_to_all | solution.py:307
  115.0 7.3 %collective-permute-start.5 = (bf16[256,256]{1,0:T(8,128)(2,1)S(1)}, bf16[256,256]{1,0:T(8,128)(2,1)S(1)}, u32[]{:S(2)}, u32[]{:S(2)}) collective-permute-start(bf16[256,256]{1,0:T(8,128)(2,1)S(1)} %get-tuple-element.32), channel_id=1, source_target_pairs={{0,256},{256,0},{1,257},{257,1},{2,258},{258,2},{3,259},{259,3},{4... | collective-permute-start | bytes 393224 | tf_op jit(solution)/shard_map/ppermute | solution.py:26
  122.3 9.7 %all-gather.4 = bf16[1024,128]{1,0:T(8,128)(2,1)S(1)} all-gather(bf16[256,128]{1,0:T(8,128)(2,1)S(1)} %get-tuple-element.33), channel_id=6, replica_groups=mesh['zh'=2,'zl'=4,'y'=4,'core'=2,'section'=2,'tp'=4] {'y'}, dimensions={0}, use_global_device_ids=true | all-gather | bytes 327680 | tf_op jit(solution)/shard_map/all_gather | solution.py:308
  132.0 2.6 %all-to-all-done.2.kv = bf16[4,256,256]{2,1,0:T(8,128)(2,1)S(1)} async-done(((bf16[4,256,256]{2,1,0:T(8,128)(2,1)}), bf16[4,256,256]{2,1,0:T(8,128)(2,1)S(1)}, u32[]{:S(2)}, u32[]{:S(2)}) %all-to-all-start.2) | async-done | bytes 524320 | tf_op jit(solution)/shard_map/all_to_all | solution.py:307
  135.4 6.7 %all-to-all-start.3 = ((bf16[4,256,256]{2,1,0:T(8,128)(2,1)}), bf16[4,256,256]{2,1,0:T(8,128)(2,1)S(1)}, u32[]{:S(2)}, u32[]{:S(2)}) async-start(bf16[4,256,256]{2,1,0:T(8,128)(2,1)} %broadcast_in_dim.2), calls=%async_computation.3 | async-start | bytes 1048576 | tf_op jit(solution)/shard_map/all_to_all | solution.py:30
  142.2 3.0 %shard_map.86 = (f32[4,256,128]{2,1,0:T(8,128)S(1)}, f32[4,256,128]{2,1,0:T(8,128)S(1)}) custom-call(s32[4]{0:T(128)S(1)} %pad_add_fusion.place, bf16[4,256,128]{2,1,0:T(8,128)(2,1)S(1)} %bitcast.20, bf16[4,256,256]{2,1,0:T(8,128)(2,1)S(1)} %all-to-all-done.2.kv), custom_call_target="tpu_custom_call" | custom-call | flops 536870912 | bytes 2097152 | tf_op jit(solution)/shard_map/pallas_call | solution.py:314
  145.2 10.9 %all-to-all-done.3.kv = bf16[4,256,256]{2,1,0:T(8,128)(2,1)S(1)} async-done(((bf16[4,256,256]{2,1,0:T(8,128)(2,1)}), bf16[4,256,256]{2,1,0:T(8,128)(2,1)S(1)}, u32[]{:S(2)}, u32[]{:S(2)}) %all-to-all-start.3) | async-done | bytes 524320 | tf_op jit(solution)/shard_map/all_to_all | solution.py:30
  157.1 11.7 %all_to_all.25.parts = bf16[8,136,128]{2,1,0:T(8,128)(2,1)S(1)} all-to-all(bf16[8,136,128]{2,1,0:T(8,128)(2,1)S(1)} %shard_map.87), channel_id=1, replica_groups=mesh['zh'=2,'zl'=4,'y'=4,'core'=2,'section'=2,'tp'=4] {'y','core'}, dimensions={0} | all-to-all | bytes 557056 | tf_op jit(solution)/shard_map/all_to_all | solution.py:322
  168.7 1.0 shard_map.88
  (29 shorter events, 6.5 us)
Async XLA Ops:
  6.5 54.5 %copy-start.2 = (bf16[4096]{0:T(1024)(128)(2,1)S(1)}, bf16[4096]{0:T(1024)(128)(2,1)}, u32[]{:S(2)}) copy-start(bf16[4096]{0:T(1024)(128)(2,1)} %param.12) | copy-start | bytes 24580
  6.5 54.6 %copy-start = (bf16[1024,512]{1,0:T(8,128)(2,1)S(1)}, bf16[1024,512]{1,0:T(8,128)(2,1)}, u32[]{:S(2)}) copy-start(bf16[1024,512]{1,0:T(8,128)(2,1)} %param.11) | copy-start | bytes 3145732
  6.5 54.6 %copy-start.1 = (bf16[128,512]{1,0:T(8,128)(2,1)S(1)}, bf16[128,512]{1,0:T(8,128)(2,1)}, u32[]{:S(2)}) copy-start(bf16[128,512]{1,0:T(8,128)(2,1)} %text.1) | copy-start | bytes 393220
  8.3 29.9 %all-to-all-start = ((bf16[8,64,384]{2,1,0:T(8,128)(2,1)}), bf16[8,64,384]{2,1,0:T(8,128)(2,1)S(1)}, u32[]{:S(2)}, u32[]{:S(2)}) async-start(bf16[8,64,384]{2,1,0:T(8,128)(2,1)} %get-tuple-element.22), calls=%async_computation | async-start | bytes 786432 | tf_op jit(solution)/shard_map/all_to_all | solution.py:259
  18.5 19.7 %collective-permute-start = (bf16[64,768]{1,0:T(8,128)(2,1)}, bf16[64,768]{1,0:T(8,128)(2,1)S(1)}, u32[]{:S(2)}, u32[]{:S(2)}) collective-permute-start(bf16[64,768]{1,0:T(8,128)(2,1)} %get-tuple-element.23), channel_id=1, source_target_pairs={{0,256},{256,0},{1,257},{257,1},{2,258},{258,2},{3,259},{259,3},{4... | collective-permute-start | bytes 294920 | tf_op jit(solution)/shard_map/ppermute | solution.py:26
  24.5 13.7 %collective-permute-start.1 = (bf16[128,128]{1,0:T(8,128)(2,1)}, bf16[128,128]{1,0:T(8,128)(2,1)S(1)}, u32[]{:S(2)}, u32[]{:S(2)}) collective-permute-start(bf16[128,128]{1,0:T(8,128)(2,1)} %param.9), channel_id=1, source_target_pairs={{0,4},{4,0},{1,5},{5,1},{2,6},{6,2},{3,7},{7,3},{8,12},{12,8},{9,1... | collective-permute-start | bytes 98312 | tf_op jit(solution)/shard_map/ppermute | solution.py:26
  39.0 20.4 %all-to-all-start.1 = ((bf16[8,64,384]{2,1,0:T(8,128)(2,1)}), bf16[8,64,384]{2,1,0:T(8,128)(2,1)S(1)}, u32[]{:S(2)}, u32[]{:S(2)}) async-start(bf16[8,64,384]{2,1,0:T(8,128)(2,1)} %shard_map.83), calls=%async_computation.1 | async-start | bytes 786432 | tf_op jit(solution)/shard_map/all_to_all | solution.py:262
  47.7 58.8 %all-gather.7.cloned.1.call-start = ((), (), s32[]{:S(2)}) async-start(), calls=%async_computation.5 | async-start | bytes 3932160 | tf_op jit(solution)/shard_map/all_gather | solution.py:266
  62.2 19.5 %collective-permute-start.2 = (bf16[128,512]{1,0:T(8,128)(2,1)S(1)}, bf16[128,512]{1,0:T(8,128)(2,1)S(1)}, u32[]{:S(2)}, u32[]{:S(2)}) collective-permute-start(bf16[128,512]{1,0:T(8,128)(2,1)S(1)} %shard_map.84), channel_id=1, source_target_pairs={{0,4},{4,0},{1,5},{5,1},{2,6},{6,2},{3,7},{7,3},{8,12},{12,8},{9,1... | collective-permute-start | bytes 393224 | tf_op jit(solution)/shard_map/ppermute | solution.py:26
  97.2 7.7 %collective-permute-start.4 = (bf16[4,128,512]{2,1,0:T(8,128)(2,1)S(1)}, bf16[4,128,512]{2,1,0:T(8,128)(2,1)S(1)}, u32[]{:S(2)}, u32[]{:S(2)}) collective-permute-start(bf16[4,128,512]{2,1,0:T(8,128)(2,1)S(1)} %bitcast.18), channel_id=1, source_target_pairs={{0,8},{8,0},{1,9},{9,1},{2,10},{10,2},{3,11},{11,3},{4,12},{12,4},... | collective-permute-start | bytes 1572872 | tf_op jit(solution)/shard_map/ppermute | solution.py:26
  102.3 3.8 %collective-permute-start.3 = (bf16[4,128,512]{2,1,0:T(8,128)(2,1)S(1)}, bf16[4,128,512]{2,1,0:T(8,128)(2,1)S(1)}, u32[]{:S(2)}, u32[]{:S(2)}) collective-permute-start(bf16[4,128,512]{2,1,0:T(8,128)(2,1)S(1)} %bitcast.16), channel_id=1, source_target_pairs={{0,8},{8,0},{1,9},{9,1},{2,10},{10,2},{3,11},{11,3},{4,12},{12,4},... | collective-permute-start | bytes 1572872 | tf_op jit(solution)/shard_map/ppermute | solution.py:26
  110.4 24.2 %all-to-all-start.2 = ((bf16[4,256,256]{2,1,0:T(8,128)(2,1)}), bf16[4,256,256]{2,1,0:T(8,128)(2,1)S(1)}, u32[]{:S(2)}, u32[]{:S(2)}) async-start(bf16[4,256,256]{2,1,0:T(8,128)(2,1)} %get-tuple-element.31), calls=%async_computation.2 | async-start | bytes 1048576 | tf_op jit(solution)/shard_map/all_to_all | solution.py:307
  115.0 17.0 %collective-permute-start.5 = (bf16[256,256]{1,0:T(8,128)(2,1)S(1)}, bf16[256,256]{1,0:T(8,128)(2,1)S(1)}, u32[]{:S(2)}, u32[]{:S(2)}) collective-permute-start(bf16[256,256]{1,0:T(8,128)(2,1)S(1)} %get-tuple-element.32), channel_id=1, source_target_pairs={{0,256},{256,0},{1,257},{257,1},{2,258},{258,2},{3,259},{259,3},{4... | collective-permute-start | bytes 393224 | tf_op jit(solution)/shard_map/ppermute | solution.py:26
  135.4 20.7 %all-to-all-start.3 = ((bf16[4,256,256]{2,1,0:T(8,128)(2,1)}), bf16[4,256,256]{2,1,0:T(8,128)(2,1)S(1)}, u32[]{:S(2)}, u32[]{:S(2)}) async-start(bf16[4,256,256]{2,1,0:T(8,128)(2,1)} %broadcast_in_dim.2), calls=%async_computation.3 | async-start | bytes 1048576 | tf_op jit(solution)/shard_map/all_to_all | solution.py:30
Sparse Core Ops, SparseCore 0:
  60.5 45.9 all-gather.6

commit v8 on v7

--- a/solution.py
+++ b/solution.py
@@ -30,13 +30,13 @@
     return lax.all_to_all(jnp.broadcast_to(v[None], (n, *v.shape)), axis, 0, 0, tiled=True)
 
 
-def join_frames_kernel(pick, feats, proj, text, out):
+def join_frames_kernel(pick, feats_a, feats_b, proj, text, out):
     vision = jnp.zeros((ROWS, 512), jnp.float32)
-    for s in range(SECTIONS):
+    for s, feats in enumerate((feats_a, feats_b)):
         first = jnp.bitwise_xor(pick[0], s) * TP
         for t in range(TP):
             vision = vision + jnp.dot(
-                feats[t, s], proj[first + t], preferred_element_type=jnp.float32
+                feats[t], proj[first + t], preferred_element_type=jnp.float32
             )
     row = lax.broadcasted_iota(jnp.int32, (ROWS, 512), 0)
     joined = jnp.where(row < pick[1], vision, text[...].astype(jnp.float32))
@@ -257,15 +257,18 @@
     )(q_weight, k_weight, v_weight)
     weight_b = swap(weight, "zh")
     weight_a = lax.all_to_all(spread, ("zl", "core"), 0, 0, tiled=True)
-    weight_a, weight_b, feats_b = lax.optimization_barrier((weight_a, weight_b, feats_b))
+    feats_a = lax.all_gather(feats, "tp", axis=0)
+    weight_a, weight_b, feats_a, feats_b = lax.optimization_barrier(
+        (weight_a, weight_b, feats_a, feats_b)
+    )
     (spread,) = call(spread_kernel, [shaped(ZL * CORES, 64, 3 * HD)], 0, 1, 1000, 1 << 20)(weight_b)
     weight_b = lax.all_to_all(spread, ("zl", "core"), 0, 0, tiled=True)
 
-    feats = lax.all_gather(jnp.stack([feats, feats_b]), "tp", axis=0)
-    weight_b, feats = lax.optimization_barrier((weight_b, feats))
+    feats_b = lax.all_gather(feats_b, "tp", axis=0)
+    weight_b, feats_b = lax.optimization_barrier((weight_b, feats_b))
     weight = lax.all_gather(jnp.stack([weight_a, weight_b]), "y", axis=0)
-    (joined,) = call(join_frames_kernel, [shaped(ROWS, 512)], 1, 3, 2 * ROWS * 1024 * 512, 2 << 20)(
-        jnp.stack([section, count[0]]), feats, proj.reshape(8, HD, 512), text
+    (joined,) = call(join_frames_kernel, [shaped(ROWS, 512)], 1, 4, 2 * ROWS * 1024 * 512, 2 << 20)(
+        jnp.stack([section, count[0]]), feats_a, feats_b, proj.reshape(8, HD, 512), text
     )
 
     joined_b = swap(joined, "section")

time: 177 us -> 179 us (1.011)
  blocking collectives: 57.6 us -> 63.7 us
  starting transfers between devices: 67 us -> 62.6 us
    all_gather x1 -> x2, blocking collectives: 9.51 us -> 20 us  [the longest x1 10.5 us: local(): feats_a = lax.all_gather(feats, 'tp', axis=0)]
    all_gather x1, blocking collectives: 15.6 us -> 11.1 us  [local(): own_b = lax.all_gather(joined_b, 'tp', axis=0)]
    ppermute x6, starting transfers between devices: 36.7 us -> 33.4 us  [swap(): return lax.ppermute(v, axis, SWAP)]
  transfers between devices with their start and end apart: 11 -> 11, of which waited for: 6 -> 6; matrix products, arithmetic and copies ran while one was open for 1% -> 0% of each run, Pallas kernels for 2% -> 2%
where the time goes in v8:
time: 179 us; the launch traced here: 178 us
  blocking collectives  63.7 us (36%)
  starting transfers between devices  62.6 us (35%)
  waiting for transfers between devices  22.8 us (13%)
  between operations  14.2 us (8%)
  Pallas kernels  12.4 us (7%)
  other arithmetic  1.82 us (1%)
    ppermute x6, starting transfers between devices, swap(): return lax.ppermute(v, axis, SWAP)  33.4 us
    all_to_all x1, blocking collectives, local(): parts = lax.all_to_all(parts, ('y', 'core'), 0, 0, tiled=True)  11.7 us
    all_gather x1, blocking collectives, local(): own_a = lax.all_gather(joined, 'tp', axis=0)  11.3 us
    all_gather x1, blocking collectives, local(): own_b = lax.all_gather(joined_b, 'tp', axis=0)  11.1 us
    all_to_all x1, waiting for transfers between devices, gather(): lax.all_to_all(jnp.broadcast_to(v[None], (n, *v.shape)), axis, 0, 0, tile...  10.9 us
    all_gather x1, blocking collectives, local(): feats_a = lax.all_gather(feats, 'tp', axis=0)  10.5 us
    all_to_all x1, starting transfers between devices, local(): weight_a = lax.all_to_all(spread, ('zl', 'core'), 0, 0, tiled=True)  10.2 us
    all_gather x1, blocking collectives, local(): queries = lax.all_gather(queries, 'y', axis=0)  9.67 us
  transfers between devices with their start and end apart: 11, of which 6 were waited for; matrix products, arithmetic and copies ran while one was open for 0% of the time, Pallas kernels for 2%

profile of v8, /device:TPU:1, one launch (start us, length us, event | category | flops | bytes accessed | tf_op | source)
XLA Modules:
  0.0 178.4 jit_solution(14792561805804448489)
XLA Ops:
  6.5 1.7 shard_map.82
  8.3 10.2 %all-to-all-start = ((bf16[8,64,384]{2,1,0:T(8,128)(2,1)}), bf16[8,64,384]{2,1,0:T(8,128)(2,1)S(1)}, u32[]{:S(2)}, u32[]{:S(2)}) async-start(bf16[8,64,384]{2,1,0:T(8,128)(2,1)} %get-tuple-element.23), calls=%async_computation | async-start | bytes 786432 | tf_op jit(solution)/shard_map/all_to_all | solution.py:259
  18.5 6.0 %collective-permute-start = (bf16[64,768]{1,0:T(8,128)(2,1)}, bf16[64,768]{1,0:T(8,128)(2,1)S(1)}, u32[]{:S(2)}, u32[]{:S(2)}) collective-permute-start(bf16[64,768]{1,0:T(8,128)(2,1)} %get-tuple-element.24), channel_id=1, source_target_pairs={{0,256},{256,0},{1,257},{257,1},{2,258},{258,2},{3,259},{259,3},{4... | collective-permute-start | bytes 294920 | tf_op jit(solution)/shard_map/ppermute | solution.py:26
  24.5 8.1 %collective-permute-start.1 = (bf16[128,128]{1,0:T(8,128)(2,1)}, bf16[128,128]{1,0:T(8,128)(2,1)S(1)}, u32[]{:S(2)}, u32[]{:S(2)}) collective-permute-start(bf16[128,128]{1,0:T(8,128)(2,1)} %param.9), channel_id=1, source_target_pairs={{0,4},{4,0},{1,5},{5,1},{2,6},{6,2},{3,7},{7,3},{8,12},{12,8},{9,1... | collective-permute-start | bytes 98312 | tf_op jit(solution)/shard_map/ppermute | solution.py:26
  32.6 10.5 %all-gather = bf16[512,128]{1,0:T(8,128)(2,1)S(1)} all-gather(bf16[128,128]{1,0:T(8,128)(2,1)} %param.9), channel_id=2, replica_groups=mesh['zh'=2,'zl'=4,'y'=4,'core'=2,'section'=2,'tp'=4] {'tp'}, dimensions={0}, use_global_device_ids=true | all-gather | bytes 163840 | tf_op jit(solution)/shard_map/all_gather | solution.py:260
  44.0 7.7 %all-to-all-start.1 = ((bf16[8,64,384]{2,1,0:T(8,128)(2,1)}), bf16[8,64,384]{2,1,0:T(8,128)(2,1)S(1)}, u32[]{:S(2)}, u32[]{:S(2)}) async-start(bf16[8,64,384]{2,1,0:T(8,128)(2,1)} %shard_map.83), calls=%async_computation.1 | async-start | bytes 786432 | tf_op jit(solution)/shard_map/all_to_all | solution.py:265
  51.7 9.5 %all-gather.1 = bf16[512,128]{1,0:T(8,128)(2,1)S(1)} all-gather(bf16[128,128]{1,0:T(8,128)(2,1)S(1)} %collective-permute-done.1), channel_id=3, replica_groups=mesh['zh'=2,'zl'=4,'y'=4,'core'=2,'section'=2,'tp'=4] {'tp'}, dimensions={0}, use_global_device_ids=true | all-gather | bytes 163840 | tf_op jit(solution)/shard_map/all_gather | solution.py:267
  61.1 2.2 %all-to-all-done.1 = bf16[8,64,384]{2,1,0:T(8,128)(2,1)S(1)} async-done(((bf16[8,64,384]{2,1,0:T(8,128)(2,1)}), bf16[8,64,384]{2,1,0:T(8,128)(2,1)S(1)}, u32[]{:S(2)}, u32[]{:S(2)}) %all-to-all-start.1) | async-done | bytes 393248 | tf_op jit(solution)/shard_map/all_to_all | solution.py:265
  66.1 5.9 %collective-permute-start.2 = (bf16[128,512]{1,0:T(8,128)(2,1)S(1)}, bf16[128,512]{1,0:T(8,128)(2,1)S(1)}, u32[]{:S(2)}, u32[]{:S(2)}) collective-permute-start(bf16[128,512]{1,0:T(8,128)(2,1)S(1)} %shard_map.84), channel_id=1, source_target_pairs={{0,4},{4,0},{1,5},{5,1},{2,6},{6,2},{3,7},{7,3},{8,12},{12,8},{9,1... | collective-permute-start | bytes 393224 | tf_op jit(solution)/shard_map/ppermute | solution.py:26
  72.0 11.3 %all-gather.2 = bf16[512,512]{1,0:T(8,128)(2,1)S(1)} all-gather(bf16[128,512]{1,0:T(8,128)(2,1)S(1)} %shard_map.84), channel_id=4, replica_groups=mesh['zh'=2,'zl'=4,'y'=4,'core'=2,'section'=2,'tp'=4] {'tp'}, dimensions={0}, use_global_device_ids=true | all-gather | bytes 655360 | tf_op jit(solution)/shard_map/all_gather | solution.py:275
  83.3 4.2 %collective-permute-done.2 = bf16[128,512]{1,0:T(8,128)(2,1)S(1)} collective-permute-done((bf16[128,512]{1,0:T(8,128)(2,1)S(1)}, bf16[128,512]{1,0:T(8,128)(2,1)S(1)}, u32[]{:S(2)}, u32[]{:S(2)}) %collective-permute-start.2) | collective-permute-done | bytes 131104 | tf_op jit(solution)/shard_map/ppermute | solution.py:26
  87.4 11.1 %all-gather.3 = bf16[512,512]{1,0:T(8,128)(2,1)S(1)} all-gather(bf16[128,512]{1,0:T(8,128)(2,1)S(1)} %collective-permute-done.2), channel_id=5, replica_groups=mesh['zh'=2,'zl'=4,'y'=4,'core'=2,'section'=2,'tp'=4] {'tp'}, dimensions={0}, use_global_device_ids=true | all-gather | bytes 655360 | tf_op jit(solution)/shard_map/all_gather | solution.py:278
  98.5 4.2 %collective-permute-start.4 = (bf16[4,128,512]{2,1,0:T(8,128)(2,1)S(1)}, bf16[4,128,512]{2,1,0:T(8,128)(2,1)S(1)}, u32[]{:S(2)}, u32[]{:S(2)}) collective-permute-start(bf16[4,128,512]{2,1,0:T(8,128)(2,1)S(1)} %bitcast.17), channel_id=1, source_target_pairs={{0,8},{8,0},{1,9},{9,1},{2,10},{10,2},{3,11},{11,3},{4,12},{12,4},... | collective-permute-start | bytes 1572872 | tf_op jit(solution)/shard_map/ppermute | solution.py:26
  102.7 1.9 %collective-permute-start.3 = (bf16[4,128,512]{2,1,0:T(8,128)(2,1)S(1)}, bf16[4,128,512]{2,1,0:T(8,128)(2,1)S(1)}, u32[]{:S(2)}, u32[]{:S(2)}) collective-permute-start(bf16[4,128,512]{2,1,0:T(8,128)(2,1)S(1)} %bitcast.15), channel_id=1, source_target_pairs={{0,8},{8,0},{1,9},{9,1},{2,10},{10,2},{3,11},{11,3},{4,12},{12,4},... | collective-permute-start | bytes 1572872 | tf_op jit(solution)/shard_map/ppermute | solution.py:26
  106.5 1.7 all-gather.8.cloned.1.call-done
  108.2 4.0 %shard_map.85 = (bf16[256,128]{1,0:T(8,128)(2,1)S(1)}, bf16[256,256]{1,0:T(8,128)(2,1)S(1)}, bf16[4,256,256]{2,1,0:T(8,128)(2,1)}) custom-call(s32[1]{0:T(128)} %bitcast.4.flip, bf16[4,128,512]{2,1,0:T(8,128)(2,1)S(1)} %bitcast.16, bf16[4,128,512]{2,1,0:T(8,128)(2,1)S(1)} %bitcast.18, bf16[4,128,512]{2,1,0:T(8,128)(2,1)S(1)} %collective-permute-done.3.other_a, ...), custom_call_target="tpu_custom_call" | custom-call | flops 805306368 | bytes 6291456 | tf_op jit(solution)/shard_map/pallas_call | solution.py:280
  112.2 4.5 %all-to-all-start.2 = ((bf16[4,256,256]{2,1,0:T(8,128)(2,1)}), bf16[4,256,256]{2,1,0:T(8,128)(2,1)S(1)}, u32[]{:S(2)}, u32[]{:S(2)}) async-start(bf16[4,256,256]{2,1,0:T(8,128)(2,1)} %get-tuple-element.33), calls=%async_computation.2 | async-start | bytes 1048576 | tf_op jit(solution)/shard_map/all_to_all | solution.py:310
  116.7 7.4 %collective-permute-start.5 = (bf16[256,256]{1,0:T(8,128)(2,1)S(1)}, bf16[256,256]{1,0:T(8,128)(2,1)S(1)}, u32[]{:S(2)}, u32[]{:S(2)}) collective-permute-start(bf16[256,256]{1,0:T(8,128)(2,1)S(1)} %get-tuple-element.34), channel_id=1, source_target_pairs={{0,256},{256,0},{1,257},{257,1},{2,258},{258,2},{3,259},{259,3},{4... | collective-permute-start | bytes 393224 | tf_op jit(solution)/shard_map/ppermute | solution.py:26
  124.1 9.7 %all-gather.5 = bf16[1024,128]{1,0:T(8,128)(2,1)S(1)} all-gather(bf16[256,128]{1,0:T(8,128)(2,1)S(1)} %get-tuple-element.35), channel_id=7, replica_groups=mesh['zh'=2,'zl'=4,'y'=4,'core'=2,'section'=2,'tp'=4] {'y'}, dimensions={0}, use_global_device_ids=true | all-gather | bytes 327680 | tf_op jit(solution)/shard_map/all_gather | solution.py:311
  133.8 2.6 %all-to-all-done.2.kv = bf16[4,256,256]{2,1,0:T(8,128)(2,1)S(1)} async-done(((bf16[4,256,256]{2,1,0:T(8,128)(2,1)}), bf16[4,256,256]{2,1,0:T(8,128)(2,1)S(1)}, u32[]{:S(2)}, u32[]{:S(2)}) %all-to-all-start.2) | async-done | bytes 524320 | tf_op jit(solution)/shard_map/all_to_all | solution.py:310
  137.2 6.7 %all-to-all-start.3 = ((bf16[4,256,256]{2,1,0:T(8,128)(2,1)}), bf16[4,256,256]{2,1,0:T(8,128)(2,1)S(1)}, u32[]{:S(2)}, u32[]{:S(2)}) async-start(bf16[4,256,256]{2,1,0:T(8,128)(2,1)} %broadcast_in_dim.2), calls=%async_computation.3 | async-start | bytes 1048576 | tf_op jit(solution)/shard_map/all_to_all | solution.py:30
  144.0 3.0 %shard_map.86 = (f32[4,256,128]{2,1,0:T(8,128)S(1)}, f32[4,256,128]{2,1,0:T(8,128)S(1)}) custom-call(s32[4]{0:T(128)S(1)} %pad_add_fusion.place, bf16[4,256,128]{2,1,0:T(8,128)(2,1)S(1)} %bitcast.19, bf16[4,256,256]{2,1,0:T(8,128)(2,1)S(1)} %all-to-all-done.2.kv), custom_call_target="tpu_custom_call" | custom-call | flops 536870912 | bytes 2097152 | tf_op jit(solution)/shard_map/pallas_call | solution.py:317
  147.0 10.9 %all-to-all-done.3.kv = bf16[4,256,256]{2,1,0:T(8,128)(2,1)S(1)} async-done(((bf16[4,256,256]{2,1,0:T(8,128)(2,1)}), bf16[4,256,256]{2,1,0:T(8,128)(2,1)S(1)}, u32[]{:S(2)}, u32[]{:S(2)}) %all-to-all-start.3) | async-done | bytes 524320 | tf_op jit(solution)/shard_map/all_to_all | solution.py:30
  158.9 11.7 %all_to_all.25.parts = bf16[8,136,128]{2,1,0:T(8,128)(2,1)S(1)} all-to-all(bf16[8,136,128]{2,1,0:T(8,128)(2,1)S(1)} %shard_map.87), channel_id=1, replica_groups=mesh['zh'=2,'zl'=4,'y'=4,'core'=2,'section'=2,'tp'=4] {'y','core'}, dimensions={0} | all-to-all | bytes 557056 | tf_op jit(solution)/shard_map/all_to_all | solution.py:325
  (29 shorter events, 7.6 us)
Async XLA Ops:
  6.5 58.5 %copy-start.2 = (bf16[4096]{0:T(1024)(128)(2,1)S(1)}, bf16[4096]{0:T(1024)(128)(2,1)}, u32[]{:S(2)}) copy-start(bf16[4096]{0:T(1024)(128)(2,1)} %param.12) | copy-start | bytes 24580
  6.5 58.6 %copy-start = (bf16[1024,512]{1,0:T(8,128)(2,1)S(1)}, bf16[1024,512]{1,0:T(8,128)(2,1)}, u32[]{:S(2)}) copy-start(bf16[1024,512]{1,0:T(8,128)(2,1)} %param.11) | copy-start | bytes 3145732
  6.5 58.6 %copy-start.1 = (bf16[128,512]{1,0:T(8,128)(2,1)S(1)}, bf16[128,512]{1,0:T(8,128)(2,1)}, u32[]{:S(2)}) copy-start(bf16[128,512]{1,0:T(8,128)(2,1)} %text.1) | copy-start | bytes 393220
  8.3 34.9 %all-to-all-start = ((bf16[8,64,384]{2,1,0:T(8,128)(2,1)}), bf16[8,64,384]{2,1,0:T(8,128)(2,1)S(1)}, u32[]{:S(2)}, u32[]{:S(2)}) async-start(bf16[8,64,384]{2,1,0:T(8,128)(2,1)} %get-tuple-element.23), calls=%async_computation | async-start | bytes 786432 | tf_op jit(solution)/shard_map/all_to_all | solution.py:259
  18.5 24.6 %collective-permute-start = (bf16[64,768]{1,0:T(8,128)(2,1)}, bf16[64,768]{1,0:T(8,128)(2,1)S(1)}, u32[]{:S(2)}, u32[]{:S(2)}) collective-permute-start(bf16[64,768]{1,0:T(8,128)(2,1)} %get-tuple-element.24), channel_id=1, source_target_pairs={{0,256},{256,0},{1,257},{257,1},{2,258},{258,2},{3,259},{259,3},{4... | collective-permute-start | bytes 294920 | tf_op jit(solution)/shard_map/ppermute | solution.py:26
  24.5 18.7 %collective-permute-start.1 = (bf16[128,128]{1,0:T(8,128)(2,1)}, bf16[128,128]{1,0:T(8,128)(2,1)S(1)}, u32[]{:S(2)}, u32[]{:S(2)}) collective-permute-start(bf16[128,128]{1,0:T(8,128)(2,1)} %param.9), channel_id=1, source_target_pairs={{0,4},{4,0},{1,5},{5,1},{2,6},{6,2},{3,7},{7,3},{8,12},{12,8},{9,1... | collective-permute-start | bytes 98312 | tf_op jit(solution)/shard_map/ppermute | solution.py:26
  44.0 19.4 %all-to-all-start.1 = ((bf16[8,64,384]{2,1,0:T(8,128)(2,1)}), bf16[8,64,384]{2,1,0:T(8,128)(2,1)S(1)}, u32[]{:S(2)}, u32[]{:S(2)}) async-start(bf16[8,64,384]{2,1,0:T(8,128)(2,1)} %shard_map.83), calls=%async_computation.1 | async-start | bytes 786432 | tf_op jit(solution)/shard_map/all_to_all | solution.py:265
  51.7 56.6 %all-gather.8.cloned.1.call-start = ((), (), s32[]{:S(2)}) async-start(), calls=%async_computation.5 | async-start | bytes 3932160 | tf_op jit(solution)/shard_map/all_gather | solution.py:269
  66.1 21.3 %collective-permute-start.2 = (bf16[128,512]{1,0:T(8,128)(2,1)S(1)}, bf16[128,512]{1,0:T(8,128)(2,1)S(1)}, u32[]{:S(2)}, u32[]{:S(2)}) collective-permute-start(bf16[128,512]{1,0:T(8,128)(2,1)S(1)} %shard_map.84), channel_id=1, source_target_pairs={{0,4},{4,0},{1,5},{5,1},{2,6},{6,2},{3,7},{7,3},{8,12},{12,8},{9,1... | collective-permute-start | bytes 393224 | tf_op jit(solution)/shard_map/ppermute | solution.py:26
  98.5 6.8 %collective-permute-start.4 = (bf16[4,128,512]{2,1,0:T(8,128)(2,1)S(1)}, bf16[4,128,512]{2,1,0:T(8,128)(2,1)S(1)}, u32[]{:S(2)}, u32[]{:S(2)}) collective-permute-start(bf16[4,128,512]{2,1,0:T(8,128)(2,1)S(1)} %bitcast.17), channel_id=1, source_target_pairs={{0,8},{8,0},{1,9},{9,1},{2,10},{10,2},{3,11},{11,3},{4,12},{12,4},... | collective-permute-start | bytes 1572872 | tf_op jit(solution)/shard_map/ppermute | solution.py:26
  102.7 3.8 %collective-permute-start.3 = (bf16[4,128,512]{2,1,0:T(8,128)(2,1)S(1)}, bf16[4,128,512]{2,1,0:T(8,128)(2,1)S(1)}, u32[]{:S(2)}, u32[]{:S(2)}) collective-permute-start(bf16[4,128,512]{2,1,0:T(8,128)(2,1)S(1)} %bitcast.15), channel_id=1, source_target_pairs={{0,8},{8,0},{1,9},{9,1},{2,10},{10,2},{3,11},{11,3},{4,12},{12,4},... | collective-permute-start | bytes 1572872 | tf_op jit(solution)/shard_map/ppermute | solution.py:26
  112.2 24.2 %all-to-all-start.2 = ((bf16[4,256,256]{2,1,0:T(8,128)(2,1)}), bf16[4,256,256]{2,1,0:T(8,128)(2,1)S(1)}, u32[]{:S(2)}, u32[]{:S(2)}) async-start(bf16[4,256,256]{2,1,0:T(8,128)(2,1)} %get-tuple-element.33), calls=%async_computation.2 | async-start | bytes 1048576 | tf_op jit(solution)/shard_map/all_to_all | solution.py:310
  116.7 17.0 %collective-permute-start.5 = (bf16[256,256]{1,0:T(8,128)(2,1)S(1)}, bf16[256,256]{1,0:T(8,128)(2,1)S(1)}, u32[]{:S(2)}, u32[]{:S(2)}) collective-permute-start(bf16[256,256]{1,0:T(8,128)(2,1)S(1)} %get-tuple-element.34), channel_id=1, source_target_pairs={{0,256},{256,0},{1,257},{257,1},{2,258},{258,2},{3,259},{259,3},{4... | collective-permute-start | bytes 393224 | tf_op jit(solution)/shard_map/ppermute | solution.py:26
  137.2 20.7 %all-to-all-start.3 = ((bf16[4,256,256]{2,1,0:T(8,128)(2,1)}), bf16[4,256,256]{2,1,0:T(8,128)(2,1)S(1)}, u32[]{:S(2)}, u32[]{:S(2)}) async-start(bf16[4,256,256]{2,1,0:T(8,128)(2,1)} %broadcast_in_dim.2), calls=%async_computation.3 | async-start | bytes 1048576 | tf_op jit(solution)/shard_map/all_to_all | solution.py:30
Sparse Core Ops, SparseCore 0:
  64.5 43.7 all-gather.7

commit v9 on v7

--- a/solution.py
+++ b/solution.py
@@ -44,7 +44,7 @@
 
 
 def project_kernel(
-    flip, own_a, own_b, other_a, other_b, stored, gain, cosine, sine, q_out, kv_out, lines_out, weight, sem
+    flip, own_a, own_b, other_a, other_b, stored, gain, cosine, sine, q_out, kv_out, lines_out, weight, sem, normed
 ):
     copies = [
         pltpu.make_async_copy(
@@ -63,17 +63,18 @@
         squares = squares + wide * wide
     mean_square = jnp.sum(squares, axis=-1, keepdims=True) * (1.0 / 4096)
     inverse = lax.rsqrt(mean_square + NORM_EPS)
+    for i, (own, other, t) in enumerate(tiles):
+        wide = jnp.concatenate([own[t], other[t]], axis=0).astype(jnp.float32)
+        normed[i] = (wide * inverse * gain[i : i + 1, :]).astype(jnp.bfloat16)
+    for copy in copies:
+        copy.wait()
     total = jnp.zeros((CHIP_ROWS, 3 * HD), jnp.float32)
-    for i, (own, other, t) in enumerate(tiles):
-        if i < TP:
-            copies[i].wait()
+    for i, (_, _, t) in enumerate(tiles):
         half = jnp.bitwise_xor(flip[0], i // TP)
-        wide = jnp.concatenate([own[t], other[t]], axis=0).astype(jnp.float32)
-        normed = (wide * inverse * gain[i : i + 1, :]).astype(jnp.bfloat16)
         block = jnp.concatenate(
             [weight[y, half, t * CORES + c] for y in range(Y) for c in range(CORES)], axis=0
         )
-        total = total + jnp.dot(normed, block, preferred_element_type=jnp.float32)
+        total = total + jnp.dot(normed[i], block, preferred_element_type=jnp.float32)
     q = total[:, :HD]
     k = total[:, HD : 2 * HD]
     cos, sin = cosine[...], sine[...]
@@ -286,6 +287,7 @@
         scratch_shapes=[
             pltpu.VMEM((Y, ZH, ZL * CORES, 64, 3 * HD), jnp.bfloat16),
             pltpu.SemaphoreType.DMA((TP,)),
+            pltpu.VMEM((SECTIONS * TP, CHIP_ROWS, 512), jnp.bfloat16),
         ],
         compiler_params=pltpu.CompilerParams(vmem_limit_bytes=LIMIT),
         cost_estimate=pl.CostEstimate(

time: 177 us -> 178 us (level)
  no operation moved by 1% of the time
where the time goes in v9:
time: 178 us; the launch traced here: 177 us
  starting transfers between devices  67 us (38%)
  blocking collectives  57.6 us (32%)
  waiting for transfers between devices  22 us (12%)
  between operations  14.2 us (8%)
  Pallas kernels  12.5 us (7%)
  other arithmetic  2.59 us (1%)
    ppermute x6, starting transfers between devices, swap(): return lax.ppermute(v, axis, SWAP)  36.8 us
    all_gather x1, blocking collectives, local(): own_b = lax.all_gather(joined_b, 'tp', axis=0)  15.6 us
    all_to_all x1, blocking collectives, local(): parts = lax.all_to_all(parts, ('y', 'core'), 0, 0, tiled=True)  11.7 us
    all_gather x1, blocking collectives, local(): own_a = lax.all_gather(joined, 'tp', axis=0)  11.1 us
    all_to_all x1, waiting for transfers between devices, gather(): lax.all_to_all(jnp.broadcast_to(v[None], (n, *v.shape)), axis, 0, 0, tile...  10.9 us
    all_to_all x1, starting transfers between devices, local(): weight_a = lax.all_to_all(spread, ('zl', 'core'), 0, 0, tiled=True)  10.2 us
    all_gather x1, blocking collectives, local(): queries = lax.all_gather(queries, 'y', axis=0)  9.67 us
    all_gather x1, blocking collectives, local(): feats = lax.all_gather(jnp.stack([feats, feats_b]), 'tp', axis=0)  9.51 us
  transfers between devices with their start and end apart: 11, of which 6 were waited for; matrix products, arithmetic and copies ran while one was open for 1% of the time, Pallas kernels for 2%

profile of v9, /device:TPU:1, one launch (start us, length us, event | category | flops | bytes accessed | tf_op | source)
XLA Modules:
  0.0 176.8 jit_solution(8096560348956032340)
XLA Ops:
  6.5 1.7 shard_map.82
  8.3 10.2 %all-to-all-start = ((bf16[8,64,384]{2,1,0:T(8,128)(2,1)}), bf16[8,64,384]{2,1,0:T(8,128)(2,1)S(1)}, u32[]{:S(2)}, u32[]{:S(2)}) async-start(bf16[8,64,384]{2,1,0:T(8,128)(2,1)} %get-tuple-element.22), calls=%async_computation | async-start | bytes 786432 | tf_op jit(solution)/shard_map/all_to_all | solution.py:260
  18.5 6.0 %collective-permute-start = (bf16[64,768]{1,0:T(8,128)(2,1)}, bf16[64,768]{1,0:T(8,128)(2,1)S(1)}, u32[]{:S(2)}, u32[]{:S(2)}) collective-permute-start(bf16[64,768]{1,0:T(8,128)(2,1)} %get-tuple-element.23), channel_id=1, source_target_pairs={{0,256},{256,0},{1,257},{257,1},{2,258},{258,2},{3,259},{259,3},{4... | collective-permute-start | bytes 294920 | tf_op jit(solution)/shard_map/ppermute | solution.py:26
  24.5 8.1 %collective-permute-start.1 = (bf16[128,128]{1,0:T(8,128)(2,1)}, bf16[128,128]{1,0:T(8,128)(2,1)S(1)}, u32[]{:S(2)}, u32[]{:S(2)}) collective-permute-start(bf16[128,128]{1,0:T(8,128)(2,1)} %param.9), channel_id=1, source_target_pairs={{0,4},{4,0},{1,5},{5,1},{2,6},{6,2},{3,7},{7,3},{8,12},{12,8},{9,1... | collective-permute-start | bytes 98312 | tf_op jit(solution)/shard_map/ppermute | solution.py:26
  32.6 5.6 %collective-permute-done.1 = bf16[128,128]{1,0:T(8,128)(2,1)S(1)} collective-permute-done((bf16[128,128]{1,0:T(8,128)(2,1)}, bf16[128,128]{1,0:T(8,128)(2,1)S(1)}, u32[]{:S(2)}, u32[]{:S(2)}) %collective-permute-start.1) | collective-permute-done | bytes 32800 | tf_op jit(solution)/shard_map/ppermute | solution.py:26
  39.0 8.7 %all-to-all-start.1 = ((bf16[8,64,384]{2,1,0:T(8,128)(2,1)}), bf16[8,64,384]{2,1,0:T(8,128)(2,1)S(1)}, u32[]{:S(2)}, u32[]{:S(2)}) async-start(bf16[8,64,384]{2,1,0:T(8,128)(2,1)} %shard_map.83), calls=%async_computation.1 | async-start | bytes 786432 | tf_op jit(solution)/shard_map/all_to_all | solution.py:263
  48.5 9.5 %all-gather = bf16[8,128,128]{2,1,0:T(8,128)(2,1)S(1)} all-gather(bf16[2,128,128]{2,1,0:T(8,128)(2,1)S(1)} %pad_maximum_fusion.3), channel_id=2, replica_groups=mesh['zh'=2,'zl'=4,'y'=4,'core'=2,'section'=2,'tp'=4] {'tp'}, dimensions={0}, use_global_device_ids=true | all-gather | bytes 327680 | tf_op jit(solution)/shard_map/all_gather | solution.py:265
  58.0 1.4 all-to-all-done.1
  62.2 8.3 %collective-permute-start.2 = (bf16[128,512]{1,0:T(8,128)(2,1)S(1)}, bf16[128,512]{1,0:T(8,128)(2,1)S(1)}, u32[]{:S(2)}, u32[]{:S(2)}) collective-permute-start(bf16[128,512]{1,0:T(8,128)(2,1)S(1)} %shard_map.84), channel_id=1, source_target_pairs={{0,4},{4,0},{1,5},{5,1},{2,6},{6,2},{3,7},{7,3},{8,12},{12,8},{9,1... | collective-permute-start | bytes 393224 | tf_op jit(solution)/shard_map/ppermute | solution.py:26
  70.5 11.1 %all-gather.1 = bf16[512,512]{1,0:T(8,128)(2,1)S(1)} all-gather(bf16[128,512]{1,0:T(8,128)(2,1)S(1)} %shard_map.84), channel_id=3, replica_groups=mesh['zh'=2,'zl'=4,'y'=4,'core'=2,'section'=2,'tp'=4] {'tp'}, dimensions={0}, use_global_device_ids=true | all-gather | bytes 655360 | tf_op jit(solution)/shard_map/all_gather | solution.py:273
  81.6 15.6 %all-gather.2 = bf16[512,512]{1,0:T(8,128)(2,1)S(1)} all-gather(bf16[128,512]{1,0:T(8,128)(2,1)S(1)} %collective-permute-done.2), channel_id=4, replica_groups=mesh['zh'=2,'zl'=4,'y'=4,'core'=2,'section'=2,'tp'=4] {'tp'}, dimensions={0}, use_global_device_ids=true | all-gather | bytes 655360 | tf_op jit(solution)/shard_map/all_gather | solution.py:276
  97.2 5.1 %collective-permute-start.4 = (bf16[4,128,512]{2,1,0:T(8,128)(2,1)S(1)}, bf16[4,128,512]{2,1,0:T(8,128)(2,1)S(1)}, u32[]{:S(2)}, u32[]{:S(2)}) collective-permute-start(bf16[4,128,512]{2,1,0:T(8,128)(2,1)S(1)} %bitcast.18), channel_id=1, source_target_pairs={{0,8},{8,0},{1,9},{9,1},{2,10},{10,2},{3,11},{11,3},{4,12},{12,4},... | collective-permute-start | bytes 1572872 | tf_op jit(solution)/shard_map/ppermute | solution.py:26
  102.3 1.9 %collective-permute-start.3 = (bf16[4,128,512]{2,1,0:T(8,128)(2,1)S(1)}, bf16[4,128,512]{2,1,0:T(8,128)(2,1)S(1)}, u32[]{:S(2)}, u32[]{:S(2)}) collective-permute-start(bf16[4,128,512]{2,1,0:T(8,128)(2,1)S(1)} %bitcast.16), channel_id=1, source_target_pairs={{0,8},{8,0},{1,9},{9,1},{2,10},{10,2},{3,11},{11,3},{4,12},{12,4},... | collective-permute-start | bytes 1572872 | tf_op jit(solution)/shard_map/ppermute | solution.py:26
  105.0 1.2 collective-permute-done.3.other_a
  106.4 4.1 %shard_map.85 = (bf16[256,128]{1,0:T(8,128)(2,1)S(1)}, bf16[256,256]{1,0:T(8,128)(2,1)S(1)}, bf16[4,256,256]{2,1,0:T(8,128)(2,1)}) custom-call(s32[1]{0:T(128)} %bitcast.4.flip, bf16[4,128,512]{2,1,0:T(8,128)(2,1)S(1)} %bitcast.17, bf16[4,128,512]{2,1,0:T(8,128)(2,1)S(1)} %bitcast.19, bf16[4,128,512]{2,1,0:T(8,128)(2,1)S(1)} %collective-permute-done.3.other_a, ...), custom_call_target="tpu_custom_call" | custom-call | flops 805306368 | bytes 6291456 | tf_op jit(solution)/shard_map/pallas_call | solution.py:278
  110.6 4.5 %all-to-all-start.2 = ((bf16[4,256,256]{2,1,0:T(8,128)(2,1)}), bf16[4,256,256]{2,1,0:T(8,128)(2,1)S(1)}, u32[]{:S(2)}, u32[]{:S(2)}) async-start(bf16[4,256,256]{2,1,0:T(8,128)(2,1)} %get-tuple-element.31), calls=%async_computation.2 | async-start | bytes 1048576 | tf_op jit(solution)/shard_map/all_to_all | solution.py:309
  115.1 7.4 %collective-permute-start.5 = (bf16[256,256]{1,0:T(8,128)(2,1)S(1)}, bf16[256,256]{1,0:T(8,128)(2,1)S(1)}, u32[]{:S(2)}, u32[]{:S(2)}) collective-permute-start(bf16[256,256]{1,0:T(8,128)(2,1)S(1)} %get-tuple-element.32), channel_id=1, source_target_pairs={{0,256},{256,0},{1,257},{257,1},{2,258},{258,2},{3,259},{259,3},{4... | collective-permute-start | bytes 393224 | tf_op jit(solution)/shard_map/ppermute | solution.py:26
  122.5 9.7 %all-gather.4 = bf16[1024,128]{1,0:T(8,128)(2,1)S(1)} all-gather(bf16[256,128]{1,0:T(8,128)(2,1)S(1)} %get-tuple-element.33), channel_id=6, replica_groups=mesh['zh'=2,'zl'=4,'y'=4,'core'=2,'section'=2,'tp'=4] {'y'}, dimensions={0}, use_global_device_ids=true | all-gather | bytes 327680 | tf_op jit(solution)/shard_map/all_gather | solution.py:310
  132.2 2.6 %all-to-all-done.2.kv = bf16[4,256,256]{2,1,0:T(8,128)(2,1)S(1)} async-done(((bf16[4,256,256]{2,1,0:T(8,128)(2,1)}), bf16[4,256,256]{2,1,0:T(8,128)(2,1)S(1)}, u32[]{:S(2)}, u32[]{:S(2)}) %all-to-all-start.2) | async-done | bytes 524320 | tf_op jit(solution)/shard_map/all_to_all | solution.py:309
  135.6 6.7 %all-to-all-start.3 = ((bf16[4,256,256]{2,1,0:T(8,128)(2,1)}), bf16[4,256,256]{2,1,0:T(8,128)(2,1)S(1)}, u32[]{:S(2)}, u32[]{:S(2)}) async-start(bf16[4,256,256]{2,1,0:T(8,128)(2,1)} %broadcast_in_dim.2), calls=%async_computation.3 | async-start | bytes 1048576 | tf_op jit(solution)/shard_map/all_to_all | solution.py:30
  142.4 3.0 %shard_map.86 = (f32[4,256,128]{2,1,0:T(8,128)S(1)}, f32[4,256,128]{2,1,0:T(8,128)S(1)}) custom-call(s32[4]{0:T(128)S(1)} %pad_add_fusion.place, bf16[4,256,128]{2,1,0:T(8,128)(2,1)S(1)} %bitcast.20, bf16[4,256,256]{2,1,0:T(8,128)(2,1)S(1)} %all-to-all-done.2.kv), custom_call_target="tpu_custom_call" | custom-call | flops 536870912 | bytes 2097152 | tf_op jit(solution)/shard_map/pallas_call | solution.py:316
  145.4 10.9 %all-to-all-done.3.kv = bf16[4,256,256]{2,1,0:T(8,128)(2,1)S(1)} async-done(((bf16[4,256,256]{2,1,0:T(8,128)(2,1)}), bf16[4,256,256]{2,1,0:T(8,128)(2,1)S(1)}, u32[]{:S(2)}, u32[]{:S(2)}) %all-to-all-start.3) | async-done | bytes 524320 | tf_op jit(solution)/shard_map/all_to_all | solution.py:30
  157.3 11.7 %all_to_all.25.parts = bf16[8,136,128]{2,1,0:T(8,128)(2,1)S(1)} all-to-all(bf16[8,136,128]{2,1,0:T(8,128)(2,1)S(1)} %shard_map.87), channel_id=1, replica_groups=mesh['zh'=2,'zl'=4,'y'=4,'core'=2,'section'=2,'tp'=4] {'y','core'}, dimensions={0} | all-to-all | bytes 557056 | tf_op jit(solution)/shard_map/all_to_all | solution.py:324
  168.9 1.0 shard_map.88
  (29 shorter events, 6.5 us)
Async XLA Ops:
  6.5 54.5 %copy-start.2 = (bf16[4096]{0:T(1024)(128)(2,1)S(1)}, bf16[4096]{0:T(1024)(128)(2,1)}, u32[]{:S(2)}) copy-start(bf16[4096]{0:T(1024)(128)(2,1)} %param.12) | copy-start | bytes 24580
  6.5 54.6 %copy-start = (bf16[1024,512]{1,0:T(8,128)(2,1)S(1)}, bf16[1024,512]{1,0:T(8,128)(2,1)}, u32[]{:S(2)}) copy-start(bf16[1024,512]{1,0:T(8,128)(2,1)} %param.11) | copy-start | bytes 3145732
  6.5 54.6 %copy-start.1 = (bf16[128,512]{1,0:T(8,128)(2,1)S(1)}, bf16[128,512]{1,0:T(8,128)(2,1)}, u32[]{:S(2)}) copy-start(bf16[128,512]{1,0:T(8,128)(2,1)} %text.1) | copy-start | bytes 393220
  8.3 29.9 %all-to-all-start = ((bf16[8,64,384]{2,1,0:T(8,128)(2,1)}), bf16[8,64,384]{2,1,0:T(8,128)(2,1)S(1)}, u32[]{:S(2)}, u32[]{:S(2)}) async-start(bf16[8,64,384]{2,1,0:T(8,128)(2,1)} %get-tuple-element.22), calls=%async_computation | async-start | bytes 786432 | tf_op jit(solution)/shard_map/all_to_all | solution.py:260
  18.5 19.7 %collective-permute-start = (bf16[64,768]{1,0:T(8,128)(2,1)}, bf16[64,768]{1,0:T(8,128)(2,1)S(1)}, u32[]{:S(2)}, u32[]{:S(2)}) collective-permute-start(bf16[64,768]{1,0:T(8,128)(2,1)} %get-tuple-element.23), channel_id=1, source_target_pairs={{0,256},{256,0},{1,257},{257,1},{2,258},{258,2},{3,259},{259,3},{4... | collective-permute-start | bytes 294920 | tf_op jit(solution)/shard_map/ppermute | solution.py:26
  24.5 13.7 %collective-permute-start.1 = (bf16[128,128]{1,0:T(8,128)(2,1)}, bf16[128,128]{1,0:T(8,128)(2,1)S(1)}, u32[]{:S(2)}, u32[]{:S(2)}) collective-permute-start(bf16[128,128]{1,0:T(8,128)(2,1)} %param.9), channel_id=1, source_target_pairs={{0,4},{4,0},{1,5},{5,1},{2,6},{6,2},{3,7},{7,3},{8,12},{12,8},{9,1... | collective-permute-start | bytes 98312 | tf_op jit(solution)/shard_map/ppermute | solution.py:26
  39.0 20.4 %all-to-all-start.1 = ((bf16[8,64,384]{2,1,0:T(8,128)(2,1)}), bf16[8,64,384]{2,1,0:T(8,128)(2,1)S(1)}, u32[]{:S(2)}, u32[]{:S(2)}) async-start(bf16[8,64,384]{2,1,0:T(8,128)(2,1)} %shard_map.83), calls=%async_computation.1 | async-start | bytes 786432 | tf_op jit(solution)/shard_map/all_to_all | solution.py:263
  47.7 58.8 %all-gather.7.cloned.1.call-start = ((), (), s32[]{:S(2)}) async-start(), calls=%async_computation.5 | async-start | bytes 3932160 | tf_op jit(solution)/shard_map/all_gather | solution.py:267
  62.2 19.5 %collective-permute-start.2 = (bf16[128,512]{1,0:T(8,128)(2,1)S(1)}, bf16[128,512]{1,0:T(8,128)(2,1)S(1)}, u32[]{:S(2)}, u32[]{:S(2)}) collective-permute-start(bf16[128,512]{1,0:T(8,128)(2,1)S(1)} %shard_map.84), channel_id=1, source_target_pairs={{0,4},{4,0},{1,5},{5,1},{2,6},{6,2},{3,7},{7,3},{8,12},{12,8},{9,1... | collective-permute-start | bytes 393224 | tf_op jit(solution)/shard_map/ppermute | solution.py:26
  97.2 7.7 %collective-permute-start.4 = (bf16[4,128,512]{2,1,0:T(8,128)(2,1)S(1)}, bf16[4,128,512]{2,1,0:T(8,128)(2,1)S(1)}, u32[]{:S(2)}, u32[]{:S(2)}) collective-permute-start(bf16[4,128,512]{2,1,0:T(8,128)(2,1)S(1)} %bitcast.18), channel_id=1, source_target_pairs={{0,8},{8,0},{1,9},{9,1},{2,10},{10,2},{3,11},{11,3},{4,12},{12,4},... | collective-permute-start | bytes 1572872 | tf_op jit(solution)/shard_map/ppermute | solution.py:26
  102.3 3.8 %collective-permute-start.3 = (bf16[4,128,512]{2,1,0:T(8,128)(2,1)S(1)}, bf16[4,128,512]{2,1,0:T(8,128)(2,1)S(1)}, u32[]{:S(2)}, u32[]{:S(2)}) collective-permute-start(bf16[4,128,512]{2,1,0:T(8,128)(2,1)S(1)} %bitcast.16), channel_id=1, source_target_pairs={{0,8},{8,0},{1,9},{9,1},{2,10},{10,2},{3,11},{11,3},{4,12},{12,4},... | collective-permute-start | bytes 1572872 | tf_op jit(solution)/shard_map/ppermute | solution.py:26
  110.6 24.2 %all-to-all-start.2 = ((bf16[4,256,256]{2,1,0:T(8,128)(2,1)}), bf16[4,256,256]{2,1,0:T(8,128)(2,1)S(1)}, u32[]{:S(2)}, u32[]{:S(2)}) async-start(bf16[4,256,256]{2,1,0:T(8,128)(2,1)} %get-tuple-element.31), calls=%async_computation.2 | async-start | bytes 1048576 | tf_op jit(solution)/shard_map/all_to_all | solution.py:309
  115.1 17.0 %collective-permute-start.5 = (bf16[256,256]{1,0:T(8,128)(2,1)S(1)}, bf16[256,256]{1,0:T(8,128)(2,1)S(1)}, u32[]{:S(2)}, u32[]{:S(2)}) collective-permute-start(bf16[256,256]{1,0:T(8,128)(2,1)S(1)} %get-tuple-element.32), channel_id=1, source_target_pairs={{0,256},{256,0},{1,257},{257,1},{2,258},{258,2},{3,259},{259,3},{4... | collective-permute-start | bytes 393224 | tf_op jit(solution)/shard_map/ppermute | solution.py:26
  135.6 20.7 %all-to-all-start.3 = ((bf16[4,256,256]{2,1,0:T(8,128)(2,1)}), bf16[4,256,256]{2,1,0:T(8,128)(2,1)S(1)}, u32[]{:S(2)}, u32[]{:S(2)}) async-start(bf16[4,256,256]{2,1,0:T(8,128)(2,1)} %broadcast_in_dim.2), calls=%async_computation.3 | async-start | bytes 1048576 | tf_op jit(solution)/shard_map/all_to_all | solution.py:30
Sparse Core Ops, SparseCore 0:
  60.5 45.9 all-gather.6

commit v10 on v9

--- a/solution.py
+++ b/solution.py
@@ -66,10 +66,10 @@
     for i, (own, other, t) in enumerate(tiles):
         wide = jnp.concatenate([own[t], other[t]], axis=0).astype(jnp.float32)
         normed[i] = (wide * inverse * gain[i : i + 1, :]).astype(jnp.bfloat16)
-    for copy in copies:
-        copy.wait()
     total = jnp.zeros((CHIP_ROWS, 3 * HD), jnp.float32)
     for i, (_, _, t) in enumerate(tiles):
+        if i < TP:
+            copies[i].wait()
         half = jnp.bitwise_xor(flip[0], i // TP)
         block = jnp.concatenate(
             [weight[y, half, t * CORES + c] for y in range(Y) for c in range(CORES)], axis=0

time: 178 us -> 177 us (level)
  no operation moved by 1% of the time
where the time goes in v10:
time: 177 us
  starting transfers between devices  67 us (38%)
  blocking collectives  57.6 us (33%)
  waiting for transfers between devices  22 us (12%)
  between operations  14.2 us (8%)
  Pallas kernels  12.3 us (7%)
  other arithmetic  2.59 us (1%)
    ppermute x6, starting transfers between devices, swap(): return lax.ppermute(v, axis, SWAP)  36.8 us
    all_gather x1, blocking collectives, local(): own_b = lax.all_gather(joined_b, 'tp', axis=0)  15.6 us
    all_to_all x1, blocking collectives, local(): parts = lax.all_to_all(parts, ('y', 'core'), 0, 0, tiled=True)  11.7 us
    all_gather x1, blocking collectives, local(): own_a = lax.all_gather(joined, 'tp', axis=0)  11.1 us
    all_to_all x1, waiting for transfers between devices, gather(): lax.all_to_all(jnp.broadcast_to(v[None], (n, *v.shape)), axis, 0, 0, tile...  10.9 us
    all_to_all x1, starting transfers between devices, local(): weight_a = lax.all_to_all(spread, ('zl', 'core'), 0, 0, tiled=True)  10.2 us
    all_gather x1, blocking collectives, local(): queries = lax.all_gather(queries, 'y', axis=0)  9.67 us
    all_gather x1, blocking collectives, local(): feats = lax.all_gather(jnp.stack([feats, feats_b]), 'tp', axis=0)  9.51 us
  transfers between devices with their start and end apart: 11, of which 6 were waited for; matrix products, arithmetic and copies ran while one was open for 1% of the time, Pallas kernels for 2%

profile of v10, /device:TPU:1, one launch (start us, length us, event | category | flops | bytes accessed | tf_op | source)
XLA Modules:
  0.0 176.6 jit_solution(9859826405748959498)
XLA Ops:
  6.5 1.7 shard_map.82
  8.3 10.2 %all-to-all-start = ((bf16[8,64,384]{2,1,0:T(8,128)(2,1)}), bf16[8,64,384]{2,1,0:T(8,128)(2,1)S(1)}, u32[]{:S(2)}, u32[]{:S(2)}) async-start(bf16[8,64,384]{2,1,0:T(8,128)(2,1)} %get-tuple-element.22), calls=%async_computation | async-start | bytes 786432 | tf_op jit(solution)/shard_map/all_to_all | solution.py:260
  18.5 6.0 %collective-permute-start = (bf16[64,768]{1,0:T(8,128)(2,1)}, bf16[64,768]{1,0:T(8,128)(2,1)S(1)}, u32[]{:S(2)}, u32[]{:S(2)}) collective-permute-start(bf16[64,768]{1,0:T(8,128)(2,1)} %get-tuple-element.23), channel_id=1, source_target_pairs={{0,256},{256,0},{1,257},{257,1},{2,258},{258,2},{3,259},{259,3},{4... | collective-permute-start | bytes 294920 | tf_op jit(solution)/shard_map/ppermute | solution.py:26
  24.5 8.1 %collective-permute-start.1 = (bf16[128,128]{1,0:T(8,128)(2,1)}, bf16[128,128]{1,0:T(8,128)(2,1)S(1)}, u32[]{:S(2)}, u32[]{:S(2)}) collective-permute-start(bf16[128,128]{1,0:T(8,128)(2,1)} %param.9), channel_id=1, source_target_pairs={{0,4},{4,0},{1,5},{5,1},{2,6},{6,2},{3,7},{7,3},{8,12},{12,8},{9,1... | collective-permute-start | bytes 98312 | tf_op jit(solution)/shard_map/ppermute | solution.py:26
  32.6 5.6 %collective-permute-done.1 = bf16[128,128]{1,0:T(8,128)(2,1)S(1)} collective-permute-done((bf16[128,128]{1,0:T(8,128)(2,1)}, bf16[128,128]{1,0:T(8,128)(2,1)S(1)}, u32[]{:S(2)}, u32[]{:S(2)}) %collective-permute-start.1) | collective-permute-done | bytes 32800 | tf_op jit(solution)/shard_map/ppermute | solution.py:26
  39.0 8.7 %all-to-all-start.1 = ((bf16[8,64,384]{2,1,0:T(8,128)(2,1)}), bf16[8,64,384]{2,1,0:T(8,128)(2,1)S(1)}, u32[]{:S(2)}, u32[]{:S(2)}) async-start(bf16[8,64,384]{2,1,0:T(8,128)(2,1)} %shard_map.83), calls=%async_computation.1 | async-start | bytes 786432 | tf_op jit(solution)/shard_map/all_to_all | solution.py:263
  48.5 9.5 %all-gather = bf16[8,128,128]{2,1,0:T(8,128)(2,1)S(1)} all-gather(bf16[2,128,128]{2,1,0:T(8,128)(2,1)S(1)} %pad_maximum_fusion.3), channel_id=2, replica_groups=mesh['zh'=2,'zl'=4,'y'=4,'core'=2,'section'=2,'tp'=4] {'tp'}, dimensions={0}, use_global_device_ids=true | all-gather | bytes 327680 | tf_op jit(solution)/shard_map/all_gather | solution.py:265
  58.0 1.4 all-to-all-done.1
  62.2 8.3 %collective-permute-start.2 = (bf16[128,512]{1,0:T(8,128)(2,1)S(1)}, bf16[128,512]{1,0:T(8,128)(2,1)S(1)}, u32[]{:S(2)}, u32[]{:S(2)}) collective-permute-start(bf16[128,512]{1,0:T(8,128)(2,1)S(1)} %shard_map.84), channel_id=1, source_target_pairs={{0,4},{4,0},{1,5},{5,1},{2,6},{6,2},{3,7},{7,3},{8,12},{12,8},{9,1... | collective-permute-start | bytes 393224 | tf_op jit(solution)/shard_map/ppermute | solution.py:26
  70.5 11.1 %all-gather.1 = bf16[512,512]{1,0:T(8,128)(2,1)S(1)} all-gather(bf16[128,512]{1,0:T(8,128)(2,1)S(1)} %shard_map.84), channel_id=3, replica_groups=mesh['zh'=2,'zl'=4,'y'=4,'core'=2,'section'=2,'tp'=4] {'tp'}, dimensions={0}, use_global_device_ids=true | all-gather | bytes 655360 | tf_op jit(solution)/shard_map/all_gather | solution.py:273
  81.6 15.6 %all-gather.2 = bf16[512,512]{1,0:T(8,128)(2,1)S(1)} all-gather(bf16[128,512]{1,0:T(8,128)(2,1)S(1)} %collective-permute-done.2), channel_id=4, replica_groups=mesh['zh'=2,'zl'=4,'y'=4,'core'=2,'section'=2,'tp'=4] {'tp'}, dimensions={0}, use_global_device_ids=true | all-gather | bytes 655360 | tf_op jit(solution)/shard_map/all_gather | solution.py:276
  97.2 5.1 %collective-permute-start.4 = (bf16[4,128,512]{2,1,0:T(8,128)(2,1)S(1)}, bf16[4,128,512]{2,1,0:T(8,128)(2,1)S(1)}, u32[]{:S(2)}, u32[]{:S(2)}) collective-permute-start(bf16[4,128,512]{2,1,0:T(8,128)(2,1)S(1)} %bitcast.18), channel_id=1, source_target_pairs={{0,8},{8,0},{1,9},{9,1},{2,10},{10,2},{3,11},{11,3},{4,12},{12,4},... | collective-permute-start | bytes 1572872 | tf_op jit(solution)/shard_map/ppermute | solution.py:26
  102.3 1.9 %collective-permute-start.3 = (bf16[4,128,512]{2,1,0:T(8,128)(2,1)S(1)}, bf16[4,128,512]{2,1,0:T(8,128)(2,1)S(1)}, u32[]{:S(2)}, u32[]{:S(2)}) collective-permute-start(bf16[4,128,512]{2,1,0:T(8,128)(2,1)S(1)} %bitcast.16), channel_id=1, source_target_pairs={{0,8},{8,0},{1,9},{9,1},{2,10},{10,2},{3,11},{11,3},{4,12},{12,4},... | collective-permute-start | bytes 1572872 | tf_op jit(solution)/shard_map/ppermute | solution.py:26
  105.0 1.2 collective-permute-done.3.other_a
  106.4 3.9 %shard_map.85 = (bf16[256,128]{1,0:T(8,128)(2,1)S(1)}, bf16[256,256]{1,0:T(8,128)(2,1)S(1)}, bf16[4,256,256]{2,1,0:T(8,128)(2,1)}) custom-call(s32[1]{0:T(128)} %bitcast.4.flip, bf16[4,128,512]{2,1,0:T(8,128)(2,1)S(1)} %bitcast.17, bf16[4,128,512]{2,1,0:T(8,128)(2,1)S(1)} %bitcast.19, bf16[4,128,512]{2,1,0:T(8,128)(2,1)S(1)} %collective-permute-done.3.other_a, ...), custom_call_target="tpu_custom_call" | custom-call | flops 805306368 | bytes 6291456 | tf_op jit(solution)/shard_map/pallas_call | solution.py:278
  110.4 4.5 %all-to-all-start.2 = ((bf16[4,256,256]{2,1,0:T(8,128)(2,1)}), bf16[4,256,256]{2,1,0:T(8,128)(2,1)S(1)}, u32[]{:S(2)}, u32[]{:S(2)}) async-start(bf16[4,256,256]{2,1,0:T(8,128)(2,1)} %get-tuple-element.31), calls=%async_computation.2 | async-start | bytes 1048576 | tf_op jit(solution)/shard_map/all_to_all | solution.py:309
  114.9 7.4 %collective-permute-start.5 = (bf16[256,256]{1,0:T(8,128)(2,1)S(1)}, bf16[256,256]{1,0:T(8,128)(2,1)S(1)}, u32[]{:S(2)}, u32[]{:S(2)}) collective-permute-start(bf16[256,256]{1,0:T(8,128)(2,1)S(1)} %get-tuple-element.32), channel_id=1, source_target_pairs={{0,256},{256,0},{1,257},{257,1},{2,258},{258,2},{3,259},{259,3},{4... | collective-permute-start | bytes 393224 | tf_op jit(solution)/shard_map/ppermute | solution.py:26
  122.3 9.7 %all-gather.4 = bf16[1024,128]{1,0:T(8,128)(2,1)S(1)} all-gather(bf16[256,128]{1,0:T(8,128)(2,1)S(1)} %get-tuple-element.33), channel_id=6, replica_groups=mesh['zh'=2,'zl'=4,'y'=4,'core'=2,'section'=2,'tp'=4] {'y'}, dimensions={0}, use_global_device_ids=true | all-gather | bytes 327680 | tf_op jit(solution)/shard_map/all_gather | solution.py:310
  132.0 2.6 %all-to-all-done.2.kv = bf16[4,256,256]{2,1,0:T(8,128)(2,1)S(1)} async-done(((bf16[4,256,256]{2,1,0:T(8,128)(2,1)}), bf16[4,256,256]{2,1,0:T(8,128)(2,1)S(1)}, u32[]{:S(2)}, u32[]{:S(2)}) %all-to-all-start.2) | async-done | bytes 524320 | tf_op jit(solution)/shard_map/all_to_all | solution.py:309
  135.4 6.7 %all-to-all-start.3 = ((bf16[4,256,256]{2,1,0:T(8,128)(2,1)}), bf16[4,256,256]{2,1,0:T(8,128)(2,1)S(1)}, u32[]{:S(2)}, u32[]{:S(2)}) async-start(bf16[4,256,256]{2,1,0:T(8,128)(2,1)} %broadcast_in_dim.2), calls=%async_computation.3 | async-start | bytes 1048576 | tf_op jit(solution)/shard_map/all_to_all | solution.py:30
  142.2 3.0 %shard_map.86 = (f32[4,256,128]{2,1,0:T(8,128)S(1)}, f32[4,256,128]{2,1,0:T(8,128)S(1)}) custom-call(s32[4]{0:T(128)S(1)} %pad_add_fusion.place, bf16[4,256,128]{2,1,0:T(8,128)(2,1)S(1)} %bitcast.20, bf16[4,256,256]{2,1,0:T(8,128)(2,1)S(1)} %all-to-all-done.2.kv), custom_call_target="tpu_custom_call" | custom-call | flops 536870912 | bytes 2097152 | tf_op jit(solution)/shard_map/pallas_call | solution.py:316
  145.2 10.9 %all-to-all-done.3.kv = bf16[4,256,256]{2,1,0:T(8,128)(2,1)S(1)} async-done(((bf16[4,256,256]{2,1,0:T(8,128)(2,1)}), bf16[4,256,256]{2,1,0:T(8,128)(2,1)S(1)}, u32[]{:S(2)}, u32[]{:S(2)}) %all-to-all-start.3) | async-done | bytes 524320 | tf_op jit(solution)/shard_map/all_to_all | solution.py:30
  157.1 11.7 %all_to_all.25.parts = bf16[8,136,128]{2,1,0:T(8,128)(2,1)S(1)} all-to-all(bf16[8,136,128]{2,1,0:T(8,128)(2,1)S(1)} %shard_map.87), channel_id=1, replica_groups=mesh['zh'=2,'zl'=4,'y'=4,'core'=2,'section'=2,'tp'=4] {'y','core'}, dimensions={0} | all-to-all | bytes 557056 | tf_op jit(solution)/shard_map/all_to_all | solution.py:324
  168.7 1.0 shard_map.88
  (29 shorter events, 6.5 us)
Async XLA Ops:
  6.5 54.5 %copy-start.2 = (bf16[4096]{0:T(1024)(128)(2,1)S(1)}, bf16[4096]{0:T(1024)(128)(2,1)}, u32[]{:S(2)}) copy-start(bf16[4096]{0:T(1024)(128)(2,1)} %param.12) | copy-start | bytes 24580
  6.5 54.6 %copy-start = (bf16[1024,512]{1,0:T(8,128)(2,1)S(1)}, bf16[1024,512]{1,0:T(8,128)(2,1)}, u32[]{:S(2)}) copy-start(bf16[1024,512]{1,0:T(8,128)(2,1)} %param.11) | copy-start | bytes 3145732
  6.5 54.6 %copy-start.1 = (bf16[128,512]{1,0:T(8,128)(2,1)S(1)}, bf16[128,512]{1,0:T(8,128)(2,1)}, u32[]{:S(2)}) copy-start(bf16[128,512]{1,0:T(8,128)(2,1)} %text.1) | copy-start | bytes 393220
  8.3 29.9 %all-to-all-start = ((bf16[8,64,384]{2,1,0:T(8,128)(2,1)}), bf16[8,64,384]{2,1,0:T(8,128)(2,1)S(1)}, u32[]{:S(2)}, u32[]{:S(2)}) async-start(bf16[8,64,384]{2,1,0:T(8,128)(2,1)} %get-tuple-element.22), calls=%async_computation | async-start | bytes 786432 | tf_op jit(solution)/shard_map/all_to_all | solution.py:260
  18.5 19.7 %collective-permute-start = (bf16[64,768]{1,0:T(8,128)(2,1)}, bf16[64,768]{1,0:T(8,128)(2,1)S(1)}, u32[]{:S(2)}, u32[]{:S(2)}) collective-permute-start(bf16[64,768]{1,0:T(8,128)(2,1)} %get-tuple-element.23), channel_id=1, source_target_pairs={{0,256},{256,0},{1,257},{257,1},{2,258},{258,2},{3,259},{259,3},{4... | collective-permute-start | bytes 294920 | tf_op jit(solution)/shard_map/ppermute | solution.py:26
  24.5 13.7 %collective-permute-start.1 = (bf16[128,128]{1,0:T(8,128)(2,1)}, bf16[128,128]{1,0:T(8,128)(2,1)S(1)}, u32[]{:S(2)}, u32[]{:S(2)}) collective-permute-start(bf16[128,128]{1,0:T(8,128)(2,1)} %param.9), channel_id=1, source_target_pairs={{0,4},{4,0},{1,5},{5,1},{2,6},{6,2},{3,7},{7,3},{8,12},{12,8},{9,1... | collective-permute-start | bytes 98312 | tf_op jit(solution)/shard_map/ppermute | solution.py:26
  39.0 20.4 %all-to-all-start.1 = ((bf16[8,64,384]{2,1,0:T(8,128)(2,1)}), bf16[8,64,384]{2,1,0:T(8,128)(2,1)S(1)}, u32[]{:S(2)}, u32[]{:S(2)}) async-start(bf16[8,64,384]{2,1,0:T(8,128)(2,1)} %shard_map.83), calls=%async_computation.1 | async-start | bytes 786432 | tf_op jit(solution)/shard_map/all_to_all | solution.py:263
  47.7 58.8 %all-gather.7.cloned.1.call-start = ((), (), s32[]{:S(2)}) async-start(), calls=%async_computation.5 | async-start | bytes 3932160 | tf_op jit(solution)/shard_map/all_gather | solution.py:267
  62.2 19.5 %collective-permute-start.2 = (bf16[128,512]{1,0:T(8,128)(2,1)S(1)}, bf16[128,512]{1,0:T(8,128)(2,1)S(1)}, u32[]{:S(2)}, u32[]{:S(2)}) collective-permute-start(bf16[128,512]{1,0:T(8,128)(2,1)S(1)} %shard_map.84), channel_id=1, source_target_pairs={{0,4},{4,0},{1,5},{5,1},{2,6},{6,2},{3,7},{7,3},{8,12},{12,8},{9,1... | collective-permute-start | bytes 393224 | tf_op jit(solution)/shard_map/ppermute | solution.py:26
  97.2 7.7 %collective-permute-start.4 = (bf16[4,128,512]{2,1,0:T(8,128)(2,1)S(1)}, bf16[4,128,512]{2,1,0:T(8,128)(2,1)S(1)}, u32[]{:S(2)}, u32[]{:S(2)}) collective-permute-start(bf16[4,128,512]{2,1,0:T(8,128)(2,1)S(1)} %bitcast.18), channel_id=1, source_target_pairs={{0,8},{8,0},{1,9},{9,1},{2,10},{10,2},{3,11},{11,3},{4,12},{12,4},... | collective-permute-start | bytes 1572872 | tf_op jit(solution)/shard_map/ppermute | solution.py:26
  102.3 3.8 %collective-permute-start.3 = (bf16[4,128,512]{2,1,0:T(8,128)(2,1)S(1)}, bf16[4,128,512]{2,1,0:T(8,128)(2,1)S(1)}, u32[]{:S(2)}, u32[]{:S(2)}) collective-permute-start(bf16[4,128,512]{2,1,0:T(8,128)(2,1)S(1)} %bitcast.16), channel_id=1, source_target_pairs={{0,8},{8,0},{1,9},{9,1},{2,10},{10,2},{3,11},{11,3},{4,12},{12,4},... | collective-permute-start | bytes 1572872 | tf_op jit(solution)/shard_map/ppermute | solution.py:26
  110.4 24.2 %all-to-all-start.2 = ((bf16[4,256,256]{2,1,0:T(8,128)(2,1)}), bf16[4,256,256]{2,1,0:T(8,128)(2,1)S(1)}, u32[]{:S(2)}, u32[]{:S(2)}) async-start(bf16[4,256,256]{2,1,0:T(8,128)(2,1)} %get-tuple-element.31), calls=%async_computation.2 | async-start | bytes 1048576 | tf_op jit(solution)/shard_map/all_to_all | solution.py:309
  114.9 17.0 %collective-permute-start.5 = (bf16[256,256]{1,0:T(8,128)(2,1)S(1)}, bf16[256,256]{1,0:T(8,128)(2,1)S(1)}, u32[]{:S(2)}, u32[]{:S(2)}) collective-permute-start(bf16[256,256]{1,0:T(8,128)(2,1)S(1)} %get-tuple-element.32), channel_id=1, source_target_pairs={{0,256},{256,0},{1,257},{257,1},{2,258},{258,2},{3,259},{259,3},{4... | collective-permute-start | bytes 393224 | tf_op jit(solution)/shard_map/ppermute | solution.py:26
  135.4 20.7 %all-to-all-start.3 = ((bf16[4,256,256]{2,1,0:T(8,128)(2,1)}), bf16[4,256,256]{2,1,0:T(8,128)(2,1)S(1)}, u32[]{:S(2)}, u32[]{:S(2)}) async-start(bf16[4,256,256]{2,1,0:T(8,128)(2,1)} %broadcast_in_dim.2), calls=%async_computation.3 | async-start | bytes 1048576 | tf_op jit(solution)/shard_map/all_to_all | solution.py:30
Sparse Core Ops, SparseCore 0:
  60.5 45.9 all-gather.6

commit v11 on v9

--- a/solution.py
+++ b/solution.py
@@ -44,7 +44,7 @@
 
 
 def project_kernel(
-    flip, own_a, own_b, other_a, other_b, stored, gain, cosine, sine, q_out, kv_out, lines_out, weight, sem, normed
+    flip, own_a, own_b, other_a, other_b, stored, gain, cosine, sine, q_out, kv_out, weight, sem, normed
 ):
     copies = [
         pltpu.make_async_copy(
@@ -83,9 +83,6 @@
     v = total[:, 2 * HD :].astype(jnp.bfloat16)
     kv_out[:, :HD] = k
     kv_out[:, HD:] = v
-    for i in range(ZL):
-        lines_out[i, :, :HD] = k
-        lines_out[i, :, HD:] = v
 
 
 def encode(level):
@@ -275,15 +272,14 @@
     other_a = swap(own_a, "core")
     own_b = lax.all_gather(joined_b, "tp", axis=0)
     other_b = swap(own_b, "core")
-    queries, kv, lines = pl.pallas_call(
+    queries, kv = pl.pallas_call(
         project_kernel,
         out_shape=[
             shaped(CHIP_ROWS, HD),
             shaped(CHIP_ROWS, 2 * HD),
-            shaped(ZL, CHIP_ROWS, 2 * HD),
         ],
         in_specs=[SMEM] + [VMEM] * 4 + [pl.BlockSpec(memory_space=pltpu.HBM)] + [VMEM] * 3,
-        out_specs=[VMEM] * 3,
+        out_specs=[VMEM] * 2,
         scratch_shapes=[
             pltpu.VMEM((Y, ZH, ZL * CORES, 64, 3 * HD), jnp.bfloat16),
             pltpu.SemaphoreType.DMA((TP,)),
@@ -306,7 +302,7 @@
     )
 
     kv_b = swap(kv, "zh")
-    kv_a = lax.all_to_all(lines, "zl", 0, 0, tiled=True)
+    kv_a = gather(kv, "zl", ZL)
     queries = lax.all_gather(queries, "y", axis=0)
     kv_a, kv_b, queries = lax.optimization_barrier((kv_a, kv_b, queries))
     place = jnp.stack([zh, zl, y, core])

time: 178 us -> 177 us (level)
    all_to_all x1 -> x0, starting transfers between devices: 4.54 us -> none  [local(): kv_a = lax.all_to_all(lines, 'zl', 0, 0, tiled=True)]
    all_to_all x1 -> x2, starting transfers between devices: 6.73 us -> 11.3 us  [gather(): lax.all_to_all(jnp.broadcast_to(v[None], (n, *v.shape)), axis, 0, 0, tile...]
    all_to_all x1 -> x2, waiting for transfers between devices: 10.9 us -> 13.5 us  [gather(): lax.all_to_all(jnp.broadcast_to(v[None], (n, *v.shape)), axis, 0, 0, tile...]
    all_to_all x1 -> x0, waiting for transfers between devices: 2.58 us -> none  [local(): kv_a = lax.all_to_all(lines, 'zl', 0, 0, tiled=True)]
where the time goes in v11:
time: 177 us
  starting transfers between devices  67 us (38%)
  blocking collectives  57.6 us (33%)
  waiting for transfers between devices  22 us (12%)
  between operations  14.2 us (8%)
  Pallas kernels  11.6 us (7%)
  other arithmetic  2.59 us (1%)
    ppermute x6, starting transfers between devices, swap(): return lax.ppermute(v, axis, SWAP)  36.8 us
    all_gather x1, blocking collectives, local(): own_b = lax.all_gather(joined_b, 'tp', axis=0)  15.6 us
    all_to_all x2, waiting for transfers between devices, gather(): lax.all_to_all(jnp.broadcast_to(v[None], (n, *v.shape)), axis, 0, 0, tile...  13.5 us
    all_to_all x1, blocking collectives, local(): parts = lax.all_to_all(parts, ('y', 'core'), 0, 0, tiled=True)  11.7 us
    all_to_all x2, starting transfers between devices, gather(): lax.all_to_all(jnp.broadcast_to(v[None], (n, *v.shape)), axis, 0, 0, tile...  11.3 us
    all_gather x1, blocking collectives, local(): own_a = lax.all_gather(joined, 'tp', axis=0)  11.1 us
    all_to_all x1, starting transfers between devices, local(): weight_a = lax.all_to_all(spread, ('zl', 'core'), 0, 0, tiled=True)  10.2 us
    all_gather x1, blocking collectives, local(): queries = lax.all_gather(queries, 'y', axis=0)  9.67 us
  transfers between devices with their start and end apart: 11, of which 6 were waited for; matrix products, arithmetic and copies ran while one was open for 1% of the time, Pallas kernels for 2%

profile of v11, /device:TPU:1, one launch (start us, length us, event | category | flops | bytes accessed | tf_op | source)
XLA Modules:
  0.0 176.7 jit_solution(12870913846540331419)
XLA Ops:
  6.5 1.7 shard_map.82
  8.3 10.2 %all-to-all-start = ((bf16[8,64,384]{2,1,0:T(8,128)(2,1)}), bf16[8,64,384]{2,1,0:T(8,128)(2,1)S(1)}, u32[]{:S(2)}, u32[]{:S(2)}) async-start(bf16[8,64,384]{2,1,0:T(8,128)(2,1)} %get-tuple-element.21), calls=%async_computation | async-start | bytes 786432 | tf_op jit(solution)/shard_map/all_to_all | solution.py:257
  18.5 6.0 %collective-permute-start = (bf16[64,768]{1,0:T(8,128)(2,1)}, bf16[64,768]{1,0:T(8,128)(2,1)S(1)}, u32[]{:S(2)}, u32[]{:S(2)}) collective-permute-start(bf16[64,768]{1,0:T(8,128)(2,1)} %get-tuple-element.22), channel_id=1, source_target_pairs={{0,256},{256,0},{1,257},{257,1},{2,258},{258,2},{3,259},{259,3},{4... | collective-permute-start | bytes 294920 | tf_op jit(solution)/shard_map/ppermute | solution.py:26
  24.5 8.1 %collective-permute-start.1 = (bf16[128,128]{1,0:T(8,128)(2,1)}, bf16[128,128]{1,0:T(8,128)(2,1)S(1)}, u32[]{:S(2)}, u32[]{:S(2)}) collective-permute-start(bf16[128,128]{1,0:T(8,128)(2,1)} %param.9), channel_id=1, source_target_pairs={{0,4},{4,0},{1,5},{5,1},{2,6},{6,2},{3,7},{7,3},{8,12},{12,8},{9,1... | collective-permute-start | bytes 98312 | tf_op jit(solution)/shard_map/ppermute | solution.py:26
  32.6 5.6 %collective-permute-done.1 = bf16[128,128]{1,0:T(8,128)(2,1)S(1)} collective-permute-done((bf16[128,128]{1,0:T(8,128)(2,1)}, bf16[128,128]{1,0:T(8,128)(2,1)S(1)}, u32[]{:S(2)}, u32[]{:S(2)}) %collective-permute-start.1) | collective-permute-done | bytes 32800 | tf_op jit(solution)/shard_map/ppermute | solution.py:26
  39.0 8.7 %all-to-all-start.1 = ((bf16[8,64,384]{2,1,0:T(8,128)(2,1)}), bf16[8,64,384]{2,1,0:T(8,128)(2,1)S(1)}, u32[]{:S(2)}, u32[]{:S(2)}) async-start(bf16[8,64,384]{2,1,0:T(8,128)(2,1)} %shard_map.83), calls=%async_computation.1 | async-start | bytes 786432 | tf_op jit(solution)/shard_map/all_to_all | solution.py:260
  48.5 9.5 %all-gather = bf16[8,128,128]{2,1,0:T(8,128)(2,1)S(1)} all-gather(bf16[2,128,128]{2,1,0:T(8,128)(2,1)S(1)} %pad_maximum_fusion.3), channel_id=2, replica_groups=mesh['zh'=2,'zl'=4,'y'=4,'core'=2,'section'=2,'tp'=4] {'tp'}, dimensions={0}, use_global_device_ids=true | all-gather | bytes 327680 | tf_op jit(solution)/shard_map/all_gather | solution.py:262
  58.0 1.4 all-to-all-done.1
  62.2 8.3 %collective-permute-start.2 = (bf16[128,512]{1,0:T(8,128)(2,1)S(1)}, bf16[128,512]{1,0:T(8,128)(2,1)S(1)}, u32[]{:S(2)}, u32[]{:S(2)}) collective-permute-start(bf16[128,512]{1,0:T(8,128)(2,1)S(1)} %shard_map.84), channel_id=1, source_target_pairs={{0,4},{4,0},{1,5},{5,1},{2,6},{6,2},{3,7},{7,3},{8,12},{12,8},{9,1... | collective-permute-start | bytes 393224 | tf_op jit(solution)/shard_map/ppermute | solution.py:26
  70.5 11.1 %all-gather.1 = bf16[512,512]{1,0:T(8,128)(2,1)S(1)} all-gather(bf16[128,512]{1,0:T(8,128)(2,1)S(1)} %shard_map.84), channel_id=3, replica_groups=mesh['zh'=2,'zl'=4,'y'=4,'core'=2,'section'=2,'tp'=4] {'tp'}, dimensions={0}, use_global_device_ids=true | all-gather | bytes 655360 | tf_op jit(solution)/shard_map/all_gather | solution.py:270
  81.6 15.6 %all-gather.2 = bf16[512,512]{1,0:T(8,128)(2,1)S(1)} all-gather(bf16[128,512]{1,0:T(8,128)(2,1)S(1)} %collective-permute-done.2), channel_id=4, replica_groups=mesh['zh'=2,'zl'=4,'y'=4,'core'=2,'section'=2,'tp'=4] {'tp'}, dimensions={0}, use_global_device_ids=true | all-gather | bytes 655360 | tf_op jit(solution)/shard_map/all_gather | solution.py:273
  97.2 5.1 %collective-permute-start.4 = (bf16[4,128,512]{2,1,0:T(8,128)(2,1)S(1)}, bf16[4,128,512]{2,1,0:T(8,128)(2,1)S(1)}, u32[]{:S(2)}, u32[]{:S(2)}) collective-permute-start(bf16[4,128,512]{2,1,0:T(8,128)(2,1)S(1)} %bitcast.18), channel_id=1, source_target_pairs={{0,8},{8,0},{1,9},{9,1},{2,10},{10,2},{3,11},{11,3},{4,12},{12,4},... | collective-permute-start | bytes 1572872 | tf_op jit(solution)/shard_map/ppermute | solution.py:26
  102.3 1.9 %collective-permute-start.3 = (bf16[4,128,512]{2,1,0:T(8,128)(2,1)S(1)}, bf16[4,128,512]{2,1,0:T(8,128)(2,1)S(1)}, u32[]{:S(2)}, u32[]{:S(2)}) collective-permute-start(bf16[4,128,512]{2,1,0:T(8,128)(2,1)S(1)} %bitcast.16), channel_id=1, source_target_pairs={{0,8},{8,0},{1,9},{9,1},{2,10},{10,2},{3,11},{11,3},{4,12},{12,4},... | collective-permute-start | bytes 1572872 | tf_op jit(solution)/shard_map/ppermute | solution.py:26
  105.0 1.2 collective-permute-done.3.other_a
  106.4 3.2 %shard_map.85 = (bf16[256,128]{1,0:T(8,128)(2,1)S(1)}, bf16[256,256]{1,0:T(8,128)(2,1)S(1)}) custom-call(s32[1]{0:T(128)} %bitcast.4.flip, bf16[4,128,512]{2,1,0:T(8,128)(2,1)S(1)} %bitcast.17, bf16[4,128,512]{2,1,0:T(8,128)(2,1)S(1)} %bitcast.19, bf16[4,128,512]{2,1,0:T(8,128)(2,1)S(1)} %collective-permute-done.3.other_a, ...), custom_call_target="tpu_custom_call" | custom-call | flops 805306368 | bytes 6291456 | tf_op jit(solution)/shard_map/pallas_call | solution.py:275
  110.5 4.5 %all-to-all-start.2 = ((bf16[4,256,256]{2,1,0:T(8,128)(2,1)}), bf16[4,256,256]{2,1,0:T(8,128)(2,1)S(1)}, u32[]{:S(2)}, u32[]{:S(2)}) async-start(bf16[4,256,256]{2,1,0:T(8,128)(2,1)} %broadcast_in_dim.4), calls=%async_computation.2 | async-start | bytes 1048576 | tf_op jit(solution)/shard_map/all_to_all | solution.py:30
  115.0 7.4 %collective-permute-start.5 = (bf16[256,256]{1,0:T(8,128)(2,1)S(1)}, bf16[256,256]{1,0:T(8,128)(2,1)S(1)}, u32[]{:S(2)}, u32[]{:S(2)}) collective-permute-start(bf16[256,256]{1,0:T(8,128)(2,1)S(1)} %get-tuple-element.30), channel_id=1, source_target_pairs={{0,256},{256,0},{1,257},{257,1},{2,258},{258,2},{3,259},{259,3},{4... | collective-permute-start | bytes 393224 | tf_op jit(solution)/shard_map/ppermute | solution.py:26
  122.4 9.7 %all-gather.4 = bf16[1024,128]{1,0:T(8,128)(2,1)S(1)} all-gather(bf16[256,128]{1,0:T(8,128)(2,1)S(1)} %get-tuple-element.31), channel_id=6, replica_groups=mesh['zh'=2,'zl'=4,'y'=4,'core'=2,'section'=2,'tp'=4] {'y'}, dimensions={0}, use_global_device_ids=true | all-gather | bytes 327680 | tf_op jit(solution)/shard_map/all_gather | solution.py:306
  132.1 2.6 %all-to-all-done.2.kv = bf16[4,256,256]{2,1,0:T(8,128)(2,1)S(1)} async-done(((bf16[4,256,256]{2,1,0:T(8,128)(2,1)}), bf16[4,256,256]{2,1,0:T(8,128)(2,1)S(1)}, u32[]{:S(2)}, u32[]{:S(2)}) %all-to-all-start.2) | async-done | bytes 524320 | tf_op jit(solution)/shard_map/all_to_all | solution.py:30
  135.5 6.7 %all-to-all-start.3 = ((bf16[4,256,256]{2,1,0:T(8,128)(2,1)}), bf16[4,256,256]{2,1,0:T(8,128)(2,1)S(1)}, u32[]{:S(2)}, u32[]{:S(2)}) async-start(bf16[4,256,256]{2,1,0:T(8,128)(2,1)} %broadcast_in_dim.5), calls=%async_computation.3 | async-start | bytes 1048576 | tf_op jit(solution)/shard_map/all_to_all | solution.py:30
  142.3 3.0 %shard_map.86 = (f32[4,256,128]{2,1,0:T(8,128)S(1)}, f32[4,256,128]{2,1,0:T(8,128)S(1)}) custom-call(s32[4]{0:T(128)S(1)} %pad_add_fusion.place, bf16[4,256,128]{2,1,0:T(8,128)(2,1)S(1)} %bitcast.20, bf16[4,256,256]{2,1,0:T(8,128)(2,1)S(1)} %all-to-all-done.2.kv), custom_call_target="tpu_custom_call" | custom-call | flops 536870912 | bytes 2097152 | tf_op jit(solution)/shard_map/pallas_call | solution.py:312
  145.3 10.9 %all-to-all-done.3.kv = bf16[4,256,256]{2,1,0:T(8,128)(2,1)S(1)} async-done(((bf16[4,256,256]{2,1,0:T(8,128)(2,1)}), bf16[4,256,256]{2,1,0:T(8,128)(2,1)S(1)}, u32[]{:S(2)}, u32[]{:S(2)}) %all-to-all-start.3) | async-done | bytes 524320 | tf_op jit(solution)/shard_map/all_to_all | solution.py:30
  157.2 11.7 %all_to_all.25.parts = bf16[8,136,128]{2,1,0:T(8,128)(2,1)S(1)} all-to-all(bf16[8,136,128]{2,1,0:T(8,128)(2,1)S(1)} %shard_map.87), channel_id=1, replica_groups=mesh['zh'=2,'zl'=4,'y'=4,'core'=2,'section'=2,'tp'=4] {'y','core'}, dimensions={0} | all-to-all | bytes 557056 | tf_op jit(solution)/shard_map/all_to_all | solution.py:320
  168.8 1.0 shard_map.88
  (30 shorter events, 7.4 us)
Async XLA Ops:
  6.5 54.5 %copy-start.2 = (bf16[4096]{0:T(1024)(128)(2,1)S(1)}, bf16[4096]{0:T(1024)(128)(2,1)}, u32[]{:S(2)}) copy-start(bf16[4096]{0:T(1024)(128)(2,1)} %param.12) | copy-start | bytes 24580
  6.5 54.6 %copy-start = (bf16[1024,512]{1,0:T(8,128)(2,1)S(1)}, bf16[1024,512]{1,0:T(8,128)(2,1)}, u32[]{:S(2)}) copy-start(bf16[1024,512]{1,0:T(8,128)(2,1)} %param.11) | copy-start | bytes 3145732
  6.5 54.6 %copy-start.1 = (bf16[128,512]{1,0:T(8,128)(2,1)S(1)}, bf16[128,512]{1,0:T(8,128)(2,1)}, u32[]{:S(2)}) copy-start(bf16[128,512]{1,0:T(8,128)(2,1)} %text.1) | copy-start | bytes 393220
  8.3 29.9 %all-to-all-start = ((bf16[8,64,384]{2,1,0:T(8,128)(2,1)}), bf16[8,64,384]{2,1,0:T(8,128)(2,1)S(1)}, u32[]{:S(2)}, u32[]{:S(2)}) async-start(bf16[8,64,384]{2,1,0:T(8,128)(2,1)} %get-tuple-element.21), calls=%async_computation | async-start | bytes 786432 | tf_op jit(solution)/shard_map/all_to_all | solution.py:257
  18.5 19.7 %collective-permute-start = (bf16[64,768]{1,0:T(8,128)(2,1)}, bf16[64,768]{1,0:T(8,128)(2,1)S(1)}, u32[]{:S(2)}, u32[]{:S(2)}) collective-permute-start(bf16[64,768]{1,0:T(8,128)(2,1)} %get-tuple-element.22), channel_id=1, source_target_pairs={{0,256},{256,0},{1,257},{257,1},{2,258},{258,2},{3,259},{259,3},{4... | collective-permute-start | bytes 294920 | tf_op jit(solution)/shard_map/ppermute | solution.py:26
  24.5 13.7 %collective-permute-start.1 = (bf16[128,128]{1,0:T(8,128)(2,1)}, bf16[128,128]{1,0:T(8,128)(2,1)S(1)}, u32[]{:S(2)}, u32[]{:S(2)}) collective-permute-start(bf16[128,128]{1,0:T(8,128)(2,1)} %param.9), channel_id=1, source_target_pairs={{0,4},{4,0},{1,5},{5,1},{2,6},{6,2},{3,7},{7,3},{8,12},{12,8},{9,1... | collective-permute-start | bytes 98312 | tf_op jit(solution)/shard_map/ppermute | solution.py:26
  39.0 20.4 %all-to-all-start.1 = ((bf16[8,64,384]{2,1,0:T(8,128)(2,1)}), bf16[8,64,384]{2,1,0:T(8,128)(2,1)S(1)}, u32[]{:S(2)}, u32[]{:S(2)}) async-start(bf16[8,64,384]{2,1,0:T(8,128)(2,1)} %shard_map.83), calls=%async_computation.1 | async-start | bytes 786432 | tf_op jit(solution)/shard_map/all_to_all | solution.py:260
  47.7 58.8 %all-gather.7.cloned.1.call-start = ((), (), s32[]{:S(2)}) async-start(), calls=%async_computation.5 | async-start | bytes 3932160 | tf_op jit(solution)/shard_map/all_gather | solution.py:264
  62.2 19.5 %collective-permute-start.2 = (bf16[128,512]{1,0:T(8,128)(2,1)S(1)}, bf16[128,512]{1,0:T(8,128)(2,1)S(1)}, u32[]{:S(2)}, u32[]{:S(2)}) collective-permute-start(bf16[128,512]{1,0:T(8,128)(2,1)S(1)} %shard_map.84), channel_id=1, source_target_pairs={{0,4},{4,0},{1,5},{5,1},{2,6},{6,2},{3,7},{7,3},{8,12},{12,8},{9,1... | collective-permute-start | bytes 393224 | tf_op jit(solution)/shard_map/ppermute | solution.py:26
  97.2 7.7 %collective-permute-start.4 = (bf16[4,128,512]{2,1,0:T(8,128)(2,1)S(1)}, bf16[4,128,512]{2,1,0:T(8,128)(2,1)S(1)}, u32[]{:S(2)}, u32[]{:S(2)}) collective-permute-start(bf16[4,128,512]{2,1,0:T(8,128)(2,1)S(1)} %bitcast.18), channel_id=1, source_target_pairs={{0,8},{8,0},{1,9},{9,1},{2,10},{10,2},{3,11},{11,3},{4,12},{12,4},... | collective-permute-start | bytes 1572872 | tf_op jit(solution)/shard_map/ppermute | solution.py:26
  102.3 3.8 %collective-permute-start.3 = (bf16[4,128,512]{2,1,0:T(8,128)(2,1)S(1)}, bf16[4,128,512]{2,1,0:T(8,128)(2,1)S(1)}, u32[]{:S(2)}, u32[]{:S(2)}) collective-permute-start(bf16[4,128,512]{2,1,0:T(8,128)(2,1)S(1)} %bitcast.16), channel_id=1, source_target_pairs={{0,8},{8,0},{1,9},{9,1},{2,10},{10,2},{3,11},{11,3},{4,12},{12,4},... | collective-permute-start | bytes 1572872 | tf_op jit(solution)/shard_map/ppermute | solution.py:26
  110.5 24.1 %all-to-all-start.2 = ((bf16[4,256,256]{2,1,0:T(8,128)(2,1)}), bf16[4,256,256]{2,1,0:T(8,128)(2,1)S(1)}, u32[]{:S(2)}, u32[]{:S(2)}) async-start(bf16[4,256,256]{2,1,0:T(8,128)(2,1)} %broadcast_in_dim.4), calls=%async_computation.2 | async-start | bytes 1048576 | tf_op jit(solution)/shard_map/all_to_all | solution.py:30
  115.0 17.0 %collective-permute-start.5 = (bf16[256,256]{1,0:T(8,128)(2,1)S(1)}, bf16[256,256]{1,0:T(8,128)(2,1)S(1)}, u32[]{:S(2)}, u32[]{:S(2)}) collective-permute-start(bf16[256,256]{1,0:T(8,128)(2,1)S(1)} %get-tuple-element.30), channel_id=1, source_target_pairs={{0,256},{256,0},{1,257},{257,1},{2,258},{258,2},{3,259},{259,3},{4... | collective-permute-start | bytes 393224 | tf_op jit(solution)/shard_map/ppermute | solution.py:26
  135.5 20.7 %all-to-all-start.3 = ((bf16[4,256,256]{2,1,0:T(8,128)(2,1)}), bf16[4,256,256]{2,1,0:T(8,128)(2,1)S(1)}, u32[]{:S(2)}, u32[]{:S(2)}) async-start(bf16[4,256,256]{2,1,0:T(8,128)(2,1)} %broadcast_in_dim.5), calls=%async_computation.3 | async-start | bytes 1048576 | tf_op jit(solution)/shard_map/all_to_all | solution.py:30
Sparse Core Ops, SparseCore 0:
  60.5 45.9 all-gather.6
